TPU v7x, 32 devices: a whole 2x2x4 slice. The times are simulated.
32 devices in a mesh: dp: 8 (over z, x), seq: 4 (over y, core).
Axes of the slice: x: 2, y: 2, z: 4, core: 2. Of those that a mesh axis runs over, the one named last changes fastest.
Arguments:
- hidden: bfloat16 [8, 512, 768], P('dp', 'seq'), may hold values from -6 to 6
- char_ids: int32 [8, 512, 16], P('dp', 'seq'), may hold values from 0 to 127, as said below
- groups: int32 [8], P('dp'), may hold values from 0 to 7
- lengths: int32 [8], P('dp'), may hold values from 128 to 512, as said below
- cotangent: bfloat16 [8, 512, 768], P('dp', 'seq'), may hold values from -6 to 6
- qkv_weight: bfloat16 [768, 2304], P(('dp', 'seq')), may hold values from -0.21875 to 0.21875
- out_weight: bfloat16 [768, 768], P(('dp', 'seq')), may hold values from -0.875 to 0.875
- up_weight: bfloat16 [768, 3072], P(('dp', 'seq')), may hold values from -0.21875 to 0.21875
- down_weight: bfloat16 [3072, 768], P(('dp', 'seq')), may hold values from -0.109375 to 0.109375
- norm_gain: bfloat16 [3, 768], P(None, ('dp', 'seq')), may hold values from 0.5 to 1.5
- norm_bias: bfloat16 [3, 768], P(None, ('dp', 'seq')), may hold values from -1.5 to 1.5
- char_table: bfloat16 [1024, 256], P(('dp', 'seq')), may hold values from -6 to 6
- gru_input: bfloat16 [512, 1152], P(('dp', 'seq')), may hold values from -0.375 to 0.375
- gru_recur: bfloat16 [768, 1152], P(('dp', 'seq')), may hold values from -0.3125 to 0.3125
- merge_weight: bfloat16 [1536, 768], P(('dp', 'seq')), may hold values from -0.21875 to 0.21875
- conv_weight: bfloat16 [4608, 768], P(('dp', 'seq')), may hold values from -0.09375 to 0.09375
Outputs:
- result: bfloat16 [8, 512, 768], P('dp', 'seq')
- hidden_grad: bfloat16 [8, 512, 768], P('dp', 'seq')
- qkv_grad: float32 [768, 2304], P(('dp', 'seq'))
- out_grad: float32 [768, 768], P(('dp', 'seq'))
- up_grad: float32 [768, 3072], P(('dp', 'seq'))
- down_grad: float32 [3072, 768], P(('dp', 'seq'))
- gain_grad: float32 [3, 768], P(None, ('dp', 'seq'))
- bias_grad: float32 [3, 768], P(None, ('dp', 'seq'))
- table_grad: float32 [1024, 256], P(('dp', 'seq'))
- gru_input_grad: float32 [512, 1152], P(('dp', 'seq'))
- gru_recur_grad: float32 [768, 1152], P(('dp', 'seq'))
- merge_grad: float32 [1536, 768], P(('dp', 'seq'))
- conv_grad: float32 [4608, 768], P(('dp', 'seq'))
Inputs may be any that keep to these rules, and one draw needn't show every extreme that they name: `char_ids`: in each token the nonzero ids come first and the rest of its 16 slots are 0; the first slot is never 0. `lengths`: positions at or past a sequence's length are padding that attention does not read as keys.
All inputs are finite; a program needn't handle non-finite values.
Results may differ from a plain program's by a relative error of at most 0.017.
Values may be sent and summed in bfloat16 or wider, within the bound.
A program may use at most 256 MiB of HBM per device.

v0:
```python
import math

import jax
import jax.numpy as jnp
from jax import lax
from jax.sharding import PartitionSpec as P

HD = 64
SUBV = 128


eps = 1e-05


def with_halo(x, sides, width):
    for axis, dim in sides:
        devices, length = (lax.axis_size(axis), x.shape[dim])
        up = [(i, (i + 1) % devices) for i in range(devices - 1)]
        down = [(j, i) for i, j in up]
        last = lax.slice_in_dim(x, length - width, length, axis=dim)
        first = lax.slice_in_dim(x, 0, width, axis=dim)
        before = lax.ppermute(last, axis, up)
        after = lax.ppermute(first, axis, down)
        x = jnp.concatenate([before, x, after], axis=dim)
    return x


def norm_rows(residual, row_gain, row_bias):
    centered = residual - jnp.mean(residual, axis=-1, keepdims=True)
    spread = jnp.mean(centered * centered, axis=-1, keepdims=True)
    return centered * lax.rsqrt(spread + eps) * row_gain + row_bias


def cell(gate_input, gate_recur, carry_state, is_live):
    units = carry_state.shape[-1]
    reset = jax.nn.sigmoid(gate_input[..., :units] + gate_recur[..., :units])
    update = jax.nn.sigmoid(gate_input[..., units : 2 * units] + gate_recur[..., units : 2 * units])
    candidate = jnp.tanh(gate_input[..., 2 * units :] + reset * gate_recur[..., 2 * units :])
    fresh = (1.0 - update) * candidate + update * carry_state
    return jnp.where(is_live, fresh, carry_state)


def gelu_exact(pre_act):
    return jax.nn.gelu(pre_act, approximate=False)


def plain_dot(left, right):
    return jnp.dot(left, right, preferred_element_type=jnp.float32)


def grad_dot(left, right):
    return lax.dot_general(
        left, right, (((0,), (0,)), ((), ())), preferred_element_type=jnp.float32
    )


def back_dot(left, right):
    return lax.dot_general(
        left, right, (((1,), (1,)), ((), ())), preferred_element_type=jnp.float32
    )


def local(
    hidden,
    char_ids,
    groups,
    lengths,
    cotangent,
    qkv_weight,
    out_weight,
    up_weight,
    down_weight,
    norm_gain,
    norm_bias,
    char_table,
    gru_input,
    gru_recur,
    merge_weight,
    conv_weight,
):
    gathered = (
        lax.all_gather(qkv_weight, ("dp", "seq"), axis=0, tiled=True),
        lax.all_gather(out_weight, ("dp", "seq"), axis=0, tiled=True),
        lax.all_gather(up_weight, ("dp", "seq"), axis=0, tiled=True),
        lax.all_gather(down_weight, ("dp", "seq"), axis=0, tiled=True),
        lax.all_gather(norm_gain, ("dp", "seq"), axis=1, tiled=True),
        lax.all_gather(norm_bias, ("dp", "seq"), axis=1, tiled=True),
        lax.all_gather(char_table, ("dp", "seq"), axis=0, tiled=True),
        lax.all_gather(gru_input, ("dp", "seq"), axis=0, tiled=True),
        lax.all_gather(gru_recur, ("dp", "seq"), axis=0, tiled=True),
        lax.all_gather(merge_weight, ("dp", "seq"), axis=0, tiled=True),
        lax.all_gather(conv_weight, ("dp", "seq"), axis=0, tiled=True),
    )
    (
        full_qkv,
        full_out,
        full_up,
        full_down,
        full_gain,
        full_bias,
        full_table,
        full_input,
        full_recur,
        full_merge,
        full_conv,
    ) = gathered
    seq_count, local_len, features = hidden.shape
    nchar = char_ids.shape[2]
    tokens = seq_count * local_len
    head_count = features // HD
    key_span = local_len * lax.axis_size("seq")
    score_scale = 1.0 / math.sqrt(HD)
    gains = full_gain.astype(jnp.float32)
    biases = full_bias.astype(jnp.float32)
    flat_in = hidden.reshape(tokens, features)
    qkv = plain_dot(flat_in, full_qkv).astype(jnp.bfloat16)
    queries = qkv[:, :features].reshape(seq_count, local_len, head_count, HD)
    own_keys = qkv[:, features : 2 * features].reshape(seq_count, local_len, features)
    own_values = qkv[:, 2 * features :].reshape(seq_count, local_len, features)
    all_keys, all_values = (
        lax.all_gather(own_keys, "seq", axis=1, tiled=True),
        lax.all_gather(own_values, "seq", axis=1, tiled=True),
    )
    all_keys = all_keys.reshape(seq_count, key_span, head_count, HD)
    all_values = all_values.reshape(seq_count, key_span, head_count, HD)
    key_valid = jnp.arange(key_span)[None, None, None, :] < lengths[:, None, None, None]

    def score_block():
        raw_scores = (
            jnp.einsum("sqhd,skhd->shqk", queries, all_keys, preferred_element_type=jnp.float32)
            * score_scale
        )
        return jnp.where(key_valid, raw_scores, -1000000000.0)

    scores = score_block()
    log_total = jax.nn.logsumexp(scores, axis=-1, keepdims=True)
    attn_probs = jnp.exp(scores - log_total).astype(jnp.bfloat16)
    attended = jnp.einsum(
        "shqk,skhd->sqhd", attn_probs, all_values, preferred_element_type=jnp.float32
    )
    attended = attended.astype(jnp.bfloat16).reshape(tokens, features)
    resid_one = flat_in.astype(jnp.float32) + plain_dot(attended, full_out)
    norm_one = norm_rows(resid_one, gains[0], biases[0]).astype(jnp.bfloat16)
    up_proj = plain_dot(norm_one, full_up)
    active = gelu_exact(up_proj).astype(jnp.bfloat16)
    resid_two = norm_one.astype(jnp.float32) + plain_dot(active, full_down)
    norm_two = norm_rows(resid_two, gains[1], biases[1]).astype(jnp.bfloat16)
    vocab_rows = full_table.shape[0]
    char_rows = (groups[:, None, None] * SUBV + char_ids).reshape(tokens * nchar)
    onehot = (char_rows[:, None] == jnp.arange(vocab_rows)[None, :]).astype(jnp.bfloat16)
    char_emb = plain_dot(onehot, full_table).astype(jnp.bfloat16).reshape(tokens, nchar, -1)
    char_live = (char_ids > 0).reshape(tokens, nchar)
    steps_in = jnp.stack([char_emb, char_emb[:, ::-1]], 0).transpose(2, 0, 1, 3)
    steps_live = jnp.stack([char_live, char_live[:, ::-1]], 0).transpose(2, 0, 1)[..., None]
    inward = full_input.reshape(2, -1, full_input.shape[1])
    recurrent = full_recur.reshape(2, -1, full_recur.shape[1])
    hidden_units = recurrent.shape[1]
    gates_in = jnp.einsum("cdtz,dzg->cdtg", steps_in, inward, preferred_element_type=jnp.float32)

    def gru_step(carry_state, step_input):
        gate_input, is_live = step_input
        gate_recur = jnp.einsum(
            "dth,dhg->dtg",
            carry_state.astype(jnp.bfloat16),
            recurrent,
            preferred_element_type=jnp.float32,
        )
        return (cell(gate_input, gate_recur, carry_state, is_live), carry_state)

    start_state = jnp.zeros((2, tokens, hidden_units), jnp.float32)
    last_state, prior_states = lax.scan(gru_step, start_state, (gates_in, steps_live))
    char_vec = jnp.concatenate([last_state[0], last_state[1]], -1).astype(jnp.bfloat16)
    merge_mats = full_merge.reshape(2, features, features)
    merged_rows = jnp.concatenate(
        [plain_dot(norm_two, merge_mats[0]), plain_dot(char_vec, merge_mats[1])], -1
    ).astype(jnp.bfloat16)
    padded = with_halo(merged_rows.reshape(seq_count, local_len, 2 * features), (("seq", 1),), 1)
    kernel = full_conv.reshape(3, 2 * features, features)
    windows = [
        padded[:, offset : offset + local_len].reshape(tokens, 2 * features) for offset in range(3)
    ]
    conv_out = (
        plain_dot(windows[0], kernel[0])
        + plain_dot(windows[1], kernel[1])
        + plain_dot(windows[2], kernel[2])
    )
    resid_three = norm_two.astype(jnp.float32) + conv_out
    result_rows, pull_three = jax.vjp(norm_rows, resid_three, gains[2], biases[2])
    result = result_rows.astype(jnp.bfloat16).reshape(seq_count, local_len, features)
    back_set = (
        lax.all_gather(qkv_weight, ("dp", "seq"), axis=0, tiled=True),
        lax.all_gather(out_weight, ("dp", "seq"), axis=0, tiled=True),
        lax.all_gather(up_weight, ("dp", "seq"), axis=0, tiled=True),
        lax.all_gather(down_weight, ("dp", "seq"), axis=0, tiled=True),
        lax.all_gather(gru_input, ("dp", "seq"), axis=0, tiled=True),
        lax.all_gather(gru_recur, ("dp", "seq"), axis=0, tiled=True),
        lax.all_gather(merge_weight, ("dp", "seq"), axis=0, tiled=True),
        lax.all_gather(conv_weight, ("dp", "seq"), axis=0, tiled=True),
    )
    back_qkv, back_out, back_up, back_down, back_input, back_recur, back_merge, back_conv = back_set
    merge_back = back_merge.reshape(2, features, features)
    kernel_back = back_conv.reshape(3, 2 * features, features)
    inward_back = back_input.reshape(2, -1, back_input.shape[1])
    recur_back = back_recur.reshape(2, -1, back_recur.shape[1])
    seed_rows = cotangent.reshape(tokens, features).astype(jnp.float32)
    grad_three, gain_three, bias_three = pull_three(seed_rows)
    conv_seed = grad_three.astype(jnp.bfloat16)
    conv_grad = jnp.concatenate([grad_dot(windows[offset], conv_seed) for offset in range(3)], 0)
    seed_padded = with_halo(conv_seed.reshape(seq_count, local_len, features), (("seq", 1),), 1)
    merged_grad = back_dot(
        seed_padded[:, 2 : 2 + local_len].reshape(tokens, features), kernel_back[0]
    )
    merged_grad = merged_grad + back_dot(
        seed_padded[:, 1 : 1 + local_len].reshape(tokens, features), kernel_back[1]
    )
    merged_grad = merged_grad + back_dot(
        seed_padded[:, 0:local_len].reshape(tokens, features), kernel_back[2]
    )
    merged_grad = merged_grad.astype(jnp.bfloat16)
    token_part = merged_grad[:, :features]
    char_part = merged_grad[:, features:]
    merge_grad = jnp.concatenate([grad_dot(norm_two, token_part), grad_dot(char_vec, char_part)], 0)
    two_grad = grad_three + back_dot(token_part, merge_back[0])
    charvec_grad = back_dot(char_part, merge_back[1])
    _, pull_two = jax.vjp(norm_rows, resid_two, gains[1], biases[1])
    grad_two, gain_two, bias_two = pull_two(two_grad)
    down_seed = grad_two.astype(jnp.bfloat16)
    down_grad = grad_dot(active, down_seed)
    active_grad = back_dot(down_seed, back_down)
    _, pull_gelu = jax.vjp(gelu_exact, up_proj)
    up_seed = pull_gelu(active_grad)[0].astype(jnp.bfloat16)
    up_grad = grad_dot(norm_one, up_seed)
    one_grad = grad_two + back_dot(up_seed, back_up)
    _, pull_one = jax.vjp(norm_rows, resid_one, gains[0], biases[0])
    grad_one, gain_one, bias_one = pull_one(one_grad)
    out_seed = grad_one.astype(jnp.bfloat16)
    out_grad = grad_dot(attended, out_seed)
    attn_seed = (
        back_dot(out_seed, back_out)
        .astype(jnp.bfloat16)
        .reshape(seq_count, local_len, head_count, HD)
    )
    probs_again = jnp.exp(score_block() - log_total)
    probs_grad = jnp.einsum(
        "sqhd,skhd->shqk", attn_seed, all_values, preferred_element_type=jnp.float32
    )
    score_grad = probs_again * (
        probs_grad - jnp.sum(probs_again * probs_grad, axis=-1, keepdims=True)
    )
    score_grad = score_grad.astype(jnp.bfloat16)
    query_grad = (
        jnp.einsum("shqk,skhd->sqhd", score_grad, all_keys, preferred_element_type=jnp.float32)
        * score_scale
    )
    key_grad = (
        jnp.einsum("shqk,sqhd->skhd", score_grad, queries, preferred_element_type=jnp.float32)
        * score_scale
    )
    value_grad = jnp.einsum(
        "shqk,sqhd->skhd",
        probs_again.astype(jnp.bfloat16),
        attn_seed,
        preferred_element_type=jnp.float32,
    )
    key_own, value_own = (
        lax.psum_scatter(
            key_grad.reshape(seq_count, key_span, features).astype(jnp.bfloat16),
            "seq",
            scatter_dimension=1,
            tiled=True,
        ).astype(jnp.float32),
        lax.psum_scatter(
            value_grad.reshape(seq_count, key_span, features).astype(jnp.bfloat16),
            "seq",
            scatter_dimension=1,
            tiled=True,
        ).astype(jnp.float32),
    )
    qkv_seed = jnp.concatenate(
        [
            query_grad.reshape(tokens, features),
            key_own.reshape(tokens, features),
            value_own.reshape(tokens, features),
        ],
        -1,
    ).astype(jnp.bfloat16)
    qkv_grad = grad_dot(flat_in, qkv_seed)
    hidden_grad = (
        (grad_one + back_dot(qkv_seed, back_qkv))
        .astype(jnp.bfloat16)
        .reshape(seq_count, local_len, features)
    )
    state_seed = jnp.stack([charvec_grad[:, :hidden_units], charvec_grad[:, hidden_units:]], 0)

    def back_step(carry_in, step_input):
        state_grad, recur_total = carry_in
        gate_input, is_live, carry_state = step_input
        state_low = carry_state.astype(jnp.bfloat16)
        gate_recur = jnp.einsum(
            "dth,dhg->dtg", state_low, recur_back, preferred_element_type=jnp.float32
        )

        def cell_local(given, recurred, previous):
            return cell(given, recurred, previous, is_live)

        _, pull_cell = jax.vjp(cell_local, gate_input, gate_recur, carry_state)
        input_part, recur_part, prior_part = pull_cell(state_grad)
        recur_low = recur_part.astype(jnp.bfloat16)
        prior_part = prior_part + jnp.einsum(
            "dtg,dhg->dth", recur_low, recur_back, preferred_element_type=jnp.float32
        )
        recur_total = recur_total + jnp.einsum(
            "dth,dtg->dhg", state_low, recur_low, preferred_element_type=jnp.float32
        )
        return ((prior_part, recur_total), input_part.astype(jnp.bfloat16))

    recur_zero = jnp.zeros((2, hidden_units, recur_back.shape[2]), jnp.float32)
    (_, recur_sum), input_seeds = lax.scan(
        back_step, (state_seed, recur_zero), (gates_in, steps_live, prior_states), reverse=True
    )
    input_mats = jnp.einsum(
        "cdtz,cdtg->dzg", steps_in, input_seeds, preferred_element_type=jnp.float32
    )
    step_chars = jnp.einsum(
        "cdtg,dzg->cdtz", input_seeds, inward_back, preferred_element_type=jnp.float32
    )
    char_grad = step_chars[:, 0].transpose(1, 0, 2) + step_chars[::-1, 1].transpose(1, 0, 2)
    char_grad = char_grad.astype(jnp.bfloat16).reshape(tokens * nchar, -1)
    table_grad = grad_dot(onehot, char_grad)
    gain_grad = jnp.stack([gain_one, gain_two, gain_three], 0)
    bias_grad = jnp.stack([bias_one, bias_two, bias_three], 0)
    input_flat = input_mats.reshape(-1, input_mats.shape[2])
    recur_flat = recur_sum.reshape(-1, recur_sum.shape[2])
    summed = (
        lax.psum_scatter(qkv_grad, ("dp", "seq"), scatter_dimension=0, tiled=True),
        lax.psum_scatter(out_grad, ("dp", "seq"), scatter_dimension=0, tiled=True),
        lax.psum_scatter(up_grad, ("dp", "seq"), scatter_dimension=0, tiled=True),
        lax.psum_scatter(down_grad, ("dp", "seq"), scatter_dimension=0, tiled=True),
        lax.psum_scatter(gain_grad, ("dp", "seq"), scatter_dimension=1, tiled=True),
        lax.psum_scatter(bias_grad, ("dp", "seq"), scatter_dimension=1, tiled=True),
        lax.psum_scatter(table_grad, ("dp", "seq"), scatter_dimension=0, tiled=True),
        lax.psum_scatter(input_flat, ("dp", "seq"), scatter_dimension=0, tiled=True),
        lax.psum_scatter(recur_flat, ("dp", "seq"), scatter_dimension=0, tiled=True),
        lax.psum_scatter(merge_grad, ("dp", "seq"), scatter_dimension=0, tiled=True),
        lax.psum_scatter(conv_grad, ("dp", "seq"), scatter_dimension=0, tiled=True),
    )
    return (result, hidden_grad) + tuple(summed)


def solution(mesh):
    placed = (
        P("dp", "seq", None),
        P("dp", "seq", None),
        P("dp"),
        P("dp"),
        P("dp", "seq", None),
        P(("dp", "seq"), None),
        P(("dp", "seq"), None),
        P(("dp", "seq"), None),
        P(("dp", "seq"), None),
        P(None, ("dp", "seq")),
        P(None, ("dp", "seq")),
        P(("dp", "seq"), None),
        P(("dp", "seq"), None),
        P(("dp", "seq"), None),
        P(("dp", "seq"), None),
        P(("dp", "seq"), None),
    )
    return jax.shard_map(
        local,
        mesh=mesh,
        in_specs=placed,
        out_specs=(
            P("dp", "seq", None),
            P("dp", "seq", None),
            P(("dp", "seq"), None),
            P(("dp", "seq"), None),
            P(("dp", "seq"), None),
            P(("dp", "seq"), None),
            P(None, ("dp", "seq")),
            P(None, ("dp", "seq")),
            P(("dp", "seq"), None),
            P(("dp", "seq"), None),
            P(("dp", "seq"), None),
            P(("dp", "seq"), None),
            P(("dp", "seq"), None),
        ),
        check_vma=False,
    )
```

profile of v0, /device:TPU:0, one launch (start us, length us, event | category | flops | bytes accessed | tf_op | source)
XLA Modules:
  0.0 1896.5 jit_solution(11569597928405346581)
XLA Ops:
  14.2 45.4 %all_gather.56 = bf16[1024,256]{1,0:T(8,128)(2,1)S(1)} all-gather(bf16[32,256]{1,0:T(8,128)(2,1)} %param.31), channel_id=1, replica_groups=mesh['dp'=8,'seq'=4] {'dp','seq'}, dimensions={0}, use_global_device_ids=true | all-gather | bytes 540672 | tf_op jit(solution)/shard_map/all_gather | solution.py:88
  64.4 36.7 %all-gather.3 = bf16[32,24,3]{1,2,0:T(4,128)(2,1)S(1)} all-gather(bf16[1,24,3]{1,2,0:T(4,128)(2,1)S(1)} %bitcast.285), channel_id=1, replica_groups=mesh['dp'=8,'seq'=4] {'dp','seq'}, dimensions={0}, use_global_device_ids=true | all-gather | bytes 4752 | tf_op jit(solution)/shard_map/all_gather | solution.py:87
  102.0 38.0 %all-gather.2 = bf16[32,24,3]{1,2,0:T(4,128)(2,1)S(1)} all-gather(bf16[1,24,3]{1,2,0:T(4,128)(2,1)S(1)} %bitcast.286), channel_id=1, replica_groups=mesh['dp'=8,'seq'=4] {'dp','seq'}, dimensions={0}, use_global_device_ids=true | all-gather | bytes 4752 | tf_op jit(solution)/shard_map/all_gather | solution.py:86
  145.1 6.8 copy.97
  151.9 71.8 %while.32 = (s32[]{:T(128)}, f32[2,128,384]{2,1,0:T(8,128)S(1)}, f32[16,2,128,384]{3,2,1,0:T(8,128)}, pred[16,2,128,1]{2,1,3,0:T(4,128)(4,1)S(1)}, f32[16,2,128,...) while((s32[]{:T(128)}, f32[2,128,384]{2,1,0:T(8,128)S(1)}, ...), condition=%wide.region_7.8_spmd.clone, body=%wide.region_6.7_spmd.clone.sunk | while | flops 228261888 | bytes 9634677 | solution.py:171
  226.1 19.5 %all-gather.13.cloned.1.call-done = bf16[768,2304]{1,0:T(8,128)(2,1)} async-done(((bf16[24,2304]{1,0:T(8,128)(2,1)}), bf16[768,2304]{1,0:T(8,128)(2,1)}) %all-gather.13.cloned.1.call-update) | async-done | bytes 3538960 | tf_op jit(solution)/shard_map/all_gather | solution.py:82
  248.4 8.6 all-gather
  258.3 9.2 all-gather.1
  273.2 28.0 %all-gather.15.cloned.1.call-done = bf16[768,768]{1,0:T(8,128)(2,1)} async-done(((bf16[24,768]{1,0:T(8,128)(2,1)}), bf16[768,768]{1,0:T(8,128)(2,1)}) %all-gather.15.cloned.1.call-update) | async-done | bytes 1179664 | tf_op jit(solution)/shard_map/all_gather | solution.py:83
  304.8 61.6 %all-gather.17.cloned.1.call-done = bf16[768,3072]{1,0:T(8,128)(2,1)} async-done(((bf16[24,3072]{1,0:T(8,128)(2,1)}), bf16[768,3072]{1,0:T(8,128)(2,1)}) %all-gather.17.cloned.1.call-update) | async-done | bytes 4718608 | tf_op jit(solution)/shard_map/all_gather | solution.py:84
  366.4 8.4 multiply_convert_fusion.2
  374.9 56.4 %all-gather.19.cloned.1.call-done = bf16[3072,768]{1,0:T(8,128)(2,1)} async-done(((bf16[96,768]{1,0:T(8,128)(2,1)}), bf16[3072,768]{1,0:T(8,128)(2,1)}) %all-gather.19.cloned.1.call-update) | async-done | bytes 4718608 | tf_op jit(solution)/shard_map/all_gather | solution.py:85
  441.6 63.0 %all-gather.27.cloned.1.call-done = bf16[4608,768]{1,0:T(8,128)(2,1)} async-done(((bf16[144,768]{1,0:T(8,128)(2,1)}), bf16[4608,768]{1,0:T(8,128)(2,1)}) %all-gather.27.cloned.1.call-update) | async-done | bytes 7077904 | tf_op jit(solution)/shard_map/all_gather | solution.py:92
  531.6 4.8 copy.112
  548.3 4.9 broadcast_in_dim.138.clone
  553.2 185.3 %while.33 = (s32[]{:T(128)}, f32[2,128,384]{2,1,0:T(8,128)S(1)}, f32[2,384,1152]{2,1,0:T(8,128)}, bf16[16,2,128,1152]{3,2,0,1:T(8,128)(2,1)}, pred[16,2,128,1]{2...) while((s32[]{:T(128)}, f32[2,128,384]{2,1,0:T(8,128)S(1)}, ...), condition=%wide.region_32.33_spmd.clone, body=%wide.region_31.32_spmd.clone.sunk | while | flops 688324608 | bytes 29689276 | solution.py:318
  738.6 5.8 convolution_bitcast_fusion.2
  751.7 8.0 fusion.66
  773.9 8.0 copy.114
  783.2 5.0 fusion.153
  789.5 5.0 fusion.138
  799.5 5.4 pad_maximum_fusion
  808.1 42.1 %all-reduce.7 = (f32[3,768]{1,0:T(4,128)}, f32[3,768]{1,0:T(4,128)}) all-reduce(f32[3,768]{1,0:T(4,128)S(1)} %pad_maximum_fusion.18, f32[3,768]{1,0:T(4,128)} %pad_maximum_fusion.19), channel_id=10, replica_groups=mesh['dp'=8,'seq'=4] {'dp','seq'}, use_global_device_ids=true, to_apply=%region_26.27.clone | all-reduce | flops 4608 | bytes 36864
  854.8 32.3 %reduce-scatter.28.cloned.1.call-done = f32[32,256]{1,0:T(8,128)} async-done(((f32[1024,256]{1,0:T(8,128)}), f32[32,256]{1,0:T(8,128)}) %reduce-scatter.28.cloned.1.call-update) | async-done | bytes 32784 | tf_op jit(solution)/shard_map/reduce_scatter | solution.py:341
  887.1 101.2 %reduce-scatter.22.cloned.1.call-done = f32[24,768]{1,0:T(8,128)} async-done(((f32[768,768]{1,0:T(8,128)}), f32[24,768]{1,0:T(8,128)}) %reduce-scatter.22.cloned.1.call-update) | async-done | bytes 73744 | tf_op jit(solution)/shard_map/reduce_scatter | solution.py:336
  988.3 104.5 %reduce-scatter.30.cloned.1.call-done = f32[16,1152]{1,0:T(8,128)} async-done(((f32[512,1152]{1,0:T(8,128)}), f32[16,1152]{1,0:T(8,128)}) %reduce-scatter.30.cloned.1.call-update) | async-done | bytes 73744 | tf_op jit(solution)/shard_map/reduce_scatter | solution.py:342
  1092.8 108.3 %reduce-scatter.42.cloned.1.call-done = f32[24,1152]{1,0:T(8,128)} async-done(((f32[768,1152]{1,0:T(8,128)}), f32[24,1152]{1,0:T(8,128)}) %reduce-scatter.42.cloned.1.call-update) | async-done | bytes 110608
  1201.1 112.8 %reduce-scatter.32.cloned.1.call-done = f32[48,768]{1,0:T(8,128)} async-done(((f32[1536,768]{1,0:T(8,128)}), f32[48,768]{1,0:T(8,128)}) %reduce-scatter.32.cloned.1.call-update) | async-done | bytes 147472 | tf_op jit(solution)/shard_map/reduce_scatter | solution.py:344
  1313.9 124.6 %reduce-scatter.40.cloned.1.call-done = f32[24,2304]{1,0:T(8,128)} async-done(((f32[768,2304]{1,0:T(8,128)}), f32[24,2304]{1,0:T(8,128)}) %reduce-scatter.40.cloned.1.call-update) | async-done | bytes 221200
  1438.5 141.5 %reduce-scatter.24.cloned.1.call-done = f32[24,3072]{1,0:T(8,128)} async-done(((f32[768,3072]{1,0:T(8,128)}), f32[24,3072]{1,0:T(8,128)}) %reduce-scatter.24.cloned.1.call-update) | async-done | bytes 294928 | tf_op jit(solution)/shard_map/reduce_scatter | solution.py:337
  1580.0 141.5 %reduce-scatter.26.cloned.1.call-done = f32[96,768]{1,0:T(8,128)} async-done(((f32[3072,768]{1,0:T(8,128)}), f32[96,768]{1,0:T(8,128)}) %reduce-scatter.26.cloned.1.call-update) | async-done | bytes 294928 | tf_op jit(solution)/shard_map/reduce_scatter | solution.py:338
  1721.4 168.1 %reduce-scatter.34.cloned.1.call-done = f32[144,768]{1,0:T(8,128)} async-done(((f32[4608,768]{1,0:T(8,128)}), f32[144,768]{1,0:T(8,128)}) %reduce-scatter.34.cloned.1.call-update) | async-done | bytes 442384 | tf_op jit(solution)/shard_map/reduce_scatter | solution.py:345
  (594 shorter events, 372.8 us)
Async XLA Ops:
  7.2 133.8 %all-gather.23.cloned.1.call-start = ((), (), s32[]{:S(2)}) async-start(), calls=%async_computation.16 | async-start | bytes 1216512 | tf_op jit(solution)/shard_map/all_gather | solution.py:89
  7.9 144.0 %all-gather.25.cloned.1.call-start = ((), (), s32[]{:S(2)}) async-start(), calls=%async_computation.17 | async-start | bytes 1824768 | tf_op jit(solution)/shard_map/all_gather | solution.py:90
  8.7 215.2 %all-gather.21.cloned.1.call-start = ((), (), s32[]{:S(2)}) async-start(), calls=%async_computation.15 | async-start | bytes 2433024 | tf_op jit(solution)/shard_map/all_gather | solution.py:91
  9.4 236.2 %all-gather.13.cloned.1.call-start = ((), (), s32[]{:S(2)}) async-start(), calls=%async_computation.11 | async-start | bytes 3649536 | tf_op jit(solution)/shard_map/all_gather | solution.py:82
  10.0 291.2 %all-gather.15.cloned.1.call-start = ((), (), s32[]{:S(2)}) async-start(), calls=%async_computation.12 | async-start | bytes 1216512 | tf_op jit(solution)/shard_map/all_gather | solution.py:83
  10.6 355.9 %all-gather.17.cloned.1.call-start = ((), (), s32[]{:S(2)}) async-start(), calls=%async_computation.13 | async-start | bytes 4866048 | tf_op jit(solution)/shard_map/all_gather | solution.py:84
  11.1 420.1 %all-gather.19.cloned.1.call-start = ((), (), s32[]{:S(2)}) async-start(), calls=%async_computation.14 | async-start | bytes 4866048 | tf_op jit(solution)/shard_map/all_gather | solution.py:85
  11.9 492.6 %all-gather.27.cloned.1.call-start = ((), (), s32[]{:S(2)}) async-start(), calls=%async_computation.18 | async-start | bytes 7299072 | tf_op jit(solution)/shard_map/all_gather | solution.py:92
  12.6 754.2 %reduce-scatter.38.cloned.1.call-start = ((), (), s32[]{:S(2)}) async-start(), calls=%async_computation.27 | async-start | bytes 983040
  63.2 38.8 %copy-start.81 = (bf16[3,24]{1,0:T(4,128)(2,1)S(1)}, bf16[3,24]{1,0:T(4,128)(2,1)}, u32[]{:S(2)}) copy-start(bf16[3,24]{1,0:T(4,128)(2,1)} %param.29) | copy-start | bytes 436
  63.3 81.8 %copy-start.14 = (bf16[1,128,16,256]{3,1,2,0:T(8,128)(2,1)}, bf16[1,128,16,256]{3,1,2,0:T(8,128)(2,1)S(1)}, u32[]{:S(2)}) copy-start(bf16[1,128,16,256]{3,1,2,0:T(8,128)(2,1)S(1)} %reverse_bitcast_fusion) | copy-start | bytes 3145732
  63.7 81.4 %copy-start.16 = (bf16[1,128,16,256]{3,1,2,0:T(8,128)(2,1)}, bf16[1,128,16,256]{3,1,2,0:T(8,128)(2,1)S(1)}, u32[]{:S(2)}) copy-start(bf16[1,128,16,256]{3,1,2,0:T(8,128)(2,1)S(1)} %copy.95) | copy-start | bytes 3145732
  64.4 207.0 %copy-start.68 = (pred[512]{0:T(512)(128)(4,1)}, pred[512]{0:T(512)(128)(4,1)S(1)}, u32[]{:S(2)}) copy-start(pred[512]{0:T(512)(128)(4,1)S(1)} %iota_compare_fusion.5) | copy-start | bytes 1540
  223.7 24.6 %copy-start.67 = (pred[16,2,128,1]{2,1,3,0:T(4,128)(4,1)}, pred[16,2,128,1]{2,1,3,0:T(4,128)(4,1)S(1)}, u32[]{:S(2)}) copy-start(pred[16,2,128,1]{2,1,3,0:T(4,128)(4,1)S(1)} %get-tuple-element.672) | copy-start | bytes 12292
  223.8 24.5 %copy-start.45 = (bf16[128,384]{1,0:T(8,128)(2,1)}, bf16[128,384]{1,0:T(8,128)(2,1)S(1)}, u32[]{:S(2)}) copy-start(bf16[128,384]{1,0:T(8,128)(2,1)S(1)} %get-tuple-element.434) | copy-start | bytes 294916
  223.8 24.5 %copy-start.47 = (bf16[128,384]{1,0:T(8,128)(2,1)}, bf16[128,384]{1,0:T(8,128)(2,1)S(1)}, u32[]{:S(2)}) copy-start(bf16[128,384]{1,0:T(8,128)(2,1)S(1)} %get-tuple-element.435) | copy-start | bytes 294916
  302.9 224.5 %copy-start.2 = (f32[128,768]{1,0:T(8,128)}, f32[128,768]{1,0:T(8,128)S(1)}, u32[]{:S(2)}) copy-start(f32[128,768]{1,0:T(8,128)S(1)} %get-tuple-element.439) | copy-start | bytes 1179652
  436.6 70.4 %collective-permute-start.1 = (bf16[1,1,1536]{2,1,0:T(2,128)(2,1)}, bf16[1,1,1536]{2,1,0:T(2,128)(2,1)}, u32[]{:S(2)}, u32[]{:S(2)}) collective-permute-start(bf16[1,1,1536]{2,1,0:T(2,128)(2,1)} %get-tuple-element.431), channel_id=1, source_target_pairs={{1,0},{2,1},{3,2},{5,4},{6,5},{7,6},{9,8},{10,9},{11,10},{13,12},{... | collective-permute-start | bytes 9224 | tf_op jit(solution)/shard_map/ppermute | solution.py:23
  437.9 72.0 %collective-permute-start = (bf16[1,1,1536]{2,1,0:T(2,128)(2,1)}, bf16[1,1,1536]{2,1,0:T(2,128)(2,1)}, u32[]{:S(2)}, u32[]{:S(2)}) collective-permute-start(bf16[1,1,1536]{2,1,0:T(2,128)(2,1)} %get-tuple-element.430), channel_id=1, source_target_pairs={{0,1},{1,2},{2,3},{4,5},{5,6},{6,7},{8,9},{9,10},{10,11},{12,13},{... | collective-permute-start | bytes 9224 | tf_op jit(solution)/shard_map/ppermute | solution.py:22
  513.5 4.5 collective-permute-start.3
  515.7 3.9 collective-permute-start.2
  538.8 229.6 %reduce-scatter.36.cloned.1.call-start = ((), (), s32[]{:S(2)}) async-start(), calls=%async_computation.26 | async-start | bytes 983040
  548.0 339.1 %reduce-scatter.28.cloned.1.call-start = ((), (), s32[]{:S(2)}) async-start(), calls=%async_computation.22 | async-start | bytes 1081344 | tf_op jit(solution)/shard_map/reduce_scatter | solution.py:341
  749.6 238.8 %reduce-scatter.22.cloned.1.call-start = ((), (), s32[]{:S(2)}) async-start(), calls=%async_computation.19 | async-start | bytes 2433024 | tf_op jit(solution)/shard_map/reduce_scatter | solution.py:336
  751.7 341.1 %reduce-scatter.30.cloned.1.call-start = ((), (), s32[]{:S(2)}) async-start(), calls=%async_computation.23 | async-start | bytes 2433024 | tf_op jit(solution)/shard_map/reduce_scatter | solution.py:342
  759.8 441.3 %reduce-scatter.42.cloned.1.call-start = ((), (), s32[]{:S(2)}) async-start(), calls=%async_computation.29 | async-start | bytes 3649536
  760.4 553.4 %reduce-scatter.32.cloned.1.call-start = ((), (), s32[]{:S(2)}) async-start(), calls=%async_computation.24 | async-start | bytes 4866048 | tf_op jit(solution)/shard_map/reduce_scatter | solution.py:344
  764.5 674.0 %reduce-scatter.40.cloned.1.call-start = ((), (), s32[]{:S(2)}) async-start(), calls=%async_computation.28 | async-start | bytes 7299072
  782.0 798.0 %reduce-scatter.24.cloned.1.call-start = ((), (), s32[]{:S(2)}) async-start(), calls=%async_computation.20 | async-start | bytes 9732096 | tf_op jit(solution)/shard_map/reduce_scatter | solution.py:337
  788.3 933.1 %reduce-scatter.26.cloned.1.call-start = ((), (), s32[]{:S(2)}) async-start(), calls=%async_computation.21 | async-start | bytes 9732096 | tf_op jit(solution)/shard_map/reduce_scatter | solution.py:338
  794.6 1095.0 %reduce-scatter.34.cloned.1.call-start = ((), (), s32[]{:S(2)}) async-start(), calls=%async_computation.25 | async-start | bytes 14598144 | tf_op jit(solution)/shard_map/reduce_scatter | solution.py:345
  804.9 46.7 %copy-start.20 = (bf16[768,2304]{1,0:T(8,128)(2,1)S(1)}, bf16[768,2304]{1,0:T(8,128)(2,1)}, u32[]{:S(2)}) copy-start(bf16[768,2304]{1,0:T(8,128)(2,1)} %all-gather.13.cloned.1.call-done) | copy-start | bytes 10616836
  (101 other events, 254.1 us)
Sparse Core Ops, SparseCore 0:
  10.9 56.9 all-gather.22
  70.7 54.4 all-gather.24
  128.1 55.8 all-gather.20
  186.8 58.7 all-gather.12
  248.4 52.7 all-gather.14
  303.9 62.4 all-gather.16
  369.3 61.8 all-gather.18
  434.1 70.3 all-gather.26
  538.9 23.8 reduce-scatter.37
  565.2 23.1 reduce-scatter.35
  749.7 137.4 reduce-scatter.27
  892.9 95.4 reduce-scatter.21
  994.2 98.5 reduce-scatter.29
  1098.7 102.4 reduce-scatter.41
  1207.0 106.8 reduce-scatter.31
  1320.0 118.4 reduce-scatter.39
  1444.8 135.1 reduce-scatter.23
  1586.3 135.0 reduce-scatter.25
  1728.0 161.4 reduce-scatter.33
where the time goes:
time: 1910 us; the launch traced here: 1900 us
  waiting for transfers between devices  1270 us (66%)
  matrix products  233 us (12%)
  blocking collectives  180 us (9%)
  local copies, waits for them, and re-layouts  107 us (6%)
  other arithmetic  78.5 us (4%)
    unnamed x23, waiting for transfers between devices  239 us
    reduce_scatter x1, waiting for transfers between devices, local(): lax.psum_scatter(conv_grad, ('dp', 'seq'), scatter_dimension=0, tiled=True)  168 us
    reduce_scatter x1, waiting for transfers between devices, local(): lax.psum_scatter(up_grad, ('dp', 'seq'), scatter_dimension=0, tiled=True)  141 us
    reduce_scatter x1, waiting for transfers between devices, local(): lax.psum_scatter(down_grad, ('dp', 'seq'), scatter_dimension=0, tiled=True)  141 us
    reduce_scatter x1, waiting for transfers between devices, local(): lax.psum_scatter(merge_grad, ('dp', 'seq'), scatter_dimension=0, tiled=True)  113 us
    reduce_scatter x1, waiting for transfers between devices, local(): lax.psum_scatter(input_flat, ('dp', 'seq'), scatter_dimension=0, tiled=True)  104 us
    reduce_scatter x1, waiting for transfers between devices, local(): lax.psum_scatter(out_grad, ('dp', 'seq'), scatter_dimension=0, tiled=True)  101 us
    dot_general x16, matrix products, back_step(): jnp.einsum('dth,dtg->dhg', state_low, recur_low, preferred_element_type=j...  73.6 us
  transfers between devices with their start and end apart: 23, of which 15 were waited for; matrix products, arithmetic and copies ran while one was open for 20% of the time, Pallas kernels for 0%

commit v1 on v0

--- a/solution.py
+++ b/solution.py
@@ -1,15 +1,377 @@
+import functools
 import math
 
 import jax
 import jax.numpy as jnp
 from jax import lax
+from jax.experimental import pallas as pl
+from jax.experimental.pallas import tpu as pltpu
 from jax.sharding import PartitionSpec as P
+
+MESH = pl.DeviceIdType.MESH
 
 HD = 64
 SUBV = 128
 
-
 eps = 1e-05
+
+class Place:
+    def __init__(self, dp_size):
+        dp, seq = lax.axis_index("dp"), lax.axis_index("seq")
+        self.lines = dp_size // 2
+        self.a, self.b = dp // 2, lax.rem(dp, 2)
+        self.y, self.c = seq // 2, lax.rem(seq, 2)
+        flip_b = (self.a * 2 + 1 - self.b, seq)
+        flip_y = (dp, (1 - self.y) * 2 + self.c)
+        pick = lambda u, v: tuple(i + self.c * (j - i) for i, j in zip(u, v))
+        self.first, self.second = pick(flip_b, flip_y), pick(flip_y, flip_b)
+        self.sibling = (dp, self.y * 2 + 1 - self.c)
+        self.up, self.down = (dp + 2, seq), (dp - 2, seq)
+        self.f = self.b + self.c * (self.y - self.b)
+        self.s = self.y + self.c * (self.b - self.y)
+        self.has_up, self.has_down = self.a < self.lines - 1, self.a > 0
+
+    def unit(self, a, f, s, c=None):
+        c = self.c if c is None else c
+        return a * 8 + f * (4 - 2 * c) + s * (2 + 2 * c) + c
+
+    def barrier(self):
+        sem = pltpu.get_barrier_semaphore()
+        for who in (self.first, self.second, self.sibling):
+            pl.semaphore_signal(sem, inc=1, device_id=who, device_id_type=MESH)
+
+        @pl.when(self.has_up)
+        def _():
+            pl.semaphore_signal(sem, inc=1, device_id=self.up, device_id_type=MESH)
+
+        @pl.when(self.has_down)
+        def _():
+            pl.semaphore_signal(sem, inc=1, device_id=self.down, device_id_type=MESH)
+
+        pl.semaphore_wait(sem, 3 + self.has_up.astype(jnp.int32) + self.has_down.astype(jnp.int32))
+
+
+def push(src, dst, send, recv, who):
+    return pltpu.make_async_remote_copy(
+        src_ref=src, dst_ref=dst, send_sem=send, recv_sem=recv, device_id=who, device_id_type=MESH
+    )
+
+
+class Gather:
+    def __init__(self, at, shard, full, sems):
+        self.at, self.shard, self.full = at, shard, full
+        self.up_s, self.down_s, self.sum_s, self.line_r, self.second_r, self.one = sems
+
+    def to_lines(self, src, slot, index, up, down):
+        at = self.at
+        if up is not False:
+            @pl.when(at.has_up if up is True else jnp.logical_and(up, at.has_up))
+            def _():
+                push(src, self.full.at[index], self.up_s.at[slot], self.line_r.at[slot], at.up).start()
+        if down is not False:
+            @pl.when(at.has_down if down is True else jnp.logical_and(down, at.has_down))
+            def _():
+                push(src, self.full.at[index], self.down_s.at[slot], self.line_r.at[slot], at.down).start()
+
+    def across(self, src, slot, index):
+        push(src, self.full.at[index], self.sum_s.at[0], self.second_r.at[slot], self.at.second).start()
+        self.aside(src, index)
+
+    def aside(self, src, index):
+        push(src, self.full.at[index], self.sum_s.at[1], self.one.at[1], self.at.sibling).start()
+
+    def begin(self):
+        at = self.at
+        me = at.unit(at.a, at.f, at.s)
+        pltpu.make_async_copy(self.shard, self.full.at[me], self.one.at[3]).start()
+        push(self.shard, self.full.at[me], self.one.at[2], self.one.at[0], at.first).start()
+        slot = at.a * 2 + at.f
+        self.to_lines(self.shard, slot, me, True, True)
+        self.across(self.shard, slot, me)
+
+    def after_first(self):
+        at = self.at
+        index = at.unit(at.a, 1 - at.f, at.s)
+        ref = self.full.at[index]
+        push(ref, ref, self.one.at[2], self.one.at[0], at.first).wait_recv()
+        slot = at.a * 2 + 1 - at.f
+        self.to_lines(ref, slot, index, True, True)
+        self.across(ref, slot, index)
+
+    def after_line(self, k, g):
+        at = self.at
+        for sign in (-1, 1):
+            a = at.a + sign * k
+            f = at.f if g == 0 else 1 - at.f
+
+            @pl.when(a >= 0 if sign < 0 else a < at.lines)
+            def _():
+                index, slot = at.unit(a, f, at.s), a * 2 + f
+                ref = self.full.at[index]
+                push(ref, ref, self.up_s.at[slot], self.line_r.at[slot], at.up).wait_recv()
+                self.to_lines(ref, slot, index, sign < 0, sign > 0)
+                self.across(ref, slot, index)
+
+    def after_second(self, k, g):
+        at = self.at
+        for sign in (-1, 1) if k else (1,):
+            a = at.a + sign * k
+            f = at.f if g == 0 else 1 - at.f
+
+            @pl.when(a >= 0 if sign < 0 else a < at.lines)
+            def _():
+                index, slot = at.unit(a, f, 1 - at.s), a * 2 + f
+                ref = self.full.at[index]
+                push(ref, ref, self.sum_s.at[0], self.second_r.at[slot], at.second).wait_recv()
+                self.aside(ref, index)
+
+    def finish(self):
+        at, n = self.at, self.at.lines
+        me = at.unit(at.a, at.f, at.s)
+        half = self.full.at[pl.ds(0, 4 * n)]
+        push(half, half, self.sum_s.at[1], self.one.at[1], at.sibling).wait_recv()
+        pltpu.make_async_copy(self.shard, self.full.at[me], self.one.at[3]).wait()
+        push(self.shard, self.full.at[me], self.one.at[2], self.one.at[0], at.first).wait_send()
+        push(half, half, self.sum_s.at[1], self.one.at[1], at.sibling).wait_send()
+        part = self.full.at[pl.ds(0, 2 * n)]
+        push(part, part, self.sum_s.at[0], self.one.at[0], at.second).wait_send()
+        for a in range(n):
+            for f in range(2):
+                slot = a * 2 + f
+                ref = self.full.at[0]
+
+                @pl.when(jnp.logical_and(at.has_up, a <= at.a))
+                def _():
+                    push(ref, ref, self.up_s.at[slot], self.line_r.at[slot], at.up).wait_send()
+
+                @pl.when(jnp.logical_and(at.has_down, a >= at.a))
+                def _():
+                    push(ref, ref, self.down_s.at[slot], self.line_r.at[slot], at.down).wait_send()
+
+
+def gather_sems(n):
+    dma = pltpu.SemaphoreType.DMA
+    return [dma((2 * n,)), dma((2 * n,)), dma((2,)), dma((2 * n,)), dma((2 * n,)), dma((4,))]
+
+
+def gather_kernel(dp_size, count, *refs):
+    shards, fulls, sems = refs[:count], refs[count : 2 * count], refs[2 * count :]
+    at = Place(dp_size)
+    at.barrier()
+    jobs = [Gather(at, shards[i], fulls[i], sems[6 * i : 6 * i + 6]) for i in range(count)]
+    for job in jobs:
+        job.begin()
+    for job in jobs:
+        job.after_first()
+    for k in range(1, at.lines):
+        for g in range(2):
+            for job in jobs:
+                job.after_line(k, g)
+            for job in jobs:
+                job.after_second(k - 1, g)
+    for g in range(2):
+        for job in jobs:
+            job.after_second(at.lines - 1, g)
+    for job in jobs:
+        job.finish()
+
+
+def gather_all(dp_size, devices, shards, cid=1):
+    count = len(shards)
+    return pl.pallas_call(
+        functools.partial(gather_kernel, dp_size, count),
+        out_shape=[jax.ShapeDtypeStruct((devices,) + x.shape, x.dtype) for x in shards],
+        in_specs=[pl.BlockSpec(memory_space=pl.ANY)] * count,
+        out_specs=[pl.BlockSpec(memory_space=pl.ANY)] * count,
+        scratch_shapes=gather_sems(dp_size // 2) * count,
+        compiler_params=pltpu.CompilerParams(collective_id=cid, has_side_effects=True),
+    )(*shards)
+
+
+def wide(x):
+    return x.astype(jnp.float32)
+
+
+def add_into(dst, src):
+    dst[...] = (wide(dst[...]) + wide(src[...])).astype(dst.dtype)
+
+
+class Scatter:
+    def __init__(self, at, part, out, bufs, sems):
+        self.at, self.part, self.out = at, part, out
+        self.own, self.sib, self.sec, self.line, self.fst = bufs
+        self.one, self.line_s, self.line_r = sems
+
+    def begin(self):
+        at = self.at
+
+        def body(j, carry):
+            a, f, s = j // 4, lax.rem(j // 2, 2), lax.rem(j, 2)
+            push(self.part.at[at.unit(a, f, s, 1 - at.c)], self.sib.at[j], self.one.at[0], self.one.at[1], at.sibling).start()
+            return carry
+
+        lax.fori_loop(0, 4 * at.lines, body, 0)
+
+        def load(j, carry):
+            a, f, s = j // 4, lax.rem(j // 2, 2), lax.rem(j, 2)
+            pltpu.make_async_copy(self.part.at[at.unit(a, f, s)], self.own.at[j], self.one.at[2]).start()
+            return carry
+
+        lax.fori_loop(0, 4 * at.lines, load, 0)
+
+    def after_sibling(self):
+        at = self.at
+        n = 2 * at.lines
+        pltpu.make_async_copy(self.part.at[pl.ds(0, 2 * n)], self.own, self.one.at[2]).wait()
+        push(self.sib, self.sib, self.one.at[0], self.one.at[1], at.sibling).wait_recv()
+
+        def far(q, carry):
+            j = q * 2 + 1 - at.s
+            add_into(self.own.at[j], self.sib.at[j])
+            return carry
+
+        def send(q, carry):
+            push(self.own.at[q * 2 + 1 - at.s], self.sec.at[q], self.one.at[3], self.one.at[4], at.second).start()
+            return carry
+
+        def near(q, carry):
+            j = q * 2 + at.s
+            add_into(self.own.at[j], self.sib.at[j])
+            return carry
+
+        lax.fori_loop(0, n, far, 0)
+        lax.fori_loop(0, n, send, 0)
+        lax.fori_loop(0, n, near, 0)
+
+    def after_second(self):
+        at = self.at
+        push(self.sec, self.sec, self.one.at[3], self.one.at[4], at.second).wait_recv()
+
+        def body(q, carry):
+            add_into(self.own.at[q * 2 + at.s], self.sec.at[q])
+            return carry
+
+        lax.fori_loop(0, 2 * at.lines, body, 0)
+
+    def hop(self, low, high, inward, dst, extra):
+        at = self.at
+        has, who = (at.has_up, at.down) if dst < 0 else (at.has_down, at.up)
+
+        def take(q, carry):
+            push(self.line.at[q], self.line.at[q], self.line_s.at[q], self.line_r.at[q], who).wait_recv()
+            add_into(self.own.at[q * 2 + at.s], self.line.at[q])
+            return carry
+
+        @pl.when(has)
+        def _():
+            lax.fori_loop(low, high, take, 0)
+
+        def send(q, carry):
+            slot = q if dst < 0 else jnp.where(q // 2 == at.a + 1, 2 * at.lines + lax.rem(q, 2), q)
+            push(self.own.at[q * 2 + at.s], self.line.at[slot], self.line_s.at[q], self.line_r.at[slot], who).start()
+            return carry
+
+        lax.fori_loop(low, high, send, 0)
+
+    def along(self, h):
+        at = self.at
+        n = at.lines
+        hops = n - 1 if n <= 4 else 1
+
+        @pl.when(jnp.logical_and(at.has_down, at.lines - 1 - at.a == h) if hops > 1 else at.has_down)
+        def _():
+            self.hop(0, 2 * at.a, at.up, -1, None)
+
+        @pl.when(jnp.logical_and(at.has_up, at.a == h) if hops > 1 else at.has_up)
+        def _():
+            self.hop(2 * at.a + 2, 2 * n, at.down, 1, None)
+
+    def ends(self, f, into):
+        at = self.at
+        for has, slot in ((at.has_up, 2 * at.a + f), (at.has_down, 2 * at.lines + f)):
+            @pl.when(has)
+            def _():
+                ref = self.line.at[slot]
+                push(ref, ref, self.line_s.at[0], self.line_r.at[slot], at.first).wait_recv()
+                into[...] = (wide(into[...]) + wide(ref[...])).astype(into.dtype)
+
+    def last_send(self):
+        at = self.at
+        mine = self.own.at[(2 * at.a + 1 - at.f) * 2 + at.s]
+        self.ends(1 - at.f, mine)
+        push(mine, self.fst, self.one.at[5], self.one.at[6], at.first).start()
+        self.out[...] = wide(self.own[(2 * at.a + at.f) * 2 + at.s])
+        self.ends(at.f, self.out)
+
+    def finish(self):
+        at = self.at
+        push(self.fst, self.fst, self.one.at[5], self.one.at[6], at.first).wait_recv()
+        self.out[...] = self.out[...] + wide(self.fst[...])
+
+    def drain(self):
+        at = self.at
+        n = at.lines
+        push(self.sib, self.sib, self.one.at[0], self.one.at[1], at.sibling).wait_send()
+        push(self.sec, self.sec, self.one.at[3], self.one.at[4], at.second).wait_send()
+        push(self.fst, self.fst, self.one.at[5], self.one.at[6], at.first).wait_send()
+
+        def body(q, carry):
+            @pl.when(q // 2 != at.a)
+            def _():
+                push(self.own.at[q], self.own.at[q], self.line_s.at[q], self.line_r.at[q], at.first).wait_send()
+            return carry
+
+        lax.fori_loop(0, 2 * n, body, 0)
+
+
+def scatter_buffers(n, shape, dtype):
+    v = lambda k: pltpu.VMEM((k,) + shape, dtype)
+    return [v(4 * n), v(4 * n), v(2 * n), v(2 * n + 2), pltpu.VMEM(shape, dtype)]
+
+
+def scatter_sems(n):
+    dma = pltpu.SemaphoreType.DMA
+    return [dma((7,)), dma((2 * n,)), dma((2 * n + 2,))]
+
+
+def scatter_stages(lines):
+    hops = lines - 1 if lines <= 4 else 1
+    stages = [Scatter.after_sibling, Scatter.after_second]
+    for h in range(hops):
+        stages.append(functools.partial(Scatter.along, h=h))
+    return stages + [Scatter.last_send, Scatter.finish]
+
+
+def scatter_kernel(dp_size, count, *refs):
+    parts, outs, rest = refs[:count], refs[count : 2 * count], refs[2 * count :]
+    at = Place(dp_size)
+    at.barrier()
+    jobs = [Scatter(at, parts[i], outs[i], rest[8 * i : 8 * i + 5], rest[8 * i + 5 : 8 * i + 8]) for i in range(count)]
+    for job in jobs:
+        job.begin()
+    stages = scatter_stages(at.lines)
+    for t in range(count + len(stages) - 1):
+        for k, stage in enumerate(stages):
+            if 0 <= t - k < count:
+                stage(jobs[t - k])
+    for job in jobs:
+        job.drain()
+
+
+def scatter_all(dp_size, parts, cid=2):
+    count = len(parts)
+    n = dp_size // 2
+    scratch = []
+    for x in parts:
+        scratch += scatter_buffers(n, x.shape[1:], x.dtype) + scatter_sems(n)
+    return pl.pallas_call(
+        functools.partial(scatter_kernel, dp_size, count),
+        out_shape=[jax.ShapeDtypeStruct(x.shape[1:], jnp.float32) for x in parts],
+        in_specs=[pl.BlockSpec(memory_space=pl.ANY)] * count,
+        out_specs=[pl.BlockSpec(memory_space=pltpu.VMEM)] * count,
+        scratch_shapes=scratch,
+        compiler_params=pltpu.CompilerParams(collective_id=cid, has_side_effects=True, vmem_limit_bytes=64000000),
+    )(*parts)
 
 
 def with_halo(x, sides, width):
@@ -58,6 +420,20 @@
     return lax.dot_general(
         left, right, (((1,), (1,)), ((), ())), preferred_element_type=jnp.float32
     )
+
+
+def pack_norms(gain, bias, devices=1):
+    both = jnp.stack([gain, bias], 0)
+    both = both.reshape(2, 3, devices, -1).transpose(2, 0, 1, 3).reshape(devices, -1)
+    both = jnp.pad(both, ((0, 0), (0, 1024 - both.shape[1]))).reshape(devices, 8, 128)
+    return both[0] if devices == 1 else both
+
+
+def unpack_norms(tiles, shape):
+    devices = tiles.shape[0]
+    flat = tiles.reshape(devices, -1)[:, : 2 * shape[0] * shape[1]].reshape(devices, 2, *shape)
+    both = flat.transpose(1, 2, 0, 3).reshape(2, shape[0], -1)
+    return both[0], both[1]
 
 
 def local(
@@ -78,32 +454,15 @@
     merge_weight,
     conv_weight,
 ):
-    gathered = (
-        lax.all_gather(qkv_weight, ("dp", "seq"), axis=0, tiled=True),
-        lax.all_gather(out_weight, ("dp", "seq"), axis=0, tiled=True),
-        lax.all_gather(up_weight, ("dp", "seq"), axis=0, tiled=True),
-        lax.all_gather(down_weight, ("dp", "seq"), axis=0, tiled=True),
-        lax.all_gather(norm_gain, ("dp", "seq"), axis=1, tiled=True),
-        lax.all_gather(norm_bias, ("dp", "seq"), axis=1, tiled=True),
-        lax.all_gather(char_table, ("dp", "seq"), axis=0, tiled=True),
-        lax.all_gather(gru_input, ("dp", "seq"), axis=0, tiled=True),
-        lax.all_gather(gru_recur, ("dp", "seq"), axis=0, tiled=True),
-        lax.all_gather(merge_weight, ("dp", "seq"), axis=0, tiled=True),
-        lax.all_gather(conv_weight, ("dp", "seq"), axis=0, tiled=True),
-    )
-    (
-        full_qkv,
-        full_out,
-        full_up,
-        full_down,
-        full_gain,
-        full_bias,
-        full_table,
-        full_input,
-        full_recur,
-        full_merge,
-        full_conv,
-    ) = gathered
+    dp_size, devices = lax.axis_size("dp"), lax.axis_size("dp") * lax.axis_size("seq")
+    norms = pack_norms(norm_gain, norm_bias)
+    order = (char_table, gru_input, gru_recur, norms, qkv_weight, out_weight, up_weight, down_weight, merge_weight, conv_weight)
+    gathered = gather_all(dp_size, devices, order)
+    full_norms = gathered[3]
+    (full_table, full_input, full_recur, _, full_qkv, full_out, full_up, full_down, full_merge, full_conv) = [
+        x.reshape(-1, x.shape[2]) for x in gathered
+    ]
+    full_gain, full_bias = unpack_norms(full_norms, norm_gain.shape)
     seq_count, local_len, features = hidden.shape
     nchar = char_ids.shape[2]
     tokens = seq_count * local_len
@@ -187,17 +546,8 @@
     resid_three = norm_two.astype(jnp.float32) + conv_out
     result_rows, pull_three = jax.vjp(norm_rows, resid_three, gains[2], biases[2])
     result = result_rows.astype(jnp.bfloat16).reshape(seq_count, local_len, features)
-    back_set = (
-        lax.all_gather(qkv_weight, ("dp", "seq"), axis=0, tiled=True),
-        lax.all_gather(out_weight, ("dp", "seq"), axis=0, tiled=True),
-        lax.all_gather(up_weight, ("dp", "seq"), axis=0, tiled=True),
-        lax.all_gather(down_weight, ("dp", "seq"), axis=0, tiled=True),
-        lax.all_gather(gru_input, ("dp", "seq"), axis=0, tiled=True),
-        lax.all_gather(gru_recur, ("dp", "seq"), axis=0, tiled=True),
-        lax.all_gather(merge_weight, ("dp", "seq"), axis=0, tiled=True),
-        lax.all_gather(conv_weight, ("dp", "seq"), axis=0, tiled=True),
-    )
-    back_qkv, back_out, back_up, back_down, back_input, back_recur, back_merge, back_conv = back_set
+    back_qkv, back_out, back_up, back_down = full_qkv, full_out, full_up, full_down
+    back_input, back_recur, back_merge, back_conv = full_input, full_recur, full_merge, full_conv
     merge_back = back_merge.reshape(2, features, features)
     kernel_back = back_conv.reshape(3, 2 * features, features)
     inward_back = back_input.reshape(2, -1, back_input.shape[1])
@@ -331,20 +681,13 @@
     bias_grad = jnp.stack([bias_one, bias_two, bias_three], 0)
     input_flat = input_mats.reshape(-1, input_mats.shape[2])
     recur_flat = recur_sum.reshape(-1, recur_sum.shape[2])
-    summed = (
-        lax.psum_scatter(qkv_grad, ("dp", "seq"), scatter_dimension=0, tiled=True),
-        lax.psum_scatter(out_grad, ("dp", "seq"), scatter_dimension=0, tiled=True),
-        lax.psum_scatter(up_grad, ("dp", "seq"), scatter_dimension=0, tiled=True),
-        lax.psum_scatter(down_grad, ("dp", "seq"), scatter_dimension=0, tiled=True),
-        lax.psum_scatter(gain_grad, ("dp", "seq"), scatter_dimension=1, tiled=True),
-        lax.psum_scatter(bias_grad, ("dp", "seq"), scatter_dimension=1, tiled=True),
-        lax.psum_scatter(table_grad, ("dp", "seq"), scatter_dimension=0, tiled=True),
-        lax.psum_scatter(input_flat, ("dp", "seq"), scatter_dimension=0, tiled=True),
-        lax.psum_scatter(recur_flat, ("dp", "seq"), scatter_dimension=0, tiled=True),
-        lax.psum_scatter(merge_grad, ("dp", "seq"), scatter_dimension=0, tiled=True),
-        lax.psum_scatter(conv_grad, ("dp", "seq"), scatter_dimension=0, tiled=True),
-    )
-    return (result, hidden_grad) + tuple(summed)
+    terms = [merge_grad, conv_grad, down_grad, up_grad, out_grad, qkv_grad, recur_flat, input_flat, table_grad]
+    parts = [x.astype(jnp.bfloat16).reshape(devices, -1, x.shape[1]) for x in terms]
+    parts.append(pack_norms(gain_grad, bias_grad, devices))
+    sums = scatter_all(dp_size, parts)
+    merge_sum, conv_sum, down_sum, up_sum, out_sum, qkv_sum, recur_total, input_total, table_sum, norm_sum = sums
+    gain_sum, bias_sum = unpack_norms(norm_sum[None], norm_gain.shape)
+    return (result, hidden_grad, qkv_sum, out_sum, up_sum, down_sum, gain_sum, bias_sum, table_sum, input_total, recur_total, merge_sum, conv_sum)
 
 
 def solution(mesh):

time: 1910 us -> 881 us (0.46)
  waiting for transfers between devices: 1270 us -> 0.16 us
  Pallas kernels: 0 us -> 294 us
  blocking collectives: 180 us -> 17.7 us
  local copies, waits for them, and re-layouts: 107 us -> 156 us
  matrix products: 233 us -> 280 us
    reduce_scatter x7 -> x0, waiting for transfers between devices: 802 us -> none  [the longest x1 168 us: local(): lax.psum_scatter(conv_grad, ('dp', 'seq'), scatter_dimension=0, tiled=True)]
    pallas_call x0 -> x2, Pallas kernels: none -> 294 us  [the longest x1 169 us: scatter_all(): pl.pallas_call(functools.partial(scatter_kernel, dp_size, count), out_sha...]
    unnamed x23 -> x4, waiting for transfers between devices: 239 us -> 0.15 us
    all_gather x8 -> x0, waiting for transfers between devices: 228 us -> none  [the longest x1 63 us: local(): lax.all_gather(conv_weight, ('dp', 'seq'), axis=0, tiled=True)]
    all_gather x3 -> x0, blocking collectives: 120 us -> none  [the longest x1 45.4 us: local(): lax.all_gather(char_table, ('dp', 'seq'), axis=0, tiled=True)]
    unnamed x1 -> x0, blocking collectives: 42.1 us -> none
    dot_general x16, matrix products: 12 us -> 35.5 us  [back_step(): jnp.einsum('dtg,dhg->dth', recur_low, recur_back, preferred_element_type=...]
    unnamed x200 -> x265, local copies, waits for them, and re-layouts: 40.6 us -> 49.7 us
  transfers between devices with their start and end apart: 23 -> 6, of which waited for: 15 -> 1; matrix products, arithmetic and copies ran while one was open for 20% -> 8% of each run, Pallas kernels for 0% -> 0%
where the time goes in v1:
time: 881 us; the launch traced here: 869 us
  Pallas kernels  294 us (33%)
  matrix products  280 us (32%)
  local copies, waits for them, and re-layouts  156 us (18%)
  other arithmetic  91.7 us (10%)
  blocking collectives  17.7 us (2%)
  between operations  17.5 us (2%)
  starting transfers between devices  9.97 us (1%)
    pallas_call x1, Pallas kernels, scatter_all(): pl.pallas_call(functools.partial(scatter_kernel, dp_size, count), out_sha...  169 us
    pallas_call x1, Pallas kernels, gather_all(): pl.pallas_call(functools.partial(gather_kernel, dp_size, count), out_shap...  125 us
    dot_general x16, matrix products, back_step(): jnp.einsum('dth,dtg->dhg', state_low, recur_low, preferred_element_type=j...  75.2 us
    unnamed x265, local copies, waits for them, and re-layouts  49.7 us
    squeeze x32, local copies, waits for them, and re-layouts, local(): lax.scan(gru_step, start_state, (gates_in, steps_live))  43.3 us
    dot_general x16, matrix products, back_step(): jnp.einsum('dtg,dhg->dth', recur_low, recur_back, preferred_element_type=...  35.5 us
    dot_general x16, matrix products, back_step(): jnp.einsum('dth,dhg->dtg', state_low, recur_back, preferred_element_type=...  34 us
    dot_general x16, matrix products, gru_step(): jnp.einsum('dth,dhg->dtg', carry_state.astype(jnp.bfloat16), recurrent, p...  31.7 us
  transfers between devices with their start and end apart: 6, of which 1 were waited for; matrix products, arithmetic and copies ran while one was open for 8% of the time, Pallas kernels for 0%

profile of v1, /device:TPU:0, one launch (start us, length us, event | category | flops | bytes accessed | tf_op | source)
XLA Modules:
  0.0 868.6 jit_solution(7104965090884605921)
XLA Ops:
  11.2 125.1 %shard_map.255 = (bf16[32,32,256]{2,1,0:T(8,128)(2,1)}, bf16[32,16,1152]{2,1,0:T(8,128)(2,1)}, bf16[32,24,1152]{2,1,0:T(8,128)(2,1)}, bf16[32,8,128]{2,1,0:T(8,1...) custom-call(bf16[32,256]{1,0:T(8,128)(2,1)} %refs_0_.1, ...), custom_call_target="tpu_custom_call" | custom-call | tf_op jit(solution)/shard_map/pallas_call | solution.py:181
  139.5 8.8 %all-gather.1 = bf16[512,768]{0,1:T(8,128)(2,1)S(1)} all-gather(bf16[128,768]{0,1:T(8,128)(2,1)S(1)} %get-tuple-element.394), channel_id=3, replica_groups=mesh['dp'=8,'seq'=4] {'seq'}, dimensions={0}, use_global_device_ids=true | all-gather | bytes 983040 | tf_op jit(solution)/shard_map/all_gather | solution.py:480
  150.5 8.9 %all-gather = bf16[512,768]{0,1:T(8,128)(2,1)S(1)} all-gather(bf16[128,768]{0,1:T(8,128)(2,1)S(1)} %get-tuple-element.396), channel_id=2, replica_groups=mesh['dp'=8,'seq'=4] {'seq'}, dimensions={0}, use_global_device_ids=true | all-gather | bytes 983040 | tf_op jit(solution)/shard_map/all_gather | solution.py:481
  169.8 8.1 multiply_convert_fusion.2
  200.3 8.1 convolution_bitcast_fusion
  208.4 18.7 %copy.75 = f32[16,2,128,1152]{3,2,1,0:T(8,128)} copy(f32[16,2,128,1152]{2,3,0,1:T(8,128)} %convolution_bitcast_fusion) | data formatting | bytes 37748736
  229.7 81.9 %while.32 = (s32[]{:T(128)}, f32[2,128,384]{2,1,0:T(8,128)S(1)}, f32[16,2,128,384]{3,2,1,0:T(8,128)}, pred[16,2,128,1]{2,1,3,0:T(4,128)(4,1)}, f32[16,2,128,1152...) while((s32[]{:T(128)}, f32[2,128,384]{2,1,0:T(8,128)S(1)}, ...), condition=%wide.region_7.8_spmd.clone, body=%wide.region_6.7_spmd.clone.sunk | while | flops 228261888 | bytes 9635177 | solution.py:530
  357.0 4.3 add_convert_fusion
  365.5 4.4 multiply_reduce_fusion
  371.8 4.9 broadcast_in_dim.138.clone
  376.6 229.9 %while.33 = (s32[]{:T(128)}, f32[2,128,384]{2,1,0:T(8,128)S(1)}, f32[2,384,1152]{2,1,0:T(8,128)}, bf16[16,2,128,1152]{3,2,0,1:T(8,128)(2,1)}, pred[16,2,128,1]{2...) while((s32[]{:T(128)}, f32[2,128,384]{2,1,0:T(8,128)S(1)}, ...), condition=%wide.region_20.21_spmd.clone, body=%wide.region_19.20_spmd.clone.sunk | while | flops 688324608 | bytes 29689268 | solution.py:668
  397.3 4.8 convolution_add_fusion.11
  411.8 4.8 convolution_add_fusion.11
  426.2 4.8 convolution_add_fusion.11
  440.7 4.8 convolution_add_fusion.11
  455.1 4.8 convolution_add_fusion.11
  469.5 4.8 convolution_add_fusion.11
  484.0 4.8 convolution_add_fusion.11
  498.4 4.8 convolution_add_fusion.11
  512.8 4.8 convolution_add_fusion.11
  527.3 4.8 convolution_add_fusion.11
  541.7 4.8 convolution_add_fusion.11
  556.2 4.8 convolution_add_fusion.11
  570.6 4.8 convolution_add_fusion.11
  585.1 4.8 convolution_add_fusion.11
  599.5 4.8 convolution_add_fusion.11
  606.5 6.0 convolution_bitcast_fusion.2
  618.9 3.7 copy.96
  630.6 3.9 copy.98
  659.8 3.7 convolution_convert_fusion.1
  663.5 7.9 fusion.44
  680.0 169.2 %shard_map.256 = (f32[48,768]{1,0:T(8,128)}, f32[144,768]{1,0:T(8,128)}, f32[96,768]{1,0:T(8,128)}, f32[24,3072]{1,0:T(8,128)}, f32[24,768]{1,0:T(8,128)}, /*ind...) custom-call(bf16[32,48,768]{2,1,0:T(8,128)(2,1)} %bitcast.299, ...), custom_call_target="tpu_custom_call" | custom-call | tf_op jit(solution)/shard_map/pallas_call | solution.py:367
  (620 shorter events, 392.8 us)
Async XLA Ops:
  7.2 664.3 %reduce-scatter.7.cloned.1.call-start = ((), (), s32[]{:S(2)}) async-start(), calls=%async_computation.2 | async-start | bytes 983040
  139.4 10.1 %copy-start.47 = (bf16[128,768]{0,1:T(8,128)(2,1)}, bf16[128,768]{0,1:T(8,128)(2,1)S(1)}, u32[]{:S(2)}) copy-start(bf16[128,768]{0,1:T(8,128)(2,1)S(1)} %get-tuple-element.395) | copy-start | bytes 589828
  148.9 10.6 %copy-start.106 = (pred[512]{0:T(512)(128)(4,1)}, pred[512]{0:T(512)(128)(4,1)S(1)}, u32[]{:S(2)}) copy-start(pred[512]{0:T(512)(128)(4,1)S(1)} %iota_compare_fusion.7) | copy-start | bytes 1540
  149.6 220.3 %copy-start.1 = (f32[12,128,512]{2,1,0:T(8,128)}, f32[12,128,512]{2,1,0:T(8,128)S(1)}, u32[]{:S(2)}) copy-start(f32[12,128,512]{2,1,0:T(8,128)S(1)} %get-tuple-element.415) | copy-start | bytes 9437188
  150.5 9.9 %copy-start.68 = (f32[12,128]{1,0:T(8,128)}, f32[12,128]{1,0:T(8,128)S(1)}, u32[]{:S(2)}) copy-start(f32[12,128]{1,0:T(8,128)S(1)} %log_add_fusion) | copy-start | bytes 18436
  169.8 8.2 copy-start.5
  169.8 8.2 copy-start.85
  169.8 8.2 copy-start.98
  187.4 139.9 %copy-start.79 = (f32[768]{0:T(1024)}, f32[768]{0:T(1024)S(1)}, u32[]{:S(2)}) copy-start(f32[768]{0:T(1024)S(1)} %add.248) | copy-start | bytes 9220
  313.5 9.0 %copy-start.23 = (bf16[128,768]{1,0:T(8,128)(2,1)}, bf16[128,768]{1,0:T(8,128)(2,1)S(1)}, u32[]{:S(2)}) copy-start(bf16[128,768]{1,0:T(8,128)(2,1)S(1)} %convolution_convert_fusion.12) | copy-start | bytes 589828
  313.9 8.6 copy-start.25
  314.6 10.2 %collective-permute-start.1 = (bf16[1,1,1536]{2,1,0:T(2,128)(2,1)}, bf16[1,1,1536]{2,1,0:T(2,128)(2,1)}, u32[]{:S(2)}, u32[]{:S(2)}) collective-permute-start(bf16[1,1,1536]{2,1,0:T(2,128)(2,1)} %get-tuple-element.401), channel_id=1, source_target_pairs={{1,0},{2,1},{3,2},{5,4},{6,5},{7,6},{9,8},{10,9},{11,10},{13,12},{... | collective-permute-start | bytes 9224 | tf_op jit(solution)/shard_map/ppermute | solution.py:385
  315.9 11.4 %collective-permute-start = (bf16[1,1,1536]{2,1,0:T(2,128)(2,1)}, bf16[1,1,1536]{2,1,0:T(2,128)(2,1)}, u32[]{:S(2)}, u32[]{:S(2)}) collective-permute-start(bf16[1,1,1536]{2,1,0:T(2,128)(2,1)} %get-tuple-element.400), channel_id=1, source_target_pairs={{0,1},{1,2},{2,3},{4,5},{5,6},{6,7},{8,9},{9,10},{10,11},{12,13},{... | collective-permute-start | bytes 9224 | tf_op jit(solution)/shard_map/ppermute | solution.py:384
  331.9 16.3 %collective-permute-start.3 = (bf16[1,1,768]{2,1,0:T(2,128)(2,1)}, bf16[1,1,768]{2,1,0:T(2,128)(2,1)}, u32[]{:S(2)}, u32[]{:S(2)}) collective-permute-start(bf16[1,1,768]{2,1,0:T(2,128)(2,1)} %get-tuple-element.403), channel_id=1, source_target_pairs={{0,1},{1,2},{2,3},{4,5},{5,6},{6,7},{8,9},{9,10},{10,11},{12,13},{... | collective-permute-start | bytes 4616 | tf_op jit(solution)/shard_map/ppermute | solution.py:384
  346.1 5.0 collective-permute-start.2
  355.3 6.0 slice-start
  397.3 4.8 copy-start.3
  411.8 4.8 copy-start.3
  455.1 4.8 copy-start.3
  469.5 4.8 copy-start.3
  484.0 4.8 copy-start.3
  512.8 4.8 copy-start.3
  541.7 4.8 copy-start.3
  556.2 4.8 copy-start.3
  606.5 9.1 %copy-start.12 = (f32[12,128,512]{2,1,0:T(8,128)S(1)}, f32[12,128,512]{2,1,0:T(8,128)}, u32[]{:S(2)}) copy-start(f32[12,128,512]{2,1,0:T(8,128)} %get-tuple-element.426) | copy-start | bytes 9437188
  623.8 49.4 %reduce-scatter.9.cloned.1.call-start = ((), (), s32[]{:S(2)}) async-start(), calls=%async_computation.3 | async-start | bytes 983040
  647.5 9.3 %copy-start = (f32[2,384,1152]{2,1,0:T(8,128)S(1)}, f32[2,384,1152]{2,1,0:T(8,128)}, u32[]{:S(2)}) copy-start(f32[2,384,1152]{2,1,0:T(8,128)} %get-tuple-element.239) | copy-start | bytes 10616836
  849.2 8.8 %copy-start.82 = (f32[32,256]{1,0:T(8,128)S(1)}, f32[32,256]{1,0:T(8,128)}, u32[]{:S(2)}) copy-start(f32[32,256]{1,0:T(8,128)} %get-tuple-element.604) | copy-start | bytes 98308
  849.2 9.4 %copy-start.67 = (f32[16,1152]{1,0:T(8,128)S(1)}, f32[16,1152]{1,0:T(8,128)}, u32[]{:S(2)}) copy-start(f32[16,1152]{1,0:T(8,128)} %get-tuple-element.605) | copy-start | bytes 221188
  849.2 10.0 %copy-start.65 = (f32[24,1152]{1,0:T(8,128)S(1)}, f32[24,1152]{1,0:T(8,128)}, u32[]{:S(2)}) copy-start(f32[24,1152]{1,0:T(8,128)} %get-tuple-element.606) | copy-start | bytes 331780
  849.2 10.6 %copy-start.64 = (f32[48,768]{1,0:T(8,128)S(1)}, f32[48,768]{1,0:T(8,128)}, u32[]{:S(2)}) copy-start(f32[48,768]{1,0:T(8,128)} %get-tuple-element.607) | copy-start | bytes 442372
  849.2 11.3 %copy-start.63 = (f32[144,768]{1,0:T(8,128)S(1)}, f32[144,768]{1,0:T(8,128)}, u32[]{:S(2)}) copy-start(f32[144,768]{1,0:T(8,128)} %get-tuple-element.608) | copy-start | bytes 1327108
  (113 other events, 306.4 us)
Sparse Core Ops, SparseCore 0:
  623.8 23.4 reduce-scatter.6
  649.9 23.2 reduce-scatter.8

commit v2 on v1

--- a/solution.py
+++ b/solution.py
@@ -393,15 +393,6 @@
     return centered * lax.rsqrt(spread + eps) * row_gain + row_bias
 
 
-def cell(gate_input, gate_recur, carry_state, is_live):
-    units = carry_state.shape[-1]
-    reset = jax.nn.sigmoid(gate_input[..., :units] + gate_recur[..., :units])
-    update = jax.nn.sigmoid(gate_input[..., units : 2 * units] + gate_recur[..., units : 2 * units])
-    candidate = jnp.tanh(gate_input[..., 2 * units :] + reset * gate_recur[..., 2 * units :])
-    fresh = (1.0 - update) * candidate + update * carry_state
-    return jnp.where(is_live, fresh, carry_state)
-
-
 def gelu_exact(pre_act):
     return jax.nn.gelu(pre_act, approximate=False)
 
@@ -420,6 +411,187 @@
     return lax.dot_general(
         left, right, (((1,), (1,)), ((), ())), preferred_element_type=jnp.float32
     )
+
+
+def squash(x):
+    return 0.5 * jnp.tanh(0.5 * x) + 0.5
+
+
+def slot_onehot(ids, slots, subset):
+    cols = lax.broadcasted_iota(jnp.int32, (ids.shape[0], subset), 1)
+    hots = [(ids[:, s : s + 1] == cols).astype(jnp.bfloat16) for s in slots]
+    return jnp.concatenate(hots, 0)
+
+
+def gru_embed(ids_ref, table, w_in, emb_ref, gates, chunk=4):
+    rows, nchar = ids_ref.shape
+    ids = ids_ref[...]
+    for k in range(0, nchar, chunk):
+        hot = slot_onehot(ids, range(k, k + chunk), table.shape[0])
+        emb = plain_dot(hot, table[...]).astype(jnp.bfloat16)
+        emb_ref[k : k + chunk] = emb.reshape(chunk, rows, -1)
+        for d in range(2):
+            gates[d, k : k + chunk] = plain_dot(emb, w_in[d]).reshape(chunk, rows, -1)
+
+
+def gru_step(d, slot, count, gates, w_rec, state, factor, keep, prior):
+    units = state.shape[2]
+    old = state[d]
+    low = old.astype(jnp.bfloat16)
+    rec = plain_dot(low, w_rec[d])
+    gi = gates[d, slot]
+    reset = squash(gi[:, :units] + rec[:, :units])
+    update = squash(gi[:, units : 2 * units] + rec[:, units : 2 * units])
+    rec_n = rec[:, 2 * units :]
+    cand = jnp.tanh(gi[:, 2 * units :] + reset * rec_n)
+    live = slot < count
+    state[d] = jnp.where(live, (1.0 - update) * cand + update * old, old)
+    by_cand = jnp.where(live, (1.0 - update) * (1.0 - cand * cand), 0.0)
+    by_update = jnp.where(live, (old - cand) * update * (1.0 - update), 0.0)
+    by_reset = by_cand * rec_n * reset * (1.0 - reset)
+    prior[...] = low
+    keep[...] = jnp.where(live, update, 1.0)
+    for k, x in enumerate((by_reset, by_update, by_cand, reset)):
+        factor[:, k * units : (k + 1) * units] = x.astype(factor.dtype)
+
+
+def gru_forward_kernel(ids_ref, table, w_in, w_rec, vec, emb, f0, f1, z0, z1, h0, h1, gates, state):
+    i = pl.program_id(0)
+    nchar = pl.num_programs(0)
+
+    @pl.when(i == 0)
+    def _():
+        gru_embed(ids_ref, table, w_in, emb, gates)
+        state[...] = jnp.zeros_like(state)
+
+    count = jnp.sum((ids_ref[...] > 0).astype(jnp.int32), axis=1, keepdims=True)
+    gru_step(0, i, count, gates, w_rec, state, f0.at[0], z0.at[0], h0.at[0])
+    gru_step(1, nchar - 1 - i, count, gates, w_rec, state, f1.at[0], z1.at[0], h1.at[0])
+
+    @pl.when(i == nchar - 1)
+    def _():
+        units = state.shape[2]
+        vec[:, :units] = state[0].astype(vec.dtype)
+        vec[:, units:] = state[1].astype(vec.dtype)
+
+
+def slot_specs(nchar, rows, cols, backward):
+    up = pl.BlockSpec((1, rows, cols), lambda i: (i, 0, 0))
+    down = pl.BlockSpec((1, rows, cols), lambda i: (nchar - 1 - i, 0, 0))
+    return [down, up] if backward else [up, down]
+
+
+def gru_forward(ids, table, w_in, w_rec):
+    rows, nchar = ids.shape
+    width, units = table.shape[1], w_rec.shape[1]
+    whole = lambda shape: pl.BlockSpec(shape, lambda i: (0,) * len(shape))
+    slots = functools.partial(slot_specs, nchar, rows, backward=False)
+    shape = jax.ShapeDtypeStruct
+    factor = shape((nchar, rows, 4 * units), jnp.bfloat16)
+    keep = shape((nchar, rows, units), jnp.float32)
+    prior = shape((nchar, rows, units), jnp.bfloat16)
+    return pl.pallas_call(
+        gru_forward_kernel,
+        grid=(nchar,),
+        out_shape=[
+            shape((rows, 2 * units), jnp.bfloat16),
+            shape((nchar, rows, width), jnp.bfloat16),
+            factor, factor, keep, keep, prior, prior,
+        ],
+        in_specs=[whole(x.shape) for x in (ids, table, w_in, w_rec)],
+        out_specs=[whole((rows, 2 * units)), whole((nchar, rows, width))]
+        + slots(4 * units) + slots(units) + slots(units),
+        scratch_shapes=[
+            pltpu.VMEM((2, nchar, rows, 3 * units), jnp.float32),
+            pltpu.VMEM((2, rows, units), jnp.float32),
+        ],
+        compiler_params=pltpu.CompilerParams(vmem_limit_bytes=60000000),
+    )(ids, table, w_in, w_rec)
+
+
+def gru_back_step(d, slot, factor, keep, w_rec, grad, seeds):
+    units = grad.shape[2]
+    g = grad[d]
+    part = lambda k: factor[:, k * units : (k + 1) * units].astype(jnp.float32)
+    by_cand = g * part(2)
+    seeds[d, slot, :, :units] = (g * part(0)).astype(seeds.dtype)
+    seeds[d, slot, :, units : 2 * units] = (g * part(1)).astype(seeds.dtype)
+    seeds[d, slot, :, 2 * units : 3 * units] = (by_cand * part(3)).astype(seeds.dtype)
+    seeds[d, slot, :, 3 * units :] = by_cand.astype(seeds.dtype)
+    grad[d] = g * keep[...] + back_dot(seeds[d, slot, :, : 3 * units], w_rec[d])
+
+
+def gru_weight_grads(d, seeds, emb, prior, d_in, d_rec):
+    _, nchar, rows, wide = seeds.shape
+    units = wide // 4
+    states = prior[...].reshape(nchar * rows, units)
+    chars = emb[...].reshape(nchar * rows, -1)
+    col = lambda k: seeds[d, :, :, k * units : (k + 1) * units].reshape(nchar * rows, units)
+    for k in range(3):
+        d_rec[d, :, k * units : (k + 1) * units] = grad_dot(states, col(k)).astype(d_rec.dtype)
+        own = col(3 if k == 2 else k)
+        d_in[d, :, k * units : (k + 1) * units] = grad_dot(chars, own).astype(d_in.dtype)
+
+
+def gru_char_grads(ids_ref, seeds, w_in, d_table, chunk=4):
+    _, nchar, rows, wide = seeds.shape
+    units = wide // 4
+    ids = ids_ref[...]
+    total = jnp.zeros(d_table.shape, jnp.float32)
+    for k in range(0, nchar, chunk):
+        grad = None
+        for d in range(2):
+            both = seeds[d, k : k + chunk].reshape(chunk * rows, wide)
+            part = back_dot(both[:, : 2 * units], w_in[d][:, : 2 * units])
+            part = part + back_dot(both[:, 3 * units :], w_in[d][:, 2 * units :])
+            grad = part if grad is None else grad + part
+        hot = slot_onehot(ids, range(k, k + chunk), d_table.shape[0])
+        total = total + grad_dot(hot, grad.astype(jnp.bfloat16))
+    d_table[...] = total
+
+
+def gru_backward_kernel(ids_ref, seed, w_in, w_rec, emb, h0, h1, f0, f1, z0, z1, d_in, d_rec, d_table, grad, seeds):
+    i = pl.program_id(0)
+    nchar = pl.num_programs(0)
+
+    @pl.when(i == 0)
+    def _():
+        units = grad.shape[2]
+        grad[0] = seed[:, :units]
+        grad[1] = seed[:, units:]
+
+    gru_back_step(0, nchar - 1 - i, f0.at[0], z0.at[0], w_rec, grad, seeds)
+    gru_back_step(1, i, f1.at[0], z1.at[0], w_rec, grad, seeds)
+
+    @pl.when(i == nchar - 1)
+    def _():
+        gru_weight_grads(0, seeds, emb, h0, d_in, d_rec)
+        gru_weight_grads(1, seeds, emb, h1, d_in, d_rec)
+        gru_char_grads(ids_ref, seeds, w_in, d_table)
+
+
+def gru_backward(ids, seed, w_in, w_rec, emb, h0, h1, f0, f1, z0, z1, subset):
+    nchar, rows, width = emb.shape
+    units = w_rec.shape[1]
+    whole = lambda shape: pl.BlockSpec(shape, lambda i: (0,) * len(shape))
+    slots = functools.partial(slot_specs, nchar, rows, backward=True)
+    shape = jax.ShapeDtypeStruct
+    return pl.pallas_call(
+        gru_backward_kernel,
+        grid=(nchar,),
+        out_shape=[
+            shape(w_in.shape, jnp.bfloat16),
+            shape(w_rec.shape, jnp.bfloat16),
+            shape((subset, width), jnp.float32),
+        ],
+        in_specs=[whole(x.shape) for x in (ids, seed, w_in, w_rec, emb, h0, h1)] + slots(4 * units) + slots(units),
+        out_specs=[whole(w_in.shape), whole(w_rec.shape), whole((subset, width))],
+        scratch_shapes=[
+            pltpu.VMEM((2, rows, units), jnp.float32),
+            pltpu.VMEM((2, nchar, rows, 4 * units), jnp.bfloat16),
+        ],
+        compiler_params=pltpu.CompilerParams(vmem_limit_bytes=60000000),
+    )(ids, seed, w_in, w_rec, emb, h0, h1, f0, f1, z0, z1)
 
 
 def pack_norms(gain, bias, devices=1):
@@ -504,31 +676,14 @@
     active = gelu_exact(up_proj).astype(jnp.bfloat16)
     resid_two = norm_one.astype(jnp.float32) + plain_dot(active, full_down)
     norm_two = norm_rows(resid_two, gains[1], biases[1]).astype(jnp.bfloat16)
-    vocab_rows = full_table.shape[0]
-    char_rows = (groups[:, None, None] * SUBV + char_ids).reshape(tokens * nchar)
-    onehot = (char_rows[:, None] == jnp.arange(vocab_rows)[None, :]).astype(jnp.bfloat16)
-    char_emb = plain_dot(onehot, full_table).astype(jnp.bfloat16).reshape(tokens, nchar, -1)
-    char_live = (char_ids > 0).reshape(tokens, nchar)
-    steps_in = jnp.stack([char_emb, char_emb[:, ::-1]], 0).transpose(2, 0, 1, 3)
-    steps_live = jnp.stack([char_live, char_live[:, ::-1]], 0).transpose(2, 0, 1)[..., None]
+    assert seq_count == 1
+    flat_ids = char_ids.reshape(tokens, nchar)
+    table_start = groups[0] * SUBV
+    own_table = lax.dynamic_slice_in_dim(full_table, table_start, SUBV, 0)
     inward = full_input.reshape(2, -1, full_input.shape[1])
     recurrent = full_recur.reshape(2, -1, full_recur.shape[1])
-    hidden_units = recurrent.shape[1]
-    gates_in = jnp.einsum("cdtz,dzg->cdtg", steps_in, inward, preferred_element_type=jnp.float32)
-
-    def gru_step(carry_state, step_input):
-        gate_input, is_live = step_input
-        gate_recur = jnp.einsum(
-            "dth,dhg->dtg",
-            carry_state.astype(jnp.bfloat16),
-            recurrent,
-            preferred_element_type=jnp.float32,
-        )
-        return (cell(gate_input, gate_recur, carry_state, is_live), carry_state)
-
-    start_state = jnp.zeros((2, tokens, hidden_units), jnp.float32)
-    last_state, prior_states = lax.scan(gru_step, start_state, (gates_in, steps_live))
-    char_vec = jnp.concatenate([last_state[0], last_state[1]], -1).astype(jnp.bfloat16)
+    char_vec, char_emb, *kept = gru_forward(flat_ids, own_table, inward, recurrent)
+    factors, keeps, priors = kept[:2], kept[2:4], kept[4:]
     merge_mats = full_merge.reshape(2, features, features)
     merged_rows = jnp.concatenate(
         [plain_dot(norm_two, merge_mats[0]), plain_dot(char_vec, merge_mats[1])], -1
@@ -547,11 +702,9 @@
     result_rows, pull_three = jax.vjp(norm_rows, resid_three, gains[2], biases[2])
     result = result_rows.astype(jnp.bfloat16).reshape(seq_count, local_len, features)
     back_qkv, back_out, back_up, back_down = full_qkv, full_out, full_up, full_down
-    back_input, back_recur, back_merge, back_conv = full_input, full_recur, full_merge, full_conv
+    back_merge, back_conv = full_merge, full_conv
     merge_back = back_merge.reshape(2, features, features)
     kernel_back = back_conv.reshape(3, 2 * features, features)
-    inward_back = back_input.reshape(2, -1, back_input.shape[1])
-    recur_back = back_recur.reshape(2, -1, back_recur.shape[1])
     seed_rows = cotangent.reshape(tokens, features).astype(jnp.float32)
     grad_three, gain_three, bias_three = pull_three(seed_rows)
     conv_seed = grad_three.astype(jnp.bfloat16)
@@ -640,43 +793,11 @@
         .astype(jnp.bfloat16)
         .reshape(seq_count, local_len, features)
     )
-    state_seed = jnp.stack([charvec_grad[:, :hidden_units], charvec_grad[:, hidden_units:]], 0)
-
-    def back_step(carry_in, step_input):
-        state_grad, recur_total = carry_in
-        gate_input, is_live, carry_state = step_input
-        state_low = carry_state.astype(jnp.bfloat16)
-        gate_recur = jnp.einsum(
-            "dth,dhg->dtg", state_low, recur_back, preferred_element_type=jnp.float32
-        )
-
-        def cell_local(given, recurred, previous):
-            return cell(given, recurred, previous, is_live)
-
-        _, pull_cell = jax.vjp(cell_local, gate_input, gate_recur, carry_state)
-        input_part, recur_part, prior_part = pull_cell(state_grad)
-        recur_low = recur_part.astype(jnp.bfloat16)
-        prior_part = prior_part + jnp.einsum(
-            "dtg,dhg->dth", recur_low, recur_back, preferred_element_type=jnp.float32
-        )
-        recur_total = recur_total + jnp.einsum(
-            "dth,dtg->dhg", state_low, recur_low, preferred_element_type=jnp.float32
-        )
-        return ((prior_part, recur_total), input_part.astype(jnp.bfloat16))
-
-    recur_zero = jnp.zeros((2, hidden_units, recur_back.shape[2]), jnp.float32)
-    (_, recur_sum), input_seeds = lax.scan(
-        back_step, (state_seed, recur_zero), (gates_in, steps_live, prior_states), reverse=True
-    )
-    input_mats = jnp.einsum(
-        "cdtz,cdtg->dzg", steps_in, input_seeds, preferred_element_type=jnp.float32
-    )
-    step_chars = jnp.einsum(
-        "cdtg,dzg->cdtz", input_seeds, inward_back, preferred_element_type=jnp.float32
-    )
-    char_grad = step_chars[:, 0].transpose(1, 0, 2) + step_chars[::-1, 1].transpose(1, 0, 2)
-    char_grad = char_grad.astype(jnp.bfloat16).reshape(tokens * nchar, -1)
-    table_grad = grad_dot(onehot, char_grad)
+    input_mats, recur_sum, own_grad = gru_backward(
+        flat_ids, charvec_grad, inward, recurrent, char_emb, *priors, *factors, *keeps, SUBV
+    )
+    table_grad = jnp.zeros(full_table.shape, jnp.bfloat16)
+    table_grad = lax.dynamic_update_slice_in_dim(table_grad, own_grad.astype(jnp.bfloat16), table_start, 0)
     gain_grad = jnp.stack([gain_one, gain_two, gain_three], 0)
     bias_grad = jnp.stack([bias_one, bias_two, bias_three], 0)
     input_flat = input_mats.reshape(-1, input_mats.shape[2])

time: 881 us -> 558 us (0.63)
  matrix products: 280 us -> 75.6 us
  local copies, waits for them, and re-layouts: 156 us -> 63.7 us
  other arithmetic: 91.7 us -> 15.8 us
  Pallas kernels: 294 us -> 349 us
    dot_general x67 -> x0, matrix products: 198 us -> none  [the longest x16 75.2 us: back_step(): jnp.einsum('dth,dtg->dhg', state_low, recur_low, preferred_element_type=j...]
    pallas_call x0 -> x2, Pallas kernels: none -> 54.8 us  [the longest x1 33.5 us: gru_backward(): pl.pallas_call(gru_backward_kernel, grid=(nchar,), out_shape=[shape(w_in....]
    squeeze x33 -> x0, local copies, waits for them, and re-layouts: 43.4 us -> none  [the longest x32 43.3 us: local(): lax.scan(gru_step, start_state, (gates_in, steps_live))]
    mul x32 -> x0, other arithmetic: 37.8 us -> none  [the longest x16 20.6 us: cell(): jax.nn.sigmoid(gate_input[..., units:2 * units] + gate_recur[..., units:2...]
    dynamic_update_slice x32 -> x1, other arithmetic: 27.1 us -> 1.53 us  [local(): lax.dynamic_update_slice_in_dim(table_grad, own_grad.astype(jnp.bfloat16)...]
    broadcast_in_dim x33 -> x1, local copies, waits for them, and re-layouts: 26.1 us -> 0.85 us  [local(): table_grad = jnp.zeros(full_table.shape, jnp.bfloat16)]
    unnamed x265 -> x214, local copies, waits for them, and re-layouts: 49.7 us -> 30.8 us
    dot_general x10 -> x9, matrix products: 28.2 us -> 22.8 us  [plain_dot(): return jnp.dot(left, right, preferred_element_type=jnp.float32)]
  transfers between devices with their start and end apart: 6 -> 6, of which waited for: 1 -> 0; matrix products, arithmetic and copies ran while one was open for 8% -> 11% of each run, Pallas kernels for 0% -> 6%
where the time goes in v2:
time: 558 us; the launch traced here: 550 us
  Pallas kernels  349 us (63%)
  matrix products  75.6 us (14%)
  local copies, waits for them, and re-layouts  63.7 us (11%)
  blocking collectives  18.4 us (3%)
  between operations  16.9 us (3%)
  other arithmetic  15.8 us (3%)
  starting transfers between devices  10.3 us (2%)
    pallas_call x1, Pallas kernels, scatter_all(): pl.pallas_call(functools.partial(scatter_kernel, dp_size, count), out_sha...  169 us
    pallas_call x1, Pallas kernels, gather_all(): pl.pallas_call(functools.partial(gather_kernel, dp_size, count), out_shap...  125 us
    pallas_call x1, Pallas kernels, gru_backward(): pl.pallas_call(gru_backward_kernel, grid=(nchar,), out_shape=[shape(w_in....  33.5 us
    unnamed x214, local copies, waits for them, and re-layouts  30.8 us
    dot_general x9, matrix products, back_dot(): lax.dot_general(left, right, (((1,), (1,)), ((), ())), preferred_element_...  23.3 us
    dot_general x9, matrix products, plain_dot(): return jnp.dot(left, right, preferred_element_type=jnp.float32)  22.8 us
    pallas_call x1, Pallas kernels, gru_forward(): pl.pallas_call(gru_forward_kernel, grid=(nchar,), out_shape=[shape((rows,...  21.3 us
    dot_general x9, matrix products, grad_dot(): lax.dot_general(left, right, (((0,), (0,)), ((), ())), preferred_element_...  19.5 us
  transfers between devices with their start and end apart: 6, of which 0 were waited for; matrix products, arithmetic and copies ran while one was open for 11% of the time, Pallas kernels for 6%

profile of v2, /device:TPU:0, one launch (start us, length us, event | category | flops | bytes accessed | tf_op | source)
XLA Modules:
  0.0 550.2 jit_solution(7167630429964079387)
XLA Ops:
  10.7 125.2 %shard_map.255 = (bf16[32,32,256]{2,1,0:T(8,128)(2,1)}, bf16[32,16,1152]{2,1,0:T(8,128)(2,1)}, bf16[32,24,1152]{2,1,0:T(8,128)(2,1)}, bf16[32,8,128]{2,1,0:T(8,1...) custom-call(bf16[32,256]{1,0:T(8,128)(2,1)} %refs_0_.1, ...), custom_call_target="tpu_custom_call" | custom-call | tf_op jit(solution)/shard_map/pallas_call | solution.py:181
  135.9 3.3 fusion.72
  140.5 9.2 %all-gather = bf16[512,768]{0,1:T(8,128)(2,1)} all-gather(bf16[128,768]{0,1:T(8,128)(2,1)S(1)} %get-tuple-element.97), channel_id=2, replica_groups=mesh['dp'=8,'seq'=4] {'seq'}, dimensions={0}, use_global_device_ids=true | all-gather | bytes 983040 | tf_op jit(solution)/shard_map/all_gather | solution.py:653
  150.3 9.2 %all-gather.1 = bf16[512,768]{0,1:T(8,128)(2,1)S(1)} all-gather(bf16[128,768]{0,1:T(8,128)(2,1)S(1)} %get-tuple-element.95), channel_id=3, replica_groups=mesh['dp'=8,'seq'=4] {'seq'}, dimensions={0}, use_global_device_ids=true | all-gather | bytes 983040 | tf_op jit(solution)/shard_map/all_gather | solution.py:652
  162.5 2.1 convolution_convert_fusion.14
  171.6 8.3 %multiply_convert_fusion.2 = (bf16[128,3072]{1,0:T(8,128)(2,1)S(1)}, f32[128,3072]{1,0:T(8,128)}, f32[128,3072]{1,0:T(8,128)}) fusion(bf16[768,3072]{1,0:T(8,128)(2,1)} %bitcast.224, f32[128,768]{1,0:T(8,128)S(1)} %get-tuple-element.114, f32[768]{0:T(1024)S(1)} %add.115, f32[768]{0:T(1024)S(1)} %mul.250, f32[128]{0:T(128)} %fusion.50, f32[128]{0:T(128)} %copy-done.63), kind=kOutput, calls=%fused_computation.32 | convolution fusion | flops 630030336 | bytes 9051136 | tf_op jit(solution)/shard_map/dot_general | solution.py:401
  179.9 3.5 fusion.78
  187.0 21.3 %shard_map.256 = (bf16[128,768]{1,0:T(8,128)(2,1)}, bf16[16,128,256]{2,1,0:T(8,128)(2,1)}, bf16[16,128,1536]{2,1,0:T(8,128)(2,1)}, bf16[16,128,1536]{2,1,0:T(8,1...) custom-call(s32[128,16]{1,0:T(8,128)} %bitcast.257, ...), custom_call_target="tpu_custom_call" | custom-call | tf_op jit(solution)/shard_map/pallas_call | solution.py:493
  211.9 3.8 collective-permute-start
  215.7 3.0 fusion.6
  226.3 2.5 fusion.8
  228.8 2.3 fusion.79
  233.9 3.5 collective-permute-start.3
  242.5 3.3 pad_maximum_fusion
  245.8 3.4 fusion.5
  250.6 2.7 fusion.7
  253.5 2.7 fusion.2
  257.9 4.3 add_convert_fusion
  262.3 2.4 multiply_reduce_fusion.2
  269.1 2.9 convolution_convert_fusion.10
  271.9 3.4 multiply_reduce_fusion
  275.3 4.9 copy.58
  280.2 2.4 copy.64
  283.1 2.4 multiply_convert_fusion
  295.3 2.5 convolution_convert_fusion.8
  302.4 33.5 %shard_map.257 = (bf16[2,256,1152]{2,1,0:T(8,128)(2,1)}, bf16[2,384,1152]{2,1,0:T(8,128)(2,1)}, f32[128,256]{1,0:T(8,128)}) custom-call(s32[128,16]{1,0:T(8,128)} %bitcast.258, f32[128,768]{1,0:T(8,128)} %fusion.39.seed, bf16[2,256,1152]{2,1,0:T(8,128)(2,1)} %bitcast.220, bf16[2,384,1152]{2,1,0:T(8,128)(2,1)} %bitcast.204, ...), custom_call_target="tpu_custom_call" | custom-call | tf_op jit(solution)/shard_map/pallas_call | solution.py:579
  339.2 1.9 copy.55.refs_9_
  344.4 3.6 convolution_convert_fusion.2
  348.0 3.6 convolution_convert_fusion.1
  354.8 4.0 fusion.21
  358.8 2.9 convolution_convert_fusion
  361.6 169.4 %shard_map.258 = (f32[48,768]{1,0:T(8,128)}, f32[144,768]{1,0:T(8,128)}, f32[96,768]{1,0:T(8,128)}, f32[24,3072]{1,0:T(8,128)}, f32[24,768]{1,0:T(8,128)}, /*ind...) custom-call(bf16[32,48,768]{2,1,0:T(8,128)(2,1)} %bitcast.200, ...), custom_call_target="tpu_custom_call" | custom-call | tf_op jit(solution)/shard_map/pallas_call | solution.py:367
  (305 shorter events, 80.0 us)
Async XLA Ops:
  7.2 344.4 %reduce-scatter.9.cloned.1.call-start = ((), (), s32[]{:S(2)}) async-start(), calls=%async_computation.3 | async-start | bytes 983040
  140.4 19.8 %copy-start.39 = (bf16[128,768]{0,1:T(8,128)(2,1)}, bf16[128,768]{0,1:T(8,128)(2,1)S(1)}, u32[]{:S(2)}) copy-start(bf16[128,768]{0,1:T(8,128)(2,1)S(1)} %get-tuple-element.96) | copy-start | bytes 589828
  150.3 12.2 %copy-start.80 = (pred[512]{0:T(512)(128)(4,1)}, pred[512]{0:T(512)(128)(4,1)S(1)}, u32[]{:S(2)}) copy-start(pred[512]{0:T(512)(128)(4,1)S(1)} %iota_compare_fusion) | copy-start | bytes 1540
  171.6 8.3 %copy-start.64 = (f32[128]{0:T(128)S(1)}, f32[128]{0:T(128)}, u32[]{:S(2)}) copy-start(f32[128]{0:T(128)} %copy-done.63) | copy-start | bytes 1540
  171.6 8.3 %copy-start.73 = (f32[128]{0:T(128)S(1)}, f32[128]{0:T(128)}, u32[]{:S(2)}) copy-start(f32[128]{0:T(128)} %fusion.50) | copy-start | bytes 1540
  186.9 21.3 %copy-start.7 = (bf16[16,48,768]{2,1,0:T(8,128)(2,1)S(1)}, bf16[16,48,768]{2,1,0:T(8,128)(2,1)}, u32[]{:S(2)}) copy-start(bf16[16,48,768]{2,1,0:T(8,128)(2,1)} %get-tuple-element.94) | copy-start | bytes 3538948
  186.9 22.6 %copy-start.3 = (f32[128,768]{1,0:T(8,128)S(1)}, f32[128,768]{1,0:T(8,128)}, u32[]{:S(2)}) copy-start(f32[128,768]{1,0:T(8,128)} %copy-done.2) | copy-start | bytes 1179652
  186.9 22.6 %copy-start.9 = (bf16[16,48,768]{2,1,0:T(8,128)(2,1)S(1)}, bf16[16,48,768]{2,1,0:T(8,128)(2,1)}, u32[]{:S(2)}) copy-start(bf16[16,48,768]{2,1,0:T(8,128)(2,1)} %get-tuple-element.93) | copy-start | bytes 3538948
  186.9 22.6 %copy-start.69 = (f32[128]{0:T(128)S(1)}, f32[128]{0:T(128)}, u32[]{:S(2)}) copy-start(f32[128]{0:T(128)} %copy-done.68) | copy-start | bytes 1540
  187.0 22.6 %copy-start.76 = (f32[128]{0:T(128)S(1)}, f32[128]{0:T(128)}, u32[]{:S(2)}) copy-start(f32[128]{0:T(128)} %fusion.51) | copy-start | bytes 1540
  209.5 9.2 %copy-start.18 = (bf16[128,768]{1,0:T(8,128)(2,1)}, bf16[128,768]{1,0:T(8,128)(2,1)S(1)}, u32[]{:S(2)}) copy-start(bf16[128,768]{1,0:T(8,128)(2,1)S(1)} %convolution_convert_fusion.12) | copy-start | bytes 589828
  209.9 8.7 %copy-start.20 = (bf16[128,768]{1,0:T(8,128)(2,1)}, bf16[128,768]{1,0:T(8,128)(2,1)S(1)}, u32[]{:S(2)}) copy-start(bf16[128,768]{1,0:T(8,128)(2,1)S(1)} %convolution_convert_fusion.13) | copy-start | bytes 589828
  210.6 15.6 %collective-permute-start.1 = (bf16[1,1,1536]{2,1,0:T(2,128)(2,1)}, bf16[1,1,1536]{2,1,0:T(2,128)(2,1)}, u32[]{:S(2)}, u32[]{:S(2)}) collective-permute-start(bf16[1,1,1536]{2,1,0:T(2,128)(2,1)} %get-tuple-element.100), channel_id=1, source_target_pairs={{1,0},{2,1},{3,2},{5,4},{6,5},{7,6},{9,8},{10,9},{11,10},{13,12},{... | collective-permute-start | bytes 9224 | tf_op jit(solution)/shard_map/ppermute | solution.py:385
  211.9 16.9 %collective-permute-start = (bf16[1,1,1536]{2,1,0:T(2,128)(2,1)}, bf16[1,1,1536]{2,1,0:T(2,128)(2,1)}, u32[]{:S(2)}, u32[]{:S(2)}) collective-permute-start(bf16[1,1,1536]{2,1,0:T(2,128)(2,1)} %get-tuple-element.99), channel_id=1, source_target_pairs={{0,1},{1,2},{2,3},{4,5},{5,6},{6,7},{8,9},{9,10},{10,11},{12,13},{... | collective-permute-start | bytes 9224 | tf_op jit(solution)/shard_map/ppermute | solution.py:384
  233.9 16.8 %collective-permute-start.3 = (bf16[1,1,768]{2,1,0:T(2,128)(2,1)}, bf16[1,1,768]{2,1,0:T(2,128)(2,1)}, u32[]{:S(2)}, u32[]{:S(2)}) collective-permute-start(bf16[1,1,768]{2,1,0:T(2,128)(2,1)} %get-tuple-element.102), channel_id=1, source_target_pairs={{0,1},{1,2},{2,3},{4,5},{5,6},{6,7},{8,9},{9,10},{10,11},{12,13},{... | collective-permute-start | bytes 4616 | tf_op jit(solution)/shard_map/ppermute | solution.py:384
  237.4 16.1 %collective-permute-start.2 = (bf16[1,1,768]{2,1,0:T(2,128)(2,1)}, bf16[1,1,768]{2,1,0:T(2,128)(2,1)}, u32[]{:S(2)}, u32[]{:S(2)}) collective-permute-start(bf16[1,1,768]{2,1,0:T(2,128)(2,1)} %get-tuple-element.101), channel_id=1, source_target_pairs={{1,0},{2,1},{3,2},{5,4},{6,5},{7,6},{9,8},{10,9},{11,10},{13,12},{... | collective-permute-start | bytes 4616 | tf_op jit(solution)/shard_map/ppermute | solution.py:385
  256.3 5.9 %slice-start = ((s8[4718592]{0:T(1024)(128)(4,1)}), s8[4194304]{0:T(1024)(128)(4,1)S(1)}, s32[]{:S(2)}) async-start(s8[4718592]{0:T(1024)(128)(4,1)} %bitcast.225), calls=%async_computation.4 | async-start | bytes 8388608
  282.6 70.6 %reduce-scatter.7.cloned.1.call-start = ((), (), s32[]{:S(2)}) async-start(), calls=%async_computation.2 | async-start | bytes 983040
  288.7 6.5 %copy-start.27 = (bf16[128,1536]{1,0:T(8,128)(2,1)S(1)}, bf16[128,1536]{1,0:T(8,128)(2,1)}, u32[]{:S(2)}) copy-start(bf16[128,1536]{1,0:T(8,128)(2,1)} %copy-done.26) | copy-start | bytes 1179652
  288.7 9.0 %copy-start.8 = (bf16[16,48,768]{2,1,0:T(8,128)(2,1)S(1)}, bf16[16,48,768]{2,1,0:T(8,128)(2,1)}, u32[]{:S(2)}) copy-start(bf16[16,48,768]{2,1,0:T(8,128)(2,1)} %get-tuple-element.94) | copy-start | bytes 3538948
  302.3 36.0 %copy-start.55 = (f32[1,1,32,24]{3,2,1,0:T(8,128)S(1)}, f32[1,1,32,24]{3,2,1,0:T(8,128)}, u32[]{:S(2)}) copy-start(f32[1,1,32,24]{3,2,1,0:T(8,128)} %stack.47) | copy-start | bytes 9220
  302.3 36.0 %copy-start.56 = (f32[1,1,32,24]{3,2,1,0:T(8,128)S(1)}, f32[1,1,32,24]{3,2,1,0:T(8,128)}, u32[]{:S(2)}) copy-start(f32[1,1,32,24]{3,2,1,0:T(8,128)} %stack.43) | copy-start | bytes 9220
  302.3 36.0 %copy-start.57 = (f32[1,1,32,24]{3,2,1,0:T(8,128)S(1)}, f32[1,1,32,24]{3,2,1,0:T(8,128)}, u32[]{:S(2)}) copy-start(f32[1,1,32,24]{3,2,1,0:T(8,128)} %stack.46) | copy-start | bytes 9220
  302.3 36.0 %copy-start.58 = (f32[1,1,32,24]{3,2,1,0:T(8,128)S(1)}, f32[1,1,32,24]{3,2,1,0:T(8,128)}, u32[]{:S(2)}) copy-start(f32[1,1,32,24]{3,2,1,0:T(8,128)} %stack.45) | copy-start | bytes 9220
  302.3 36.0 %copy-start.59 = (f32[1,1,32,24]{3,2,1,0:T(8,128)S(1)}, f32[1,1,32,24]{3,2,1,0:T(8,128)}, u32[]{:S(2)}) copy-start(f32[1,1,32,24]{3,2,1,0:T(8,128)} %stack.42) | copy-start | bytes 9220
  302.3 36.0 %copy-start.60 = (f32[1,1,32,24]{3,2,1,0:T(8,128)S(1)}, f32[1,1,32,24]{3,2,1,0:T(8,128)}, u32[]{:S(2)}) copy-start(f32[1,1,32,24]{3,2,1,0:T(8,128)} %stack.41) | copy-start | bytes 9220
  302.3 38.8 %copy-start.13 = (bf16[512,768]{0,1:T(8,128)(2,1)S(1)}, bf16[512,768]{0,1:T(8,128)(2,1)}, u32[]{:S(2)}) copy-start(bf16[512,768]{0,1:T(8,128)(2,1)} %copy-done.12) | copy-start | bytes 2359300
  531.1 8.8 %copy-start.62 = (f32[32,256]{1,0:T(8,128)S(1)}, f32[32,256]{1,0:T(8,128)}, u32[]{:S(2)}) copy-start(f32[32,256]{1,0:T(8,128)} %get-tuple-element.148) | copy-start | bytes 98308
  531.1 9.4 %copy-start.51 = (f32[16,1152]{1,0:T(8,128)S(1)}, f32[16,1152]{1,0:T(8,128)}, u32[]{:S(2)}) copy-start(f32[16,1152]{1,0:T(8,128)} %get-tuple-element.149) | copy-start | bytes 221188
  531.1 10.0 %copy-start.50 = (f32[24,1152]{1,0:T(8,128)S(1)}, f32[24,1152]{1,0:T(8,128)}, u32[]{:S(2)}) copy-start(f32[24,1152]{1,0:T(8,128)} %get-tuple-element.150) | copy-start | bytes 331780
  531.1 10.6 %copy-start.49 = (f32[48,768]{1,0:T(8,128)S(1)}, f32[48,768]{1,0:T(8,128)}, u32[]{:S(2)}) copy-start(f32[48,768]{1,0:T(8,128)} %get-tuple-element.151) | copy-start | bytes 442372
  531.1 11.3 %copy-start.48 = (f32[144,768]{1,0:T(8,128)S(1)}, f32[144,768]{1,0:T(8,128)}, u32[]{:S(2)}) copy-start(f32[144,768]{1,0:T(8,128)} %get-tuple-element.152) | copy-start | bytes 1327108
  (72 other events, 198.0 us)
Sparse Core Ops, SparseCore 0:
  282.7 23.4 reduce-scatter.8
  308.8 23.1 reduce-scatter.6

commit v3 on v2

--- a/solution.py
+++ b/solution.py
@@ -207,14 +207,14 @@
 
         def body(j, carry):
             a, f, s = j // 4, lax.rem(j // 2, 2), lax.rem(j, 2)
-            push(self.part.at[at.unit(a, f, s, 1 - at.c)], self.sib.at[j], self.one.at[0], self.one.at[1], at.sibling).start()
+            push(self.part(at.unit(a, f, s, 1 - at.c)), self.sib.at[j], self.one.at[0], self.one.at[1], at.sibling).start()
             return carry
 
         lax.fori_loop(0, 4 * at.lines, body, 0)
 
         def load(j, carry):
             a, f, s = j // 4, lax.rem(j // 2, 2), lax.rem(j, 2)
-            pltpu.make_async_copy(self.part.at[at.unit(a, f, s)], self.own.at[j], self.one.at[2]).start()
+            pltpu.make_async_copy(self.part(at.unit(a, f, s)), self.own.at[j], self.one.at[2]).start()
             return carry
 
         lax.fori_loop(0, 4 * at.lines, load, 0)
@@ -222,7 +222,7 @@
     def after_sibling(self):
         at = self.at
         n = 2 * at.lines
-        pltpu.make_async_copy(self.part.at[pl.ds(0, 2 * n)], self.own, self.one.at[2]).wait()
+        pltpu.make_async_copy(self.own, self.own, self.one.at[2]).wait()
         push(self.sib, self.sib, self.one.at[0], self.one.at[1], at.sibling).wait_recv()
 
         def far(q, carry):
@@ -342,36 +342,93 @@
     return stages + [Scatter.last_send, Scatter.finish]
 
 
-def scatter_kernel(dp_size, count, *refs):
+LANES = 128
+
+
+def window_start(unit, width, features):
+    tile = unit * width // LANES
+    return (tile - tile // (features // LANES - 1)) * LANES
+
+
+def whole_part(ref, rows, cols):
+    return lambda unit: ref.at[unit, pl.ds(*rows), pl.ds(*cols)]
+
+
+def window_part(ref, width):
+    features = ref.shape[1]
+    return lambda unit: ref.at[:, pl.ds(pl.multiple_of(window_start(unit, width, features), LANES), 2 * LANES)]
+
+
+def cut(shape, cap):
+    rows, cols = shape
+    pieces = max(1, round(rows * cols / cap))
+    while pieces > 1 and not (rows % (16 * pieces) == 0 or cols % (LANES * pieces) == 0):
+        pieces -= 1
+    if rows % (16 * pieces) == 0:
+        step = rows // pieces
+        return [((k * step, step), (0, cols)) for k in range(pieces)]
+    step = cols // pieces
+    return [((0, rows), (k * step, step)) for k in range(pieces)]
+
+
+def scatter_kernel(dp_size, chunks, count, width, *refs):
     parts, outs, rest = refs[:count], refs[count : 2 * count], refs[2 * count :]
     at = Place(dp_size)
     at.barrier()
-    jobs = [Scatter(at, parts[i], outs[i], rest[8 * i : 8 * i + 5], rest[8 * i + 5 : 8 * i + 8]) for i in range(count)]
+    jobs = []
+    for k, (i, rows, cols) in enumerate(chunks):
+        last = i == count - 1
+        part = window_part(parts[i], width) if last else whole_part(parts[i], rows, cols)
+        out = outs[i] if last else outs[i].at[pl.ds(*rows), pl.ds(*cols)]
+        jobs.append(Scatter(at, part, out, rest[8 * k : 8 * k + 5], rest[8 * k + 5 : 8 * k + 8]))
     for job in jobs:
         job.begin()
     stages = scatter_stages(at.lines)
-    for t in range(count + len(stages) - 1):
+    total = len(jobs)
+    for t in range(total + len(stages) - 1):
         for k, stage in enumerate(stages):
-            if 0 <= t - k < count:
+            if 0 <= t - k < total:
                 stage(jobs[t - k])
     for job in jobs:
         job.drain()
 
 
-def scatter_all(dp_size, parts, cid=2):
-    count = len(parts)
+def scatter_all(dp_size, parts, norm_rows, width, cap=36864, cid=2):
+    count = len(parts) + 1
     n = dp_size // 2
-    scratch = []
-    for x in parts:
-        scratch += scatter_buffers(n, x.shape[1:], x.dtype) + scatter_sems(n)
+    outs = [jax.ShapeDtypeStruct(x.shape[1:], jnp.float32) for x in parts]
+    outs.append(jax.ShapeDtypeStruct((norm_rows.shape[0], 2 * LANES), jnp.float32))
+    chunks, scratch = [], []
+    for i, x in enumerate(parts):
+        for rows, cols in cut(x.shape[1:], cap):
+            chunks.append((i, rows, cols))
+            scratch += scatter_buffers(n, (rows[1], cols[1]), x.dtype) + scatter_sems(n)
+    chunks.append((count - 1, None, None))
+    scratch += scatter_buffers(n, outs[-1].shape, jnp.float32) + scatter_sems(n)
     return pl.pallas_call(
-        functools.partial(scatter_kernel, dp_size, count),
-        out_shape=[jax.ShapeDtypeStruct(x.shape[1:], jnp.float32) for x in parts],
+        functools.partial(scatter_kernel, dp_size, chunks, count, width),
+        out_shape=outs,
         in_specs=[pl.BlockSpec(memory_space=pl.ANY)] * count,
         out_specs=[pl.BlockSpec(memory_space=pltpu.VMEM)] * count,
         scratch_shapes=scratch,
         compiler_params=pltpu.CompilerParams(collective_id=cid, has_side_effects=True, vmem_limit_bytes=64000000),
-    )(*parts)
+    )(*parts, norm_rows)
+
+
+def settle_kernel(*refs):
+    half = len(refs) // 2
+    for src, dst in zip(refs[:half], refs[half:]):
+        dst[...] = src[...]
+
+
+def settle(arrays):
+    spec = [pl.BlockSpec(memory_space=pltpu.VMEM)] * len(arrays)
+    return pl.pallas_call(
+        settle_kernel,
+        out_shape=[jax.ShapeDtypeStruct(x.shape, x.dtype) for x in arrays],
+        in_specs=spec,
+        out_specs=spec,
+    )(*arrays)
 
 
 def with_halo(x, sides, width):
@@ -594,18 +651,24 @@
     )(ids, seed, w_in, w_rec, emb, h0, h1, f0, f1, z0, z1)
 
 
-def pack_norms(gain, bias, devices=1):
-    both = jnp.stack([gain, bias], 0)
-    both = both.reshape(2, 3, devices, -1).transpose(2, 0, 1, 3).reshape(devices, -1)
-    both = jnp.pad(both, ((0, 0), (0, 1024 - both.shape[1]))).reshape(devices, 8, 128)
-    return both[0] if devices == 1 else both
-
-
-def unpack_norms(tiles, shape):
-    devices = tiles.shape[0]
-    flat = tiles.reshape(devices, -1)[:, : 2 * shape[0] * shape[1]].reshape(devices, 2, *shape)
-    both = flat.transpose(1, 2, 0, 3).reshape(2, shape[0], -1)
-    return both[0], both[1]
+def norm_back(residual, row_gain, seed):
+    centered = residual - jnp.mean(residual, axis=-1, keepdims=True)
+    spread = jnp.mean(centered * centered, axis=-1, keepdims=True)
+    scale = lax.rsqrt(spread + eps)
+    unit = centered * scale
+    inner = seed * row_gain
+    drop = jnp.mean(inner, axis=-1, keepdims=True) + unit * jnp.mean(inner * unit, axis=-1, keepdims=True)
+    gain_grad = jnp.sum(seed * unit, axis=0, keepdims=True)
+    return scale * (inner - drop), gain_grad, jnp.sum(seed, axis=0, keepdims=True)
+
+
+def place_norms(gain, bias, index, devices):
+    both = jnp.concatenate([gain, bias], 0)
+    width = both.shape[1]
+    shape = (width, devices * width)
+    spot = lax.broadcasted_iota(jnp.int32, shape, 0) + index * width == lax.broadcasted_iota(jnp.int32, shape, 1)
+    placed = plain_dot(both, spot.astype(both.dtype)).astype(both.dtype)
+    return jnp.pad(placed, ((0, 8 - both.shape[0]), (0, 0)))
 
 
 def local(
@@ -627,22 +690,22 @@
     conv_weight,
 ):
     dp_size, devices = lax.axis_size("dp"), lax.axis_size("dp") * lax.axis_size("seq")
-    norms = pack_norms(norm_gain, norm_bias)
+    me = lax.axis_index("dp") * lax.axis_size("seq") + lax.axis_index("seq")
+    norms = place_norms(norm_gain, norm_bias, me, devices)
     order = (char_table, gru_input, gru_recur, norms, qkv_weight, out_weight, up_weight, down_weight, merge_weight, conv_weight)
     gathered = gather_all(dp_size, devices, order)
-    full_norms = gathered[3]
+    all_norms = jnp.sum(gathered[3].astype(jnp.float32), axis=0)
     (full_table, full_input, full_recur, _, full_qkv, full_out, full_up, full_down, full_merge, full_conv) = [
         x.reshape(-1, x.shape[2]) for x in gathered
     ]
-    full_gain, full_bias = unpack_norms(full_norms, norm_gain.shape)
     seq_count, local_len, features = hidden.shape
     nchar = char_ids.shape[2]
     tokens = seq_count * local_len
     head_count = features // HD
     key_span = local_len * lax.axis_size("seq")
     score_scale = 1.0 / math.sqrt(HD)
-    gains = full_gain.astype(jnp.float32)
-    biases = full_bias.astype(jnp.float32)
+    gains = [all_norms[k : k + 1] for k in range(3)]
+    biases = [all_norms[k : k + 1] for k in range(3, 6)]
     flat_in = hidden.reshape(tokens, features)
     qkv = plain_dot(flat_in, full_qkv).astype(jnp.bfloat16)
     queries = qkv[:, :features].reshape(seq_count, local_len, head_count, HD)
@@ -685,9 +748,9 @@
     char_vec, char_emb, *kept = gru_forward(flat_ids, own_table, inward, recurrent)
     factors, keeps, priors = kept[:2], kept[2:4], kept[4:]
     merge_mats = full_merge.reshape(2, features, features)
-    merged_rows = jnp.concatenate(
-        [plain_dot(norm_two, merge_mats[0]), plain_dot(char_vec, merge_mats[1])], -1
-    ).astype(jnp.bfloat16)
+    streams = jnp.stack([norm_two, char_vec], 0)
+    merged_pair = jnp.einsum("btd,bdf->btf", streams, merge_mats, preferred_element_type=jnp.float32)
+    merged_rows = jnp.concatenate([merged_pair[0], merged_pair[1]], -1).astype(jnp.bfloat16)
     padded = with_halo(merged_rows.reshape(seq_count, local_len, 2 * features), (("seq", 1),), 1)
     kernel = full_conv.reshape(3, 2 * features, features)
     windows = [
@@ -699,16 +762,15 @@
         + plain_dot(windows[2], kernel[2])
     )
     resid_three = norm_two.astype(jnp.float32) + conv_out
-    result_rows, pull_three = jax.vjp(norm_rows, resid_three, gains[2], biases[2])
-    result = result_rows.astype(jnp.bfloat16).reshape(seq_count, local_len, features)
+    result = norm_rows(resid_three, gains[2], biases[2]).astype(jnp.bfloat16).reshape(seq_count, local_len, features)
     back_qkv, back_out, back_up, back_down = full_qkv, full_out, full_up, full_down
     back_merge, back_conv = full_merge, full_conv
     merge_back = back_merge.reshape(2, features, features)
     kernel_back = back_conv.reshape(3, 2 * features, features)
     seed_rows = cotangent.reshape(tokens, features).astype(jnp.float32)
-    grad_three, gain_three, bias_three = pull_three(seed_rows)
+    grad_three, gain_three, bias_three = norm_back(resid_three, gains[2], seed_rows)
     conv_seed = grad_three.astype(jnp.bfloat16)
-    conv_grad = jnp.concatenate([grad_dot(windows[offset], conv_seed) for offset in range(3)], 0)
+    conv_grad = grad_dot(jnp.concatenate(windows, 1), conv_seed)
     seed_padded = with_halo(conv_seed.reshape(seq_count, local_len, features), (("seq", 1),), 1)
     merged_grad = back_dot(
         seed_padded[:, 2 : 2 + local_len].reshape(tokens, features), kernel_back[0]
@@ -720,13 +782,12 @@
         seed_padded[:, 0:local_len].reshape(tokens, features), kernel_back[2]
     )
     merged_grad = merged_grad.astype(jnp.bfloat16)
-    token_part = merged_grad[:, :features]
-    char_part = merged_grad[:, features:]
-    merge_grad = jnp.concatenate([grad_dot(norm_two, token_part), grad_dot(char_vec, char_part)], 0)
-    two_grad = grad_three + back_dot(token_part, merge_back[0])
-    charvec_grad = back_dot(char_part, merge_back[1])
-    _, pull_two = jax.vjp(norm_rows, resid_two, gains[1], biases[1])
-    grad_two, gain_two, bias_two = pull_two(two_grad)
+    pair_grad = jnp.stack([merged_grad[:, :features], merged_grad[:, features:]], 0)
+    merge_grad = jnp.einsum("btd,btf->bdf", streams, pair_grad, preferred_element_type=jnp.float32)
+    stream_grad = jnp.einsum("btf,bdf->btd", pair_grad, merge_back, preferred_element_type=jnp.float32)
+    two_grad = grad_three + stream_grad[0]
+    charvec_grad = stream_grad[1]
+    grad_two, gain_two, bias_two = norm_back(resid_two, gains[1], two_grad)
     down_seed = grad_two.astype(jnp.bfloat16)
     down_grad = grad_dot(active, down_seed)
     active_grad = back_dot(down_seed, back_down)
@@ -734,8 +795,7 @@
     up_seed = pull_gelu(active_grad)[0].astype(jnp.bfloat16)
     up_grad = grad_dot(norm_one, up_seed)
     one_grad = grad_two + back_dot(up_seed, back_up)
-    _, pull_one = jax.vjp(norm_rows, resid_one, gains[0], biases[0])
-    grad_one, gain_one, bias_one = pull_one(one_grad)
+    grad_one, gain_one, bias_one = norm_back(resid_one, gains[0], one_grad)
     out_seed = grad_one.astype(jnp.bfloat16)
     out_grad = grad_dot(attended, out_seed)
     attn_seed = (
@@ -798,16 +858,17 @@
     )
     table_grad = jnp.zeros(full_table.shape, jnp.bfloat16)
     table_grad = lax.dynamic_update_slice_in_dim(table_grad, own_grad.astype(jnp.bfloat16), table_start, 0)
-    gain_grad = jnp.stack([gain_one, gain_two, gain_three], 0)
-    bias_grad = jnp.stack([bias_one, bias_two, bias_three], 0)
-    input_flat = input_mats.reshape(-1, input_mats.shape[2])
-    recur_flat = recur_sum.reshape(-1, recur_sum.shape[2])
-    terms = [merge_grad, conv_grad, down_grad, up_grad, out_grad, qkv_grad, recur_flat, input_flat, table_grad]
-    parts = [x.astype(jnp.bfloat16).reshape(devices, -1, x.shape[1]) for x in terms]
-    parts.append(pack_norms(gain_grad, bias_grad, devices))
-    sums = scatter_all(dp_size, parts)
-    merge_sum, conv_sum, down_sum, up_sum, out_sum, qkv_sum, recur_total, input_total, table_sum, norm_sum = sums
-    gain_sum, bias_sum = unpack_norms(norm_sum[None], norm_gain.shape)
+    norm_grads = jnp.concatenate(
+        [gain_one, gain_two, gain_three, bias_one, bias_two, bias_three, jnp.zeros((2, features), jnp.float32)], 0
+    )
+    terms = [input_mats, recur_sum, merge_grad, conv_grad, down_grad, up_grad, qkv_grad, out_grad, table_grad]
+    parts = [x.astype(jnp.bfloat16).reshape(devices, -1, x.shape[-1]) for x in terms]
+    width = norm_gain.shape[1]
+    *sums, norm_sum = scatter_all(dp_size, parts, norm_grads, width)
+    input_total, recur_total, merge_sum, conv_sum, down_sum, up_sum, qkv_sum, out_sum, table_sum = settle(sums)
+    skip = me * width - window_start(me, width, features)
+    gain_sum = lax.dynamic_slice(norm_sum, (0, skip), (3, width))
+    bias_sum = lax.dynamic_slice(norm_sum, (3, skip), (3, width))
     return (result, hidden_grad, qkv_sum, out_sum, up_sum, down_sum, gain_sum, bias_sum, table_sum, input_total, recur_total, merge_sum, conv_sum)
 
 

time: 558 us -> 492 us (0.88)
  local copies, waits for them, and re-layouts: 63.7 us -> 29.7 us
  matrix products: 75.6 us -> 62.5 us
  Pallas kernels: 349 us -> 337 us
    pallas_call x1 -> x2, Pallas kernels: 169 us -> 156 us  [the longest x1 153 us: scatter_all(): pl.pallas_call(functools.partial(scatter_kernel, dp_size, chunks, count,...]
    unnamed x214 -> x167, local copies, waits for them, and re-layouts: 30.8 us -> 20.2 us
    slice x10 -> x2, local copies, waits for them, and re-layouts: 10.5 us -> 0.66 us  [the longest x1 0.63 us: local(): gains = [all_norms[k:k + 1] for k in range(3)]]
    dot_general x9 -> x7, matrix products: 23.3 us -> 14 us  [back_dot(): lax.dot_general(left, right, (((1,), (1,)), ((), ())), preferred_element_...]
    another operation x7 -> x1, local copies, waits for them, and re-layouts: 8.29 us -> 0.03 us  [local(): jnp.stack([merged_grad[:, :features], merged_grad[:, features:]], 0)]
    dot_general x9 -> x8, matrix products: 22.8 us -> 19.4 us  [plain_dot(): return jnp.dot(left, right, preferred_element_type=jnp.float32)]
    dot_general x9 -> x5, matrix products: 19.5 us -> 18 us  [grad_dot(): lax.dot_general(left, right, (((0,), (0,)), ((), ())), preferred_element_...]
  transfers between devices with their start and end apart: 6 -> 6, of which waited for: 0 -> 1; matrix products, arithmetic and copies ran while one was open for 11% -> 8% of each run, Pallas kernels for 6% -> 7%
where the time goes in v3:
time: 492 us; the launch traced here: 485 us
  Pallas kernels  337 us (68%)
  matrix products  62.5 us (13%)
  local copies, waits for them, and re-layouts  29.7 us (6%)
  blocking collectives  18 us (4%)
  between operations  16.7 us (3%)
  other arithmetic  11.4 us (2%)
  starting transfers between devices  8.7 us (2%)
    pallas_call x1, Pallas kernels, scatter_all(): pl.pallas_call(functools.partial(scatter_kernel, dp_size, chunks, count,...  153 us
    pallas_call x1, Pallas kernels, gather_all(): pl.pallas_call(functools.partial(gather_kernel, dp_size, count), out_shap...  126 us
    pallas_call x1, Pallas kernels, gru_backward(): pl.pallas_call(gru_backward_kernel, grid=(nchar,), out_shape=[shape(w_in....  33.8 us
    pallas_call x1, Pallas kernels, gru_forward(): pl.pallas_call(gru_forward_kernel, grid=(nchar,), out_shape=[shape((rows,...  21.3 us
    unnamed x167, local copies, waits for them, and re-layouts  20.2 us
    dot_general x8, matrix products, plain_dot(): return jnp.dot(left, right, preferred_element_type=jnp.float32)  19.4 us
    dot_general x5, matrix products, grad_dot(): lax.dot_general(left, right, (((0,), (0,)), ((), ())), preferred_element_...  18 us
    dot_general x7, matrix products, back_dot(): lax.dot_general(left, right, (((1,), (1,)), ((), ())), preferred_element_...  14 us
  transfers between devices with their start and end apart: 6, of which 1 were waited for; matrix products, arithmetic and copies ran while one was open for 8% of the time, Pallas kernels for 7%

profile of v3, /device:TPU:0, one launch (start us, length us, event | category | flops | bytes accessed | tf_op | source)
XLA Modules:
  0.0 484.9 jit_solution(8656302039233684075)
XLA Ops:
  7.3 1.5 copy.36
  10.9 126.4 %shard_map.255 = (bf16[32,32,256]{2,1,0:T(8,128)(2,1)}, bf16[32,16,1152]{2,1,0:T(8,128)(2,1)}, bf16[32,24,1152]{2,1,0:T(8,128)(2,1)}, bf16[32,8,768]{2,1,0:T(8,1...) custom-call(bf16[32,256]{1,0:T(8,128)(2,1)} %refs_0_.1, ...), custom_call_target="tpu_custom_call" | custom-call | tf_op jit(solution)/shard_map/pallas_call | solution.py:181
  139.0 3.3 fusion
  142.3 8.8 %all-gather = bf16[512,768]{0,1:T(8,128)(2,1)S(1)} all-gather(bf16[128,768]{0,1:T(8,128)(2,1)S(1)} %get-tuple-element.117), channel_id=2, replica_groups=mesh['dp'=8,'seq'=4] {'seq'}, dimensions={0}, use_global_device_ids=true | all-gather | bytes 983040 | tf_op jit(solution)/shard_map/all_gather | solution.py:716
  151.7 9.3 %all-gather.1 = bf16[512,768]{0,1:T(8,128)(2,1)S(1)} all-gather(bf16[128,768]{0,1:T(8,128)(2,1)S(1)} %get-tuple-element.115), channel_id=3, replica_groups=mesh['dp'=8,'seq'=4] {'seq'}, dimensions={0}, use_global_device_ids=true | all-gather | bytes 983040 | tf_op jit(solution)/shard_map/all_gather | solution.py:715
  164.8 6.0 %multiply_convert_fusion.2 = (bf16[128,3072]{1,0:T(8,128)(2,1)S(1)}, f32[128,3072]{1,0:T(8,128)}, f32[128,3072]{1,0:T(8,128)}) fusion(bf16[768,3072]{1,0:T(8,128)(2,1)S(1)} %bitcast.201, f32[128,768]{1,0:T(8,128)S(1)} %get-tuple-element.134, f32[768]{0:T(1024)S(1)} %get-tuple-element.108, f32[768]{0:T(1024)S(1)} %get-tuple-element.109, ...), kind=kOutput, calls=%fused_computation.29 | convolution fusion | flops 630030336 | bytes 9051136 | tf_op jit(solution)/shard_map/dot_general | solution.py:458
  173.3 1.5 constant_dynamic-slice_fusion.1.table
  175.9 21.3 %shard_map.256 = (bf16[128,768]{1,0:T(8,128)(2,1)}, bf16[16,128,256]{2,1,0:T(8,128)(2,1)}, bf16[16,128,1536]{2,1,0:T(8,128)(2,1)}, bf16[16,128,1536]{2,1,0:T(8,1...) custom-call(s32[128,16]{1,0:T(8,128)} %bitcast.238, ...), custom_call_target="tpu_custom_call" | custom-call | tf_op jit(solution)/shard_map/pallas_call | solution.py:550
  199.4 2.8 collective-permute-start
  203.7 2.9 fusion.6
  208.6 1.5 fusion.39
  210.2 2.4 fusion.8
  212.7 2.4 fusion.92
  216.6 3.0 collective-permute-start.3
  219.6 2.7 fusion.5
  229.6 1.9 add_convert_fusion
  231.8 2.4 multiply_reduce_fusion.2
  236.8 1.7 copy.37
  238.5 2.7 convolution_convert_fusion.7
  241.2 4.8 copy.42
  246.0 2.4 copy.48
  248.5 6.4 %convolution_convert_fusion = bf16[4608,768]{1,0:T(8,128)(2,1)} fusion(bf16[128,1536]{1,0:T(8,128)(2,1)} %copy-done.40, bf16[128,768]{1,0:T(8,128)(2,1)} %bitcast.217, bf16[128,768]{1,0:T(8,128)(2,1)} %bitcast.215, bf16[128,1536]{1,0:T(8,128)(2,1)} %copy-done.13, f32[128,768]{1,0:T(8,128)} %copy-done.8), kind=kOutput, calls=%fused_computation | convolution fusion | flops 914325504 | bytes 8650752 | tf_op jit(solution)/shard_map/dot_general | solution.py:462
  258.9 1.6 copy.40
  262.8 33.8 %shard_map.257 = (bf16[2,256,1152]{2,1,0:T(8,128)(2,1)}, bf16[2,384,1152]{2,1,0:T(8,128)(2,1)}, f32[128,256]{1,0:T(8,128)}) custom-call(s32[128,16]{1,0:T(8,128)} %bitcast.239, f32[128,768]{1,0:T(8,128)} %slice_bitcast_fusion.15.seed, bf16[2,256,1152]{2,1,0:T(8,128)(2,1)} %bitcast.195, bf16[2,384,1152]{2,1,0:T(8,128)(2,1)} %bitcast.181, ...), custom_call_target="tpu_custom_call" | custom-call | tf_op jit(solution)/shard_map/pallas_call | solution.py:636
  298.4 2.2 convolution_convert_fusion.5
  300.7 1.6 convolution_convert_fusion.6
  303.5 3.6 convolution_convert_fusion.3
  307.1 3.6 convolution_convert_fusion.2
  313.8 4.0 fusion.28
  317.8 2.9 convolution_convert_fusion.1
  320.7 153.2 %shard_map.258 = (f32[16,1152]{1,0:T(8,128)}, f32[24,1152]{1,0:T(8,128)}, f32[48,768]{1,0:T(8,128)}, f32[144,768]{1,0:T(8,128)}, f32[96,768]{1,0:T(8,128)}, /*in...) custom-call(bf16[32,16,1152]{2,1,0:T(8,128)(2,1)} %bitcast.224, ...), custom_call_target="tpu_custom_call" | custom-call | tf_op jit(solution)/shard_map/pallas_call | solution.py:408
  475.3 2.6 shard_map.259
  (240 shorter events, 41.1 us)
Async XLA Ops:
  7.2 131.8 %copy-start.27 = (bf16[1,128,768]{2,1,0:T(8,128)(2,1)S(1)}, bf16[1,128,768]{2,1,0:T(8,128)(2,1)}, u32[]{:S(2)}) copy-start(bf16[1,128,768]{2,1,0:T(8,128)(2,1)} %param.16) | copy-start | bytes 589828
  7.2 303.5 %reduce-scatter.9.cloned.1.call-start = ((), (), s32[]{:S(2)}) async-start(), calls=%async_computation.3 | async-start | bytes 983040
  139.0 25.8 %slice-start.2 = ((s8[4718592]{0:T(1024)(128)(4,1)}), s8[4194304]{0:T(1024)(128)(4,1)S(1)}, s32[]{:S(2)}) async-start(s8[4718592]{0:T(1024)(128)(4,1)} %bitcast.199), calls=%async_computation.6 | async-start | bytes 8388608
  142.3 19.4 %copy-start.30 = (bf16[128,768]{0,1:T(8,128)(2,1)}, bf16[128,768]{0,1:T(8,128)(2,1)S(1)}, u32[]{:S(2)}) copy-start(bf16[128,768]{0,1:T(8,128)(2,1)S(1)} %get-tuple-element.116) | copy-start | bytes 589828
  151.1 11.7 %copy-start.24 = (bf16[512,768]{0,1:T(8,128)(2,1)}, bf16[512,768]{0,1:T(8,128)(2,1)S(1)}, u32[]{:S(2)}) copy-start(bf16[512,768]{0,1:T(8,128)(2,1)S(1)} %all-gather) | copy-start | bytes 2359300
  151.7 11.1 %copy-start.65 = (pred[512]{0:T(512)(128)(4,1)}, pred[512]{0:T(512)(128)(4,1)S(1)}, u32[]{:S(2)}) copy-start(pred[512]{0:T(512)(128)(4,1)S(1)} %iota_compare_fusion.2) | copy-start | bytes 1540
  164.1 6.7 %slice-start.6 = ((s8[4718592]{0:T(1024)(128)(4,1)}), s8[4194304]{0:T(1024)(128)(4,1)S(1)}, s32[]{:S(2)}) async-start(s8[4718592]{0:T(1024)(128)(4,1)} %bitcast.205), calls=%async_computation.10 | async-start | bytes 8388608
  164.5 6.3 %copy-start.49 = (f32[128]{0:T(128)}, f32[128]{0:T(128)S(1)}, u32[]{:S(2)}) copy-start(f32[128]{0:T(128)S(1)} %broadcast_multiply_fusion.8) | copy-start | bytes 1540
  164.7 6.1 %copy-start.59 = (f32[128]{0:T(128)}, f32[128]{0:T(128)S(1)}, u32[]{:S(2)}) copy-start(f32[128]{0:T(128)S(1)} %add_rsqrt_fusion.2) | copy-start | bytes 1540
  164.8 6.0 %slice-start.7 = ((s8[4718592]{0:T(1024)(128)(4,1)}), s8[524288]{0:T(1024)(128)(4,1)S(1)}, s32[]{:S(2)}) async-start(s8[4718592]{0:T(1024)(128)(4,1)} %bitcast.205), calls=%async_computation.11 | async-start | bytes 1048576
  175.9 22.8 %copy-start.32 = (bf16[1,128,768]{2,1,0:T(8,128)(2,1)}, bf16[1,128,768]{2,1,0:T(8,128)(2,1)S(1)}, u32[]{:S(2)}) copy-start(bf16[1,128,768]{2,1,0:T(8,128)(2,1)S(1)} %fusion.83) | copy-start | bytes 589828
  175.9 21.3 %copy-start.4 = (bf16[32,48,768]{2,1,0:T(8,128)(2,1)S(1)}, bf16[32,48,768]{2,1,0:T(8,128)(2,1)}, u32[]{:S(2)}) copy-start(bf16[32,48,768]{2,1,0:T(8,128)(2,1)} %get-tuple-element.62) | copy-start | bytes 7077892
  198.7 7.9 %copy-start.22 = (bf16[1,128,768]{2,1,0:T(8,128)(2,1)}, bf16[1,128,768]{2,1,0:T(8,128)(2,1)S(1)}, u32[]{:S(2)}) copy-start(bf16[1,128,768]{2,1,0:T(8,128)(2,1)S(1)} %get-tuple-element.125) | copy-start | bytes 589828
  198.7 7.9 %copy-start.23 = (bf16[1,128,768]{2,1,0:T(8,128)(2,1)}, bf16[1,128,768]{2,1,0:T(8,128)(2,1)S(1)}, u32[]{:S(2)}) copy-start(bf16[1,128,768]{2,1,0:T(8,128)(2,1)S(1)} %get-tuple-element.126) | copy-start | bytes 589828
  199.4 9.2 %collective-permute-start = (bf16[1,1,1536]{2,1,0:T(2,128)(2,1)}, bf16[1,1,1536]{2,1,0:T(2,128)(2,1)}, u32[]{:S(2)}, u32[]{:S(2)}) collective-permute-start(bf16[1,1,1536]{2,1,0:T(2,128)(2,1)} %get-tuple-element.123), channel_id=1, source_target_pairs={{0,1},{1,2},{2,3},{4,5},{5,6},{6,7},{8,9},{9,10},{10,11},{12,13},{... | collective-permute-start | bytes 9224 | tf_op jit(solution)/shard_map/ppermute | solution.py:441
  202.3 6.3 %collective-permute-start.1 = (bf16[1,1,1536]{2,1,0:T(2,128)(2,1)}, bf16[1,1,1536]{2,1,0:T(2,128)(2,1)}, u32[]{:S(2)}, u32[]{:S(2)}) collective-permute-start(bf16[1,1,1536]{2,1,0:T(2,128)(2,1)} %get-tuple-element.124), channel_id=1, source_target_pairs={{1,0},{2,1},{3,2},{5,4},{6,5},{7,6},{9,8},{10,9},{11,10},{13,12},{... | collective-permute-start | bytes 9224 | tf_op jit(solution)/shard_map/ppermute | solution.py:442
  210.1 14.1 %slice-start = ((s8[7077888]{0:T(1024)(128)(4,1)}), s8[4194304]{0:T(1024)(128)(4,1)S(1)}, s32[]{:S(2)}) async-start(s8[7077888]{0:T(1024)(128)(4,1)} %bitcast.186), calls=%async_computation.4 | async-start | bytes 8388608
  212.7 11.5 %slice-start.1 = ((s8[7077888]{0:T(1024)(128)(4,1)}), s8[2883584]{0:T(1024)(128)(4,1)S(1)}, s32[]{:S(2)}) async-start(s8[7077888]{0:T(1024)(128)(4,1)} %bitcast.186), calls=%async_computation.5 | async-start | bytes 5767168
  216.5 11.2 %copy-start.8 = (f32[128,768]{1,0:T(8,128)}, f32[128,768]{1,0:T(8,128)S(1)}, u32[]{:S(2)}) copy-start(f32[128,768]{1,0:T(8,128)S(1)} %get-tuple-element.112) | copy-start | bytes 1179652
  216.6 7.7 %collective-permute-start.3 = (bf16[1,1,768]{2,1,0:T(2,128)(2,1)S(1)}, bf16[1,1,768]{2,1,0:T(2,128)(2,1)S(1)}, u32[]{:S(2)}, u32[]{:S(2)}) collective-permute-start(bf16[1,1,768]{2,1,0:T(2,128)(2,1)S(1)} %get-tuple-element.128), channel_id=1, source_target_pairs={{0,1},{1,2},{2,3},{4,5},{5,6},{6,7},{8,9},{9,10},{10,11},{12,13},{... | collective-permute-start | bytes 4616 | tf_op jit(solution)/shard_map/ppermute | solution.py:441
  219.6 9.1 %slice-start.8 = ((s8[4718592]{0:T(1024)(128)(4,1)}), s8[4194304]{0:T(1024)(128)(4,1)S(1)}, s32[]{:S(2)}) async-start(s8[4718592]{0:T(1024)(128)(4,1)} %bitcast.208), calls=%async_computation.12 | async-start | bytes 8388608
  222.3 3.5 collective-permute-start.2
  248.5 63.8 %reduce-scatter.7.cloned.1.call-start = ((), (), s32[]{:S(2)}) async-start(), calls=%async_computation.2 | async-start | bytes 983040
  248.5 6.4 %copy-start.25 = (bf16[512,768]{0,1:T(8,128)(2,1)S(1)}, bf16[512,768]{0,1:T(8,128)(2,1)}, u32[]{:S(2)}) copy-start(bf16[512,768]{0,1:T(8,128)(2,1)} %copy-done.24) | copy-start | bytes 2359300
  248.5 6.4 %copy-start.44 = (bf16[128,768]{0,1:T(8,128)(2,1)S(1)}, bf16[128,768]{0,1:T(8,128)(2,1)}, u32[]{:S(2)}) copy-start(bf16[128,768]{0,1:T(8,128)(2,1)} %copy.37) | copy-start | bytes 589828
  248.5 6.4 %copy-start.66 = (pred[512]{0:T(512)(128)(4,1)S(1)}, pred[512]{0:T(512)(128)(4,1)}, u32[]{:S(2)}) copy-start(pred[512]{0:T(512)(128)(4,1)} %copy-done.65) | copy-start | bytes 1540
  262.8 34.8 %copy-start.62 = (f32[1,768]{1,0:T(1,128)S(1)}, f32[1,768]{1,0:T(1,128)}, u32[]{:S(2)}) copy-start(f32[1,768]{1,0:T(1,128)} %broadcast_in_dim.75) | copy-start | bytes 9220
  262.8 34.8 %copy-start.63 = (f32[1,768]{1,0:T(1,128)S(1)}, f32[1,768]{1,0:T(1,128)}, u32[]{:S(2)}) copy-start(f32[1,768]{1,0:T(1,128)} %broadcast_in_dim.72) | copy-start | bytes 9220
  262.8 35.6 %copy-start.33 = (bf16[1,128,768]{2,1,0:T(8,128)(2,1)S(1)}, bf16[1,128,768]{2,1,0:T(8,128)(2,1)}, u32[]{:S(2)}) copy-start(bf16[1,128,768]{2,1,0:T(8,128)(2,1)} %copy-done.32) | copy-start | bytes 589828
  262.8 35.6 %copy-start.35 = (bf16[1,128,768]{2,1,0:T(8,128)(2,1)S(1)}, bf16[1,128,768]{2,1,0:T(8,128)(2,1)}, u32[]{:S(2)}) copy-start(bf16[1,128,768]{2,1,0:T(8,128)(2,1)} %copy-done.34) | copy-start | bytes 589828
  262.8 35.6 %copy-start.37 = (bf16[1,128,768]{2,1,0:T(8,128)(2,1)S(1)}, bf16[1,128,768]{2,1,0:T(8,128)(2,1)}, u32[]{:S(2)}) copy-start(bf16[1,128,768]{2,1,0:T(8,128)(2,1)} %copy-done.36) | copy-start | bytes 589828
  262.8 35.6 %copy-start.43 = (bf16[128,768]{1,0:T(8,128)(2,1)S(1)}, bf16[128,768]{1,0:T(8,128)(2,1)}, u32[]{:S(2)}) copy-start(bf16[128,768]{1,0:T(8,128)(2,1)} %get-tuple-element.61) | copy-start | bytes 589828
  (53 other events, 117.4 us)
Sparse Core Ops, SparseCore 0:
  248.6 24.9 reduce-scatter.8
  276.1 23.1 reduce-scatter.6

commit v4 on v3

--- a/solution.py
+++ b/solution.py
@@ -536,6 +536,15 @@
     up = pl.BlockSpec((1, rows, cols), lambda i: (i, 0, 0))
     down = pl.BlockSpec((1, rows, cols), lambda i: (nchar - 1 - i, 0, 0))
     return [down, up] if backward else [up, down]
+
+
+def gru_cost(nchar, rows, width, units, products):
+    steps = 2 * nchar * rows
+    return pl.CostEstimate(
+        flops=12 * products * steps * (width + units) * units,
+        bytes_accessed=16 * steps * units,
+        transcendentals=3 * steps * units,
+    )
 
 
 def gru_forward(ids, table, w_in, w_rec):
@@ -563,6 +572,7 @@
             pltpu.VMEM((2, rows, units), jnp.float32),
         ],
         compiler_params=pltpu.CompilerParams(vmem_limit_bytes=60000000),
+        cost_estimate=gru_cost(nchar, rows, width, units, 1),
     )(ids, table, w_in, w_rec)
 
 
@@ -648,7 +658,113 @@
             pltpu.VMEM((2, nchar, rows, 4 * units), jnp.bfloat16),
         ],
         compiler_params=pltpu.CompilerParams(vmem_limit_bytes=60000000),
+        cost_estimate=gru_cost(nchar, rows, width, units, 2),
     )(ids, seed, w_in, w_rec, emb, h0, h1, f0, f1, z0, z1)
+
+
+def head_pair(q_ref, blocks, valid, pair, half):
+    features = q_ref.shape[1]
+    cols = pl.ds(pair * 2 * HD, 2 * HD)
+    queries = q_ref[:, cols]
+    keys = jnp.concatenate([b[:, cols] for b in blocks], 0)
+    values = jnp.concatenate([b[:, pl.ds(features + pair * 2 * HD, 2 * HD)] for b in blocks], 0)
+    scores = back_dot(one_head(queries, half), keys) * (1.0 / math.sqrt(HD))
+    scores = jnp.where(valid, scores, -1000000000.0)
+    weight = jnp.exp(scores - jnp.max(scores, axis=-1, keepdims=True))
+    return weight / jnp.sum(weight, axis=-1, keepdims=True), queries, keys, values
+
+
+def first_lanes(shape):
+    return lax.broadcasted_iota(jnp.int32, shape, 1) < HD
+
+
+def one_head(x, half):
+    keep = first_lanes(x.shape) if half == 0 else jnp.logical_not(first_lanes(x.shape))
+    return jnp.where(keep, x, jnp.zeros_like(x))
+
+
+def side_by_side(left, right):
+    return jnp.where(first_lanes(left.shape), left, right)
+
+
+def attention_kernel(count, q_ref, valid_ref, *refs):
+    blocks, out = refs[:count], refs[count]
+    valid = jnp.broadcast_to(valid_ref[...] > 0, (q_ref.shape[0], valid_ref.shape[1]))
+    for pair in range(q_ref.shape[1] // (2 * HD)):
+        both = []
+        for half in range(2):
+            probs, _, _, values = head_pair(q_ref, blocks, valid, pair, half)
+            both.append(plain_dot(probs.astype(jnp.bfloat16), values))
+        out[:, pl.ds(pair * 2 * HD, 2 * HD)] = side_by_side(*both).astype(out.dtype)
+
+
+def attention_back_kernel(count, q_ref, valid_ref, seed_ref, *refs):
+    blocks, q_out, outs = refs[:count], refs[count], refs[count + 1 :]
+    rows, features = q_ref.shape
+    scale = 1.0 / math.sqrt(HD)
+    valid = jnp.broadcast_to(valid_ref[...] > 0, (rows, valid_ref.shape[1]))
+    for pair in range(features // (2 * HD)):
+        cols = pl.ds(pair * 2 * HD, 2 * HD)
+        seed = seed_ref[:, cols]
+        q_both, k_both, v_both = [], [], []
+        for half in range(2):
+            probs, queries, keys, values = head_pair(q_ref, blocks, valid, pair, half)
+            probs_grad = back_dot(one_head(seed, half), values)
+            inner = jnp.sum(probs * probs_grad, axis=-1, keepdims=True)
+            score_grad = (probs * (probs_grad - inner)).astype(jnp.bfloat16)
+            q_both.append(plain_dot(score_grad, keys))
+            k_both.append(grad_dot(score_grad, queries))
+            v_both.append(grad_dot(probs.astype(jnp.bfloat16), seed))
+        q_out[:, cols] = (side_by_side(*q_both) * scale).astype(q_out.dtype)
+        k_grad = (side_by_side(*k_both) * scale).astype(jnp.bfloat16)
+        v_grad = side_by_side(*v_both).astype(jnp.bfloat16)
+        for j, out in enumerate(outs):
+            out[:, cols] = k_grad[j * rows : (j + 1) * rows]
+            out[:, pl.ds(features + pair * 2 * HD, 2 * HD)] = v_grad[j * rows : (j + 1) * rows]
+
+
+def attention_cost(rows, blocks, features, products):
+    span = rows * len(blocks)
+    return pl.CostEstimate(
+        flops=2 * products * rows * span * features,
+        bytes_accessed=8 * span * features,
+        transcendentals=rows * span * (features // HD),
+    )
+
+
+def attention(queries, valid, blocks):
+    rows, features = queries.shape
+    vmem = pl.BlockSpec(memory_space=pltpu.VMEM)
+    return pl.pallas_call(
+        functools.partial(attention_kernel, len(blocks)),
+        out_shape=jax.ShapeDtypeStruct((rows, features), jnp.bfloat16),
+        in_specs=[vmem] * (2 + len(blocks)),
+        out_specs=vmem,
+        cost_estimate=attention_cost(rows, blocks, features, 2),
+    )(queries, valid, *blocks)
+
+
+def attention_back(queries, valid, seed, blocks):
+    rows, features = queries.shape
+    vmem = pl.BlockSpec(memory_space=pltpu.VMEM)
+    return pl.pallas_call(
+        functools.partial(attention_back_kernel, len(blocks)),
+        out_shape=[jax.ShapeDtypeStruct((rows, features), jnp.bfloat16)]
+        + [jax.ShapeDtypeStruct((rows, 2 * features), jnp.bfloat16)] * len(blocks),
+        in_specs=[vmem] * (3 + len(blocks)),
+        out_specs=[vmem] * (1 + len(blocks)),
+        cost_estimate=attention_cost(rows, blocks, features, 5),
+    )(queries, valid, seed, *blocks)
+
+
+def from_next(x, axis, step):
+    size = lax.axis_size(axis)
+    return lax.ppermute(x, axis, [((i + step) % size, i) for i in range(size)])
+
+
+def to_next(x, axis, step):
+    size = lax.axis_size(axis)
+    return lax.ppermute(x, axis, [(i, (i + step) % size) for i in range(size)])
 
 
 def norm_back(residual, row_gain, seed):
@@ -701,44 +817,17 @@
     seq_count, local_len, features = hidden.shape
     nchar = char_ids.shape[2]
     tokens = seq_count * local_len
-    head_count = features // HD
     key_span = local_len * lax.axis_size("seq")
-    score_scale = 1.0 / math.sqrt(HD)
     gains = [all_norms[k : k + 1] for k in range(3)]
     biases = [all_norms[k : k + 1] for k in range(3, 6)]
     flat_in = hidden.reshape(tokens, features)
     qkv = plain_dot(flat_in, full_qkv).astype(jnp.bfloat16)
-    queries = qkv[:, :features].reshape(seq_count, local_len, head_count, HD)
-    own_keys = qkv[:, features : 2 * features].reshape(seq_count, local_len, features)
-    own_values = qkv[:, 2 * features :].reshape(seq_count, local_len, features)
-    all_keys, all_values = (
-        lax.all_gather(own_keys, "seq", axis=1, tiled=True),
-        lax.all_gather(own_values, "seq", axis=1, tiled=True),
-    )
-    all_keys = all_keys.reshape(seq_count, key_span, head_count, HD)
-    all_values = all_values.reshape(seq_count, key_span, head_count, HD)
-    key_valid = jnp.arange(key_span)[None, None, None, :] < lengths[:, None, None, None]
-
-    def score_block():
-        raw_scores = (
-            jnp.einsum("sqhd,skhd->shqk", queries, all_keys, preferred_element_type=jnp.float32)
-            * score_scale
-        )
-        return jnp.where(key_valid, raw_scores, -1000000000.0)
-
-    scores = score_block()
-    log_total = jax.nn.logsumexp(scores, axis=-1, keepdims=True)
-    attn_probs = jnp.exp(scores - log_total).astype(jnp.bfloat16)
-    attended = jnp.einsum(
-        "shqk,skhd->sqhd", attn_probs, all_values, preferred_element_type=jnp.float32
-    )
-    attended = attended.astype(jnp.bfloat16).reshape(tokens, features)
-    resid_one = flat_in.astype(jnp.float32) + plain_dot(attended, full_out)
-    norm_one = norm_rows(resid_one, gains[0], biases[0]).astype(jnp.bfloat16)
-    up_proj = plain_dot(norm_one, full_up)
-    active = gelu_exact(up_proj).astype(jnp.bfloat16)
-    resid_two = norm_one.astype(jnp.float32) + plain_dot(active, full_down)
-    norm_two = norm_rows(resid_two, gains[1], biases[1]).astype(jnp.bfloat16)
+    queries, own_kv = qkv[:, :features], qkv[:, features:]
+    peers = lax.axis_size("seq")
+    kv_blocks = [own_kv] + [from_next(own_kv, "seq", j) for j in range(1, peers)]
+    place = lax.rem(lax.axis_index("seq") + jnp.arange(peers), peers) * local_len
+    positions = place[:, None] + jnp.arange(local_len)[None, :]
+    key_valid = (positions < lengths[0]).astype(jnp.int32).reshape(1, key_span)
     assert seq_count == 1
     flat_ids = char_ids.reshape(tokens, nchar)
     table_start = groups[0] * SUBV
@@ -747,6 +836,13 @@
     recurrent = full_recur.reshape(2, -1, full_recur.shape[1])
     char_vec, char_emb, *kept = gru_forward(flat_ids, own_table, inward, recurrent)
     factors, keeps, priors = kept[:2], kept[2:4], kept[4:]
+    attended = attention(queries, key_valid, kv_blocks)
+    resid_one = flat_in.astype(jnp.float32) + plain_dot(attended, full_out)
+    norm_one = norm_rows(resid_one, gains[0], biases[0]).astype(jnp.bfloat16)
+    up_proj = plain_dot(norm_one, full_up)
+    active = gelu_exact(up_proj).astype(jnp.bfloat16)
+    resid_two = norm_one.astype(jnp.float32) + plain_dot(active, full_down)
+    norm_two = norm_rows(resid_two, gains[1], biases[1]).astype(jnp.bfloat16)
     merge_mats = full_merge.reshape(2, features, features)
     streams = jnp.stack([norm_two, char_vec], 0)
     merged_pair = jnp.einsum("btd,bdf->btf", streams, merge_mats, preferred_element_type=jnp.float32)
@@ -798,55 +894,12 @@
     grad_one, gain_one, bias_one = norm_back(resid_one, gains[0], one_grad)
     out_seed = grad_one.astype(jnp.bfloat16)
     out_grad = grad_dot(attended, out_seed)
-    attn_seed = (
-        back_dot(out_seed, back_out)
-        .astype(jnp.bfloat16)
-        .reshape(seq_count, local_len, head_count, HD)
-    )
-    probs_again = jnp.exp(score_block() - log_total)
-    probs_grad = jnp.einsum(
-        "sqhd,skhd->shqk", attn_seed, all_values, preferred_element_type=jnp.float32
-    )
-    score_grad = probs_again * (
-        probs_grad - jnp.sum(probs_again * probs_grad, axis=-1, keepdims=True)
-    )
-    score_grad = score_grad.astype(jnp.bfloat16)
-    query_grad = (
-        jnp.einsum("shqk,skhd->sqhd", score_grad, all_keys, preferred_element_type=jnp.float32)
-        * score_scale
-    )
-    key_grad = (
-        jnp.einsum("shqk,sqhd->skhd", score_grad, queries, preferred_element_type=jnp.float32)
-        * score_scale
-    )
-    value_grad = jnp.einsum(
-        "shqk,sqhd->skhd",
-        probs_again.astype(jnp.bfloat16),
-        attn_seed,
-        preferred_element_type=jnp.float32,
-    )
-    key_own, value_own = (
-        lax.psum_scatter(
-            key_grad.reshape(seq_count, key_span, features).astype(jnp.bfloat16),
-            "seq",
-            scatter_dimension=1,
-            tiled=True,
-        ).astype(jnp.float32),
-        lax.psum_scatter(
-            value_grad.reshape(seq_count, key_span, features).astype(jnp.bfloat16),
-            "seq",
-            scatter_dimension=1,
-            tiled=True,
-        ).astype(jnp.float32),
-    )
-    qkv_seed = jnp.concatenate(
-        [
-            query_grad.reshape(tokens, features),
-            key_own.reshape(tokens, features),
-            value_own.reshape(tokens, features),
-        ],
-        -1,
-    ).astype(jnp.bfloat16)
+    attn_seed = back_dot(out_seed, back_out).astype(jnp.bfloat16)
+    query_grad, *kv_grads = attention_back(queries, key_valid, attn_seed, kv_blocks)
+    kv_own = kv_grads[0].astype(jnp.float32)
+    for j in range(1, peers):
+        kv_own = kv_own + to_next(kv_grads[j], "seq", j).astype(jnp.float32)
+    qkv_seed = jnp.concatenate([query_grad, kv_own.astype(jnp.bfloat16)], -1)
     qkv_grad = grad_dot(flat_in, qkv_seed)
     hidden_grad = (
         (grad_one + back_dot(qkv_seed, back_qkv))

time: 492 us -> 436 us (0.89)
  local copies, waits for them, and re-layouts: 29.7 us -> 9.08 us
  blocking collectives: 18 us -> 0 us
  matrix products: 62.5 us -> 44.6 us
  between operations: 16.7 us -> 2.91 us
  Pallas kernels: 337 us -> 350 us
  starting transfers between devices: 8.7 us -> 15 us
  other arithmetic: 11.4 us -> 6.28 us
    unnamed x167 -> x59, local copies, waits for them, and re-layouts: 20.2 us -> 2.07 us
    all_gather x2 -> x0, blocking collectives: 18 us -> none  [the longest x1 9.26 us: local(): lax.all_gather(own_keys, 'seq', axis=1, tiled=True)]
    pallas_call x0 -> x2, Pallas kernels: none -> 15.8 us  [the longest x1 9.36 us: attention_back(): pl.pallas_call(functools.partial(attention_back_kernel, len(blocks)), out...]
    dot_general x6 -> x0, matrix products: 6.58 us -> none  [the longest x1 2.72 us: local(): jnp.einsum('shqk,sqhd->skhd', probs_again.astype(jnp.bfloat16), attn_seed...]
    ppermute x0 -> x6, starting transfers between devices: none -> 5.77 us  [the longest x3 3.55 us: to_next(): return lax.ppermute(x, axis, [(i, (i + step) % size) for i in range(size)])]
    dot_general x8, matrix products: 19.4 us -> 14.2 us  [plain_dot(): return jnp.dot(left, right, preferred_element_type=jnp.float32)]
  transfers between devices with their start and end apart: 6 -> 10, of which waited for: 1 -> 1; matrix products, arithmetic and copies ran while one was open for 8% -> 5% of each run, Pallas kernels for 7% -> 13%
where the time goes in v4:
time: 436 us; the launch traced here: 430 us
  Pallas kernels  350 us (80%)
  matrix products  44.6 us (10%)
  starting transfers between devices  15 us (3%)
  local copies, waits for them, and re-layouts  9.08 us (2%)
  other arithmetic  6.28 us (1%)
    pallas_call x1, Pallas kernels, scatter_all(): pl.pallas_call(functools.partial(scatter_kernel, dp_size, chunks, count,...  151 us
    pallas_call x1, Pallas kernels, gather_all(): pl.pallas_call(functools.partial(gather_kernel, dp_size, count), out_shap...  126 us
    pallas_call x1, Pallas kernels, gru_backward(): pl.pallas_call(gru_backward_kernel, grid=(nchar,), out_shape=[shape(w_in....  33.4 us
    pallas_call x1, Pallas kernels, gru_forward(): pl.pallas_call(gru_forward_kernel, grid=(nchar,), out_shape=[shape((rows,...  20.9 us
    dot_general x5, matrix products, grad_dot(): lax.dot_general(left, right, (((0,), (0,)), ((), ())), preferred_element_...  16.7 us
    dot_general x8, matrix products, plain_dot(): return jnp.dot(left, right, preferred_element_type=jnp.float32)  14.2 us
    dot_general x7, matrix products, back_dot(): lax.dot_general(left, right, (((1,), (1,)), ((), ())), preferred_element_...  10.1 us
    pallas_call x1, Pallas kernels, attention_back(): pl.pallas_call(functools.partial(attention_back_kernel, len(blocks)), out...  9.36 us
  transfers between devices with their start and end apart: 10, of which 1 were waited for; matrix products, arithmetic and copies ran while one was open for 5% of the time, Pallas kernels for 13%

profile of v4, /device:TPU:0, one launch (start us, length us, event | category | flops | bytes accessed | tf_op | source)
XLA Modules:
  0.0 429.5 jit_solution(8665156498525028633)
XLA Ops:
  2.2 126.4 %shard_map.255 = (bf16[32,32,256]{2,1,0:T(8,128)(2,1)}, bf16[32,16,1152]{2,1,0:T(8,128)(2,1)}, bf16[32,24,1152]{2,1,0:T(8,128)(2,1)}, bf16[32,8,768]{2,1,0:T(8,1...) custom-call(bf16[32,256]{1,0:T(8,128)(2,1)} %refs_0_.1, ...), custom_call_target="tpu_custom_call" | custom-call | tf_op jit(solution)/shard_map/pallas_call | solution.py:181
  128.6 2.8 fusion
  132.0 1.5 collective-permute-start.1
  135.2 1.5 constant_dynamic-slice_fusion.1.table
  136.7 20.9 %shard_map.257 = (bf16[128,768]{1,0:T(8,128)(2,1)}, bf16[16,128,256]{2,1,0:T(8,128)(2,1)}, bf16[16,128,1536]{2,1,0:T(8,128)(2,1)}, bf16[16,128,1536]{2,1,0:T(8,1...) custom-call(s32[128,16]{1,0:T(8,128)} %bitcast.159, ...), custom_call_target="tpu_custom_call" | custom-call | flops 12079595520 | bytes 25165824 | tf_op jit(solution)/shard_map/pallas_call | solution.py:559
  161.2 6.4 %shard_map.256 = bf16[128,768]{1,0:T(8,128)(2,1)} custom-call(bf16[128,768]{1,0:T(8,128)(2,1)} %slice.107.q_ref, s32[1,512]{1,0:T(1,128)} %bitcast.161, bf16[128,1536]{1,0:T(8,128)(2,1)} %copy-done.3, bf16[128,1536]{1,0:T(8,128)(2,1)} %copy-done.8, bf16[128,1536]{1,0:T(8,128)(2,1)} %copy-done.9, bf16[128,1536]{1,0:T(8,128)(2,1)} %collective-permute-done.2.refs_3_), custom_call_target="tpu_custom_call" | custom-call | flops 201326592 | bytes 3145728 | tf_op jit(solution)/shard_map/pallas_call | solution.py:738
  167.7 1.5 fusion.83
  169.4 6.5 %multiply_convert_fusion = (bf16[128,3072]{1,0:T(8,128)(2,1)S(1)}, f32[128,3072]{1,0:T(8,128)S(1)}, f32[128,3072]{1,0:T(8,128)S(1)}) fusion(bf16[768,3072]{1,0:T(8,128)(2,1)} %bitcast.142, f32[128,768]{1,0:T(8,128)S(1)} %get-tuple-element.139, f32[768]{0:T(1024)S(1)} %get-tuple-element.118, f32[768]{0:T(1024)S(1)} %get-tuple-element.119, ...), kind=kOutput, calls=%fused_computation.21 | convolution fusion | flops 630030336 | bytes 9051136 | tf_op jit(solution)/shard_map/dot_general | solution.py:458
  176.0 0.9 fusion.84
  178.2 2.5 collective-permute-start.3
  180.7 1.3 collective-permute-start.4
  182.5 1.2 collective-permute-done.4
  186.4 3.8 collective-permute-start.6
  190.2 4.9 %convolution_convert_fusion = bf16[4608,768]{1,0:T(8,128)(2,1)} fusion(bf16[128,1536]{1,0:T(8,128)(2,1)S(1)} %get-tuple-element.129, bf16[128,768]{1,0:T(8,128)(2,1)S(1)} %bitcast.153, bf16[128,768]{1,0:T(8,128)(2,1)S(1)} %bitcast.151, bf16[128,1536]{1,0:T(8,128)(2,1)S(1)} %get-tuple-element.128, f32[128,768]{1,0:T(8,128)S(1)} %get-tuple-element.122), kind=kOutput, calls=%fused_computation | convolution fusion | flops 914325504 | bytes 8650752 | tf_op jit(solution)/shard_map/dot_general | solution.py:462
  196.1 1.7 collective-permute-start.5
  202.9 3.6 convolution_convert_fusion.3
  206.4 1.9 add_convert_fusion
  208.4 2.4 multiply_reduce_fusion.1
  210.9 1.2 convolution_convert_fusion.7.seed_ref
  212.2 1.5 convolution_convert_fusion.6
  213.6 9.4 %shard_map.258 = (bf16[128,768]{1,0:T(8,128)(2,1)}, bf16[128,1536]{1,0:T(8,128)(2,1)}, bf16[128,1536]{1,0:T(8,128)(2,1)}, bf16[128,1536]{1,0:T(8,128)(2,1)}, bf16[128,1536]{1,0:T(8,128)(2,1)}) custom-call(bf16[128,768]{1,0:T(8,128)(2,1)} %slice.107.q_ref, s32[1,512]{1,0:T(1,128)} %bitcast.162, bf16[128,768]{1,0:T(8,128)(2,1)} %convolution_convert_fusion.7.seed_ref, ...), custom_call_target="tpu_custom_call" | custom-call | flops 503316480 | bytes 3145728 | tf_op jit(solution)/shard_map/pallas_call | solution.py:750
  223.7 2.7 collective-permute-start.8
  226.6 33.4 %shard_map.259 = (bf16[2,256,1152]{2,1,0:T(8,128)(2,1)}, bf16[2,384,1152]{2,1,0:T(8,128)(2,1)}, f32[128,256]{1,0:T(8,128)}) custom-call(s32[128,16]{1,0:T(8,128)} %bitcast.160, f32[128,768]{1,0:T(8,128)} %slice_bitcast_fusion.15.seed, bf16[2,256,1152]{2,1,0:T(8,128)(2,1)} %bitcast.167, bf16[2,384,1152]{2,1,0:T(8,128)(2,1)} %bitcast.165, ...), custom_call_target="tpu_custom_call" | custom-call | flops 24159191040 | bytes 25165824 | tf_op jit(solution)/shard_map/pallas_call | solution.py:646
  260.0 0.9 convert_dynamic-update-slice_fusion
  261.0 2.2 convolution_convert_fusion.5
  264.0 3.7 convolution_convert_fusion.2
  267.7 1.4 add_convert_fusion.1
  269.1 2.0 fusion.25
  271.1 3.0 convolution_convert_fusion.1
  274.1 151.2 %shard_map.260 = (f32[16,1152]{1,0:T(8,128)}, f32[24,1152]{1,0:T(8,128)}, f32[48,768]{1,0:T(8,128)}, f32[144,768]{1,0:T(8,128)}, f32[96,768]{1,0:T(8,128)}, /*in...) custom-call(bf16[32,16,1152]{2,1,0:T(8,128)(2,1)} %bitcast.156, ...), custom_call_target="tpu_custom_call" | custom-call | tf_op jit(solution)/shard_map/pallas_call | solution.py:408
  425.3 1.4 constant_dynamic-slice_fusion.2
  426.7 2.6 shard_map.261
  (128 shorter events, 18.2 us)
Async XLA Ops:
  128.6 5.1 %copy-start.22 = (s32[1,128,16]{1,2,0:T(8,128)S(1)}, s32[1,128,16]{1,2,0:T(8,128)}, u32[]{:S(2)}) copy-start(s32[1,128,16]{1,2,0:T(8,128)} %param.17) | copy-start | bytes 24580
  128.6 6.5 %copy-start.13 = (bf16[32,8,768]{2,1,0:T(8,128)(2,1)S(1)}, bf16[32,8,768]{2,1,0:T(8,128)(2,1)}, u32[]{:S(2)}) copy-start(bf16[32,8,768]{2,1,0:T(8,128)(2,1)} %get-tuple-element.60) | copy-start | bytes 1179652
  128.6 6.6 %copy-start.7 = (bf16[1,128,768]{2,1,0:T(8,128)(2,1)S(1)}, bf16[1,128,768]{2,1,0:T(8,128)(2,1)}, u32[]{:S(2)}) copy-start(bf16[1,128,768]{2,1,0:T(8,128)(2,1)} %param.20) | copy-start | bytes 589828
  131.4 26.2 %copy-start.3 = (bf16[128,1536]{1,0:T(8,128)(2,1)}, bf16[128,1536]{1,0:T(8,128)(2,1)S(1)}, u32[]{:S(2)}) copy-start(bf16[128,1536]{1,0:T(8,128)(2,1)S(1)} %slice.108.refs_0_) | copy-start | bytes 1179652
  131.5 28.9 %collective-permute-start = (bf16[128,1536]{1,0:T(8,128)(2,1)S(1)}, bf16[128,1536]{1,0:T(8,128)(2,1)S(1)}, u32[]{:S(2)}, u32[]{:S(2)}) collective-permute-start(bf16[128,1536]{1,0:T(8,128)(2,1)S(1)} %slice.108.refs_0_), channel_id=1, source_target_pairs={{1,0},{2,1},{3,2},{0,3},{5,4},{6,5},{7,6},{4,7},{9,8},{10,9},{11,1... | collective-permute-start | bytes 1179656 | tf_op jit(solution)/shard_map/ppermute | solution.py:762
  132.0 28.3 %collective-permute-start.1 = (bf16[128,1536]{1,0:T(8,128)(2,1)S(1)}, bf16[128,1536]{1,0:T(8,128)(2,1)S(1)}, u32[]{:S(2)}, u32[]{:S(2)}) collective-permute-start(bf16[128,1536]{1,0:T(8,128)(2,1)S(1)} %slice.108.refs_0_), channel_id=1, source_target_pairs={{2,0},{3,1},{0,2},{1,3},{6,4},{7,5},{4,6},{5,7},{10,8},{11,9},{8,1... | collective-permute-start | bytes 1179656 | tf_op jit(solution)/shard_map/ppermute | solution.py:762
  133.5 26.8 %collective-permute-start.2 = (bf16[128,1536]{1,0:T(8,128)(2,1)S(1)}, bf16[128,1536]{1,0:T(8,128)(2,1)}, u32[]{:S(2)}, u32[]{:S(2)}) collective-permute-start(bf16[128,1536]{1,0:T(8,128)(2,1)S(1)} %slice.108.refs_0_), channel_id=1, source_target_pairs={{3,0},{0,1},{1,2},{2,3},{7,4},{4,5},{5,6},{6,7},{11,8},{8,9},{9,10... | collective-permute-start | bytes 1179656 | tf_op jit(solution)/shard_map/ppermute | solution.py:762
  157.7 10.0 %copy-start.2 = (bf16[32,24,768]{2,1,0:T(8,128)(2,1)S(1)}, bf16[32,24,768]{2,1,0:T(8,128)(2,1)}, u32[]{:S(2)}) copy-start(bf16[32,24,768]{2,1,0:T(8,128)(2,1)} %get-tuple-element.59) | copy-start | bytes 3538948
  157.7 10.0 %copy-start.5 = (bf16[1,128,768]{2,1,0:T(8,128)(2,1)S(1)}, bf16[1,128,768]{2,1,0:T(8,128)(2,1)}, u32[]{:S(2)}) copy-start(bf16[1,128,768]{2,1,0:T(8,128)(2,1)} %param.16) | copy-start | bytes 589828
  167.7 8.3 %slice-start.4 = ((s8[4718592]{0:T(1024)(128)(4,1)}), s8[4194304]{0:T(1024)(128)(4,1)S(1)}, s32[]{:S(2)}) async-start(s8[4718592]{0:T(1024)(128)(4,1)} %bitcast.146), calls=%async_computation.4 | async-start | bytes 8388608
  167.7 14.3 %slice-start = ((s8[7077888]{0:T(1024)(128)(4,1)}), s8[4194304]{0:T(1024)(128)(4,1)S(1)}, s32[]{:S(2)}) async-start(s8[7077888]{0:T(1024)(128)(4,1)} %bitcast.131), calls=%async_computation | async-start | bytes 8388608
  169.4 41.4 %copy-start.18 = (f32[128]{0:T(128)}, f32[128]{0:T(128)S(1)}, u32[]{:S(2)}) copy-start(f32[128]{0:T(128)S(1)} %add_rsqrt_fusion.2) | copy-start | bytes 1540
  169.4 6.6 %slice-start.5 = ((s8[4718592]{0:T(1024)(128)(4,1)}), s8[524288]{0:T(1024)(128)(4,1)S(1)}, s32[]{:S(2)}) async-start(s8[4718592]{0:T(1024)(128)(4,1)} %bitcast.146), calls=%async_computation.5 | async-start | bytes 1048576
  169.4 12.6 %slice-start.1 = ((s8[7077888]{0:T(1024)(128)(4,1)}), s8[2883584]{0:T(1024)(128)(4,1)S(1)}, s32[]{:S(2)}) async-start(s8[7077888]{0:T(1024)(128)(4,1)} %bitcast.131), calls=%async_computation.1 | async-start | bytes 5767168
  178.2 4.3 collective-permute-start.3
  180.7 3.1 collective-permute-start.4
  186.4 12.0 %collective-permute-start.6 = (bf16[1,1,768]{2,1,0:T(2,128)(2,1)S(1)}, bf16[1,1,768]{2,1,0:T(2,128)(2,1)S(1)}, u32[]{:S(2)}, u32[]{:S(2)}) collective-permute-start(bf16[1,1,768]{2,1,0:T(2,128)(2,1)S(1)} %get-tuple-element.135), channel_id=1, source_target_pairs={{0,1},{1,2},{2,3},{4,5},{5,6},{6,7},{8,9},{9,10},{10,11},{12,13},{... | collective-permute-start | bytes 4616 | tf_op jit(solution)/shard_map/ppermute | solution.py:441
  196.1 3.2 collective-permute-start.5
  201.9 6.4 %slice-start.2 = ((s8[4718592]{0:T(1024)(128)(4,1)}), s8[4194304]{0:T(1024)(128)(4,1)S(1)}, s32[]{:S(2)}) async-start(s8[4718592]{0:T(1024)(128)(4,1)} %bitcast.143), calls=%async_computation.2 | async-start | bytes 8388608
  202.8 5.5 %slice-start.3 = ((s8[4718592]{0:T(1024)(128)(4,1)}), s8[524288]{0:T(1024)(128)(4,1)S(1)}, s32[]{:S(2)}) async-start(s8[4718592]{0:T(1024)(128)(4,1)} %bitcast.143), calls=%async_computation.3 | async-start | bytes 1048576
  223.0 44.7 %collective-permute-start.9 = (bf16[128,1536]{1,0:T(8,128)(2,1)}, bf16[128,1536]{1,0:T(8,128)(2,1)S(1)}, u32[]{:S(2)}, u32[]{:S(2)}) collective-permute-start(bf16[128,1536]{1,0:T(8,128)(2,1)} %get-tuple-element.73), channel_id=1, source_target_pairs={{0,3},{1,0},{2,1},{3,2},{4,7},{5,4},{6,5},{7,6},{8,11},{9,8},{10,9... | collective-permute-start | bytes 1179656 | tf_op jit(solution)/shard_map/ppermute | solution.py:767
  223.7 44.1 %collective-permute-start.8 = (bf16[128,1536]{1,0:T(8,128)(2,1)}, bf16[128,1536]{1,0:T(8,128)(2,1)}, u32[]{:S(2)}, u32[]{:S(2)}) collective-permute-start(bf16[128,1536]{1,0:T(8,128)(2,1)} %get-tuple-element.72), channel_id=1, source_target_pairs={{0,2},{1,3},{2,0},{3,1},{4,6},{5,7},{6,4},{7,5},{8,10},{9,11},{10,... | collective-permute-start | bytes 1179656 | tf_op jit(solution)/shard_map/ppermute | solution.py:767
  226.4 41.3 %collective-permute-start.7 = (bf16[128,1536]{1,0:T(8,128)(2,1)}, bf16[128,1536]{1,0:T(8,128)(2,1)}, u32[]{:S(2)}, u32[]{:S(2)}) collective-permute-start(bf16[128,1536]{1,0:T(8,128)(2,1)} %get-tuple-element.71), channel_id=1, source_target_pairs={{0,1},{1,2},{2,3},{3,0},{4,5},{5,6},{6,7},{7,4},{8,9},{9,10},{10,1... | collective-permute-start | bytes 1179656 | tf_op jit(solution)/shard_map/ppermute | solution.py:767
  226.6 34.4 %copy-start.12 = (bf16[128,768]{1,0:T(8,128)(2,1)S(1)}, bf16[128,768]{1,0:T(8,128)(2,1)}, u32[]{:S(2)}) copy-start(bf16[128,768]{1,0:T(8,128)(2,1)} %get-tuple-element.66) | copy-start | bytes 589828
  260.9 2.3 copy-start.4
  261.0 2.3 copy-start.17
  261.0 2.3 copy-start.16
  261.0 2.3 copy-start.20
  261.0 2.3 copy-start.21
  261.0 3.0 copy-start.19
  264.0 3.8 copy-start.14
  264.0 5.1 %copy-start = (bf16[32,24,2304]{2,1,0:T(8,128)(2,1)S(1)}, bf16[32,24,2304]{2,1,0:T(8,128)(2,1)}, u32[]{:S(2)}) copy-start(bf16[32,24,2304]{2,1,0:T(8,128)(2,1)} %get-tuple-element.58) | copy-start | bytes 10616836
  (7 other events, 10.0 us)

commit v5 on v4

--- a/solution.py
+++ b/solution.py
@@ -193,7 +193,7 @@
 
 
 def add_into(dst, src):
-    dst[...] = (wide(dst[...]) + wide(src[...])).astype(dst.dtype)
+    dst[...] = dst[...] + src[...]
 
 
 class Scatter:
@@ -808,10 +808,11 @@
     dp_size, devices = lax.axis_size("dp"), lax.axis_size("dp") * lax.axis_size("seq")
     me = lax.axis_index("dp") * lax.axis_size("seq") + lax.axis_index("seq")
     norms = place_norms(norm_gain, norm_bias, me, devices)
-    order = (char_table, gru_input, gru_recur, norms, qkv_weight, out_weight, up_weight, down_weight, merge_weight, conv_weight)
+    order = (char_table, gru_input, gru_recur, norms, qkv_weight, out_weight, up_weight, down_weight, merge_weight)
+    full_conv = lax.all_gather(conv_weight, ("dp", "seq"), axis=0, tiled=True)
     gathered = gather_all(dp_size, devices, order)
     all_norms = jnp.sum(gathered[3].astype(jnp.float32), axis=0)
-    (full_table, full_input, full_recur, _, full_qkv, full_out, full_up, full_down, full_merge, full_conv) = [
+    (full_table, full_input, full_recur, _, full_qkv, full_out, full_up, full_down, full_merge) = [
         x.reshape(-1, x.shape[2]) for x in gathered
     ]
     seq_count, local_len, features = hidden.shape
@@ -867,6 +868,7 @@
     grad_three, gain_three, bias_three = norm_back(resid_three, gains[2], seed_rows)
     conv_seed = grad_three.astype(jnp.bfloat16)
     conv_grad = grad_dot(jnp.concatenate(windows, 1), conv_seed)
+    conv_sum = lax.psum_scatter(conv_grad.astype(jnp.bfloat16), ("dp", "seq"), scatter_dimension=0, tiled=True).astype(jnp.float32)
     seed_padded = with_halo(conv_seed.reshape(seq_count, local_len, features), (("seq", 1),), 1)
     merged_grad = back_dot(
         seed_padded[:, 2 : 2 + local_len].reshape(tokens, features), kernel_back[0]
@@ -914,11 +916,11 @@
     norm_grads = jnp.concatenate(
         [gain_one, gain_two, gain_three, bias_one, bias_two, bias_three, jnp.zeros((2, features), jnp.float32)], 0
     )
-    terms = [input_mats, recur_sum, merge_grad, conv_grad, down_grad, up_grad, qkv_grad, out_grad, table_grad]
+    terms = [input_mats, recur_sum, merge_grad, down_grad, up_grad, qkv_grad, out_grad, table_grad]
     parts = [x.astype(jnp.bfloat16).reshape(devices, -1, x.shape[-1]) for x in terms]
     width = norm_gain.shape[1]
     *sums, norm_sum = scatter_all(dp_size, parts, norm_grads, width)
-    input_total, recur_total, merge_sum, conv_sum, down_sum, up_sum, qkv_sum, out_sum, table_sum = settle(sums)
+    input_total, recur_total, merge_sum, down_sum, up_sum, qkv_sum, out_sum, table_sum = settle(sums)
     skip = me * width - window_start(me, width, features)
     gain_sum = lax.dynamic_slice(norm_sum, (0, skip), (3, width))
     bias_sum = lax.dynamic_slice(norm_sum, (3, skip), (3, width))

time: 436 us -> 450 us (1.032)
  Pallas kernels: 350 us -> 328 us
  between operations: 2.91 us -> 16.9 us
  matrix products: 44.6 us -> 58.4 us
  local copies, waits for them, and re-layouts: 9.08 us -> 14.2 us
    pallas_call x1, Pallas kernels: 151 us -> 125 us  [scatter_all(): pl.pallas_call(functools.partial(scatter_kernel, dp_size, chunks, count,...]
    dot_general x8, matrix products: 14.2 us -> 21.4 us  [plain_dot(): return jnp.dot(left, right, preferred_element_type=jnp.float32)]
    dot_general x7, matrix products: 10.1 us -> 16.8 us  [back_dot(): lax.dot_general(left, right, (((1,), (1,)), ((), ())), preferred_element_...]
    unnamed x59 -> x125, local copies, waits for them, and re-layouts: 2.07 us -> 6.63 us
  transfers between devices with their start and end apart: 10 -> 12, of which waited for: 1 -> 1; matrix products, arithmetic and copies ran while one was open for 5% -> 15% of each run, Pallas kernels for 13% -> 74%
where the time goes in v5:
time: 450 us; the launch traced here: 444 us
  Pallas kernels  328 us (73%)
  matrix products  58.4 us (13%)
  between operations  16.9 us (4%)
  starting transfers between devices  15 us (3%)
  local copies, waits for them, and re-layouts  14.2 us (3%)
  other arithmetic  10 us (2%)
    pallas_call x1, Pallas kernels, gather_all(): pl.pallas_call(functools.partial(gather_kernel, dp_size, count), out_shap...  130 us
    pallas_call x1, Pallas kernels, scatter_all(): pl.pallas_call(functools.partial(scatter_kernel, dp_size, chunks, count,...  125 us
    pallas_call x1, Pallas kernels, gru_backward(): pl.pallas_call(gru_backward_kernel, grid=(nchar,), out_shape=[shape(w_in....  33.9 us
    dot_general x8, matrix products, plain_dot(): return jnp.dot(left, right, preferred_element_type=jnp.float32)  21.4 us
    pallas_call x1, Pallas kernels, gru_forward(): pl.pallas_call(gru_forward_kernel, grid=(nchar,), out_shape=[shape((rows,...  21.2 us
    dot_general x7, matrix products, back_dot(): lax.dot_general(left, right, (((1,), (1,)), ((), ())), preferred_element_...  16.8 us
    dot_general x5, matrix products, grad_dot(): lax.dot_general(left, right, (((0,), (0,)), ((), ())), preferred_element_...  16.5 us
    pallas_call x1, Pallas kernels, attention_back(): pl.pallas_call(functools.partial(attention_back_kernel, len(blocks)), out...  9.46 us
  transfers between devices with their start and end apart: 12, of which 1 were waited for; matrix products, arithmetic and copies ran while one was open for 15% of the time, Pallas kernels for 74%

profile of v5, /device:TPU:0, one launch (start us, length us, event | category | flops | bytes accessed | tf_op | source)
XLA Modules:
  0.0 443.7 jit_solution(6919790400361244684)
XLA Ops:
  9.5 129.8 %shard_map.255 = (bf16[32,32,256]{2,1,0:T(8,128)(2,1)}, bf16[32,16,1152]{2,1,0:T(8,128)(2,1)}, bf16[32,24,1152]{2,1,0:T(8,128)(2,1)}, bf16[32,8,768]{2,1,0:T(8,1...) custom-call(bf16[32,256]{1,0:T(8,128)(2,1)} %refs_0_.1, ...), custom_call_target="tpu_custom_call" | custom-call | tf_op jit(solution)/shard_map/pallas_call | solution.py:181
  139.3 2.8 fusion
  142.7 1.5 collective-permute-start.1
  146.1 1.5 constant_dynamic-slice_fusion.1.table
  147.6 21.2 %shard_map.257 = (bf16[128,768]{1,0:T(8,128)(2,1)}, bf16[16,128,256]{2,1,0:T(8,128)(2,1)}, bf16[16,128,1536]{2,1,0:T(8,128)(2,1)}, bf16[16,128,1536]{2,1,0:T(8,1...) custom-call(s32[128,16]{1,0:T(8,128)} %bitcast.130, ...), custom_call_target="tpu_custom_call" | custom-call | flops 12079595520 | bytes 25165824 | tf_op jit(solution)/shard_map/pallas_call | solution.py:559
  172.5 6.4 %shard_map.256 = bf16[128,768]{1,0:T(8,128)(2,1)} custom-call(bf16[128,768]{1,0:T(8,128)(2,1)} %slice.110.q_ref, s32[1,512]{1,0:T(1,128)} %bitcast.132, bf16[128,1536]{1,0:T(8,128)(2,1)} %copy-done.7, bf16[128,1536]{1,0:T(8,128)(2,1)} %copy-done.27, bf16[128,1536]{1,0:T(8,128)(2,1)} %copy-done.28, bf16[128,1536]{1,0:T(8,128)(2,1)} %copy-done.29), custom_call_target="tpu_custom_call" | custom-call | flops 201326592 | bytes 3145728 | tf_op jit(solution)/shard_map/pallas_call | solution.py:738
  179.0 1.5 fusion.95
  180.7 8.3 %multiply_convert_fusion = (bf16[128,3072]{1,0:T(8,128)(2,1)S(1)}, f32[128,3072]{1,0:T(8,128)}, f32[128,3072]{1,0:T(8,128)}) fusion(bf16[768,3072]{1,0:T(8,128)(2,1)} %bitcast.110, f32[128,768]{1,0:T(8,128)S(1)} %get-tuple-element.133, f32[768]{0:T(1024)S(1)} %get-tuple-element.112, f32[768]{0:T(1024)S(1)} %get-tuple-element.113, ...), kind=kOutput, calls=%fused_computation.24 | convolution fusion | flops 630030336 | bytes 9051136 | tf_op jit(solution)/shard_map/dot_general | solution.py:458
  192.4 2.5 collective-permute-start.3
  198.0 2.2 fusion.48
  200.2 2.4 fusion.5
  202.7 2.2 fusion.9
  205.0 2.3 fusion.97
  210.4 4.4 collective-permute-start.6
  214.9 1.5 collective-permute-start.5
  216.3 4.9 %convolution_convert_fusion = bf16[4608,768]{1,0:T(8,128)(2,1)} fusion(bf16[128,1536]{1,0:T(8,128)(2,1)S(1)} %copy-done.26, bf16[128,768]{1,0:T(8,128)(2,1)S(1)} %bitcast.124, bf16[128,768]{1,0:T(8,128)(2,1)S(1)} %bitcast.122, bf16[128,1536]{1,0:T(8,128)(2,1)S(1)} %copy-done.6, f32[128,768]{1,0:T(8,128)S(1)} %get-tuple-element.116), kind=kOutput, calls=%fused_computation | convolution fusion | flops 914325504 | bytes 8650752 | tf_op jit(solution)/shard_map/dot_general | solution.py:462
  221.3 2.6 fusion.7
  223.9 2.7 fusion.3
  226.7 2.7 fusion.2
  231.9 1.9 add_convert_fusion
  233.8 1.8 multiply_reduce_fusion.1
  238.2 9.5 %shard_map.258 = (bf16[128,768]{1,0:T(8,128)(2,1)}, bf16[128,1536]{1,0:T(8,128)(2,1)}, bf16[128,1536]{1,0:T(8,128)(2,1)}, bf16[128,1536]{1,0:T(8,128)(2,1)}, bf16[128,1536]{1,0:T(8,128)(2,1)}) custom-call(bf16[128,768]{1,0:T(8,128)(2,1)} %slice.110.q_ref, s32[1,512]{1,0:T(1,128)} %bitcast.133, bf16[128,768]{1,0:T(8,128)(2,1)} %convolution_convert_fusion.7.seed_ref, ...), custom_call_target="tpu_custom_call" | custom-call | flops 503316480 | bytes 3145728 | tf_op jit(solution)/shard_map/pallas_call | solution.py:750
  251.2 33.9 %shard_map.259 = (bf16[2,256,1152]{2,1,0:T(8,128)(2,1)}, bf16[2,384,1152]{2,1,0:T(8,128)(2,1)}, f32[128,256]{1,0:T(8,128)}) custom-call(s32[128,16]{1,0:T(8,128)} %bitcast.131, f32[128,768]{1,0:T(8,128)} %slice_bitcast_fusion.seed, bf16[2,256,1152]{2,1,0:T(8,128)(2,1)} %bitcast.138, bf16[2,384,1152]{2,1,0:T(8,128)(2,1)} %bitcast.136, ...), custom_call_target="tpu_custom_call" | custom-call | flops 24159191040 | bytes 25165824 | tf_op jit(solution)/shard_map/pallas_call | solution.py:646
  286.2 1.6 convolution_convert_fusion.6
  287.8 3.6 convolution_convert_fusion.3
  291.4 2.3 convolution_convert_fusion.5
  294.3 3.6 convolution_convert_fusion.2
  299.4 2.9 convolution_convert_fusion.1
  302.2 124.8 %shard_map.260 = (f32[16,1152]{1,0:T(8,128)}, f32[24,1152]{1,0:T(8,128)}, f32[48,768]{1,0:T(8,128)}, f32[96,768]{1,0:T(8,128)}, f32[24,3072]{1,0:T(8,128)}, /*in...) custom-call(bf16[32,16,1152]{2,1,0:T(8,128)(2,1)} %bitcast.127, ...), custom_call_target="tpu_custom_call" | custom-call | tf_op jit(solution)/shard_map/pallas_call | solution.py:408
  427.0 2.3 shard_map.261
  430.8 4.0 fusion.37
  434.7 1.7 convert_element_type.161
  (201 shorter events, 29.8 us)
Async XLA Ops:
  7.2 193.0 %all-gather.2.cloned.1.call-start = ((), (), s32[]{:S(2)}) async-start(), calls=%async_computation.1 | async-start | bytes 7299072 | tf_op jit(solution)/shard_map/all_gather | solution.py:812
  7.9 426.8 %reduce-scatter.2.cloned.1.call-start = ((), (), s32[]{:S(2)}) async-start(), calls=%async_computation.2 | async-start | bytes 7299072 | tf_op jit(solution)/shard_map/reduce_scatter | solution.py:871
  139.3 5.4 %copy-start.52 = (s32[1,128,16]{1,2,0:T(8,128)S(1)}, s32[1,128,16]{1,2,0:T(8,128)}, u32[]{:S(2)}) copy-start(s32[1,128,16]{1,2,0:T(8,128)} %param.17) | copy-start | bytes 24580
  139.3 8.2 %copy-start.35 = (bf16[32,8,768]{2,1,0:T(8,128)(2,1)S(1)}, bf16[32,8,768]{2,1,0:T(8,128)(2,1)}, u32[]{:S(2)}) copy-start(bf16[32,8,768]{2,1,0:T(8,128)(2,1)} %get-tuple-element.57) | copy-start | bytes 1179652
  142.2 26.7 %copy-start.7 = (bf16[128,1536]{1,0:T(8,128)(2,1)}, bf16[128,1536]{1,0:T(8,128)(2,1)S(1)}, u32[]{:S(2)}) copy-start(bf16[128,1536]{1,0:T(8,128)(2,1)S(1)} %slice.111.refs_0_) | copy-start | bytes 1179652
  142.2 29.3 %collective-permute-start = (bf16[128,1536]{1,0:T(8,128)(2,1)S(1)}, bf16[128,1536]{1,0:T(8,128)(2,1)S(1)}, u32[]{:S(2)}, u32[]{:S(2)}) collective-permute-start(bf16[128,1536]{1,0:T(8,128)(2,1)S(1)} %slice.111.refs_0_), channel_id=1, source_target_pairs={{1,0},{2,1},{3,2},{0,3},{5,4},{6,5},{7,6},{4,7},{9,8},{10,9},{11,1... | collective-permute-start | bytes 1179656 | tf_op jit(solution)/shard_map/ppermute | solution.py:762
  142.7 28.8 %collective-permute-start.1 = (bf16[128,1536]{1,0:T(8,128)(2,1)S(1)}, bf16[128,1536]{1,0:T(8,128)(2,1)S(1)}, u32[]{:S(2)}, u32[]{:S(2)}) collective-permute-start(bf16[128,1536]{1,0:T(8,128)(2,1)S(1)} %slice.111.refs_0_), channel_id=1, source_target_pairs={{2,0},{3,1},{0,2},{1,3},{6,4},{7,5},{4,6},{5,7},{10,8},{11,9},{8,1... | collective-permute-start | bytes 1179656 | tf_op jit(solution)/shard_map/ppermute | solution.py:762
  144.2 27.3 %collective-permute-start.2 = (bf16[128,1536]{1,0:T(8,128)(2,1)S(1)}, bf16[128,1536]{1,0:T(8,128)(2,1)S(1)}, u32[]{:S(2)}, u32[]{:S(2)}) collective-permute-start(bf16[128,1536]{1,0:T(8,128)(2,1)S(1)} %slice.111.refs_0_), channel_id=1, source_target_pairs={{3,0},{0,1},{1,2},{2,3},{7,4},{4,5},{5,6},{6,7},{11,8},{8,9},{9,10... | collective-permute-start | bytes 1179656 | tf_op jit(solution)/shard_map/ppermute | solution.py:762
  168.9 10.1 %copy-start.3 = (bf16[32,24,768]{2,1,0:T(8,128)(2,1)S(1)}, bf16[32,24,768]{2,1,0:T(8,128)(2,1)}, u32[]{:S(2)}) copy-start(bf16[32,24,768]{2,1,0:T(8,128)(2,1)} %get-tuple-element.56) | copy-start | bytes 3538948
  168.9 10.1 %copy-start.15 = (bf16[1,128,768]{2,1,0:T(8,128)(2,1)S(1)}, bf16[1,128,768]{2,1,0:T(8,128)(2,1)}, u32[]{:S(2)}) copy-start(bf16[1,128,768]{2,1,0:T(8,128)(2,1)} %param.16) | copy-start | bytes 589828
  179.0 10.1 %slice-start.2 = ((s8[4718592]{0:T(1024)(128)(4,1)}), s8[4194304]{0:T(1024)(128)(4,1)S(1)}, s32[]{:S(2)}) async-start(s8[4718592]{0:T(1024)(128)(4,1)} %bitcast.114), calls=%async_computation.5 | async-start | bytes 8388608
  180.5 8.6 %copy-start.39 = (f32[128]{0:T(128)}, f32[128]{0:T(128)S(1)}, u32[]{:S(2)}) copy-start(f32[128]{0:T(128)S(1)} %broadcast_multiply_fusion.8) | copy-start | bytes 1540
  180.7 8.4 %copy-start.46 = (f32[128]{0:T(128)}, f32[128]{0:T(128)S(1)}, u32[]{:S(2)}) copy-start(f32[128]{0:T(128)S(1)} %add_rsqrt_fusion.2) | copy-start | bytes 1540
  180.7 8.4 %slice-start.3 = ((s8[4718592]{0:T(1024)(128)(4,1)}), s8[524288]{0:T(1024)(128)(4,1)S(1)}, s32[]{:S(2)}) async-start(s8[4718592]{0:T(1024)(128)(4,1)} %bitcast.114), calls=%async_computation.6 | async-start | bytes 1048576
  191.0 5.1 %copy-start.24 = (bf16[1,128,768]{2,1,0:T(8,128)(2,1)S(1)}, bf16[1,128,768]{2,1,0:T(8,128)(2,1)}, u32[]{:S(2)}) copy-start(bf16[1,128,768]{2,1,0:T(8,128)(2,1)} %param.20) | copy-start | bytes 589828
  192.4 4.5 %collective-permute-start.3 = (bf16[1,1,1536]{2,1,0:T(2,128)(2,1)S(1)}, bf16[1,1,1536]{2,1,0:T(2,128)(2,1)S(1)}, u32[]{:S(2)}, u32[]{:S(2)}) collective-permute-start(bf16[1,1,1536]{2,1,0:T(2,128)(2,1)S(1)} %get-tuple-element.124), channel_id=1, source_target_pairs={{0,1},{1,2},{2,3},{4,5},{5,6},{6,7},{8,9},{9,10},{10,11},{12,13},{... | collective-permute-start | bytes 9224 | tf_op jit(solution)/shard_map/ppermute | solution.py:441
  194.8 3.2 collective-permute-start.4
  200.2 4.7 %copy-start.5 = (bf16[128,1536]{1,0:T(8,128)(2,1)}, bf16[128,1536]{1,0:T(8,128)(2,1)S(1)}, u32[]{:S(2)}) copy-start(bf16[128,1536]{1,0:T(8,128)(2,1)S(1)} %get-tuple-element.122) | copy-start | bytes 1179652
  207.3 9.0 %copy-start.6 = (bf16[128,1536]{1,0:T(8,128)(2,1)S(1)}, bf16[128,1536]{1,0:T(8,128)(2,1)}, u32[]{:S(2)}) copy-start(bf16[128,1536]{1,0:T(8,128)(2,1)} %copy-done.5) | copy-start | bytes 1179652
  207.3 9.0 %copy-start.26 = (bf16[128,1536]{1,0:T(8,128)(2,1)S(1)}, bf16[128,1536]{1,0:T(8,128)(2,1)}, u32[]{:S(2)}) copy-start(bf16[128,1536]{1,0:T(8,128)(2,1)} %get-tuple-element.123) | copy-start | bytes 1179652
  210.4 13.5 %collective-permute-start.6 = (bf16[1,1,768]{2,1,0:T(2,128)(2,1)}, bf16[1,1,768]{2,1,0:T(2,128)(2,1)}, u32[]{:S(2)}, u32[]{:S(2)}) collective-permute-start(bf16[1,1,768]{2,1,0:T(2,128)(2,1)} %get-tuple-element.129), channel_id=1, source_target_pairs={{0,1},{1,2},{2,3},{4,5},{5,6},{6,7},{8,9},{9,10},{10,11},{12,13},{... | collective-permute-start | bytes 4616 | tf_op jit(solution)/shard_map/ppermute | solution.py:441
  214.9 11.8 %collective-permute-start.5 = (bf16[1,1,768]{2,1,0:T(2,128)(2,1)}, bf16[1,1,768]{2,1,0:T(2,128)(2,1)}, u32[]{:S(2)}, u32[]{:S(2)}) collective-permute-start(bf16[1,1,768]{2,1,0:T(2,128)(2,1)} %get-tuple-element.128), channel_id=1, source_target_pairs={{1,0},{2,1},{3,2},{5,4},{6,5},{7,6},{9,8},{10,9},{11,10},{13,12},{... | collective-permute-start | bytes 4616 | tf_op jit(solution)/shard_map/ppermute | solution.py:442
  223.9 7.4 %slice-start.4 = ((s8[4718592]{0:T(1024)(128)(4,1)}), s8[4194304]{0:T(1024)(128)(4,1)S(1)}, s32[]{:S(2)}) async-start(s8[4718592]{0:T(1024)(128)(4,1)} %bitcast.117), calls=%async_computation.7 | async-start | bytes 8388608
  226.6 4.6 %slice-start.5 = ((s8[4718592]{0:T(1024)(128)(4,1)}), s8[524288]{0:T(1024)(128)(4,1)S(1)}, s32[]{:S(2)}) async-start(s8[4718592]{0:T(1024)(128)(4,1)} %bitcast.117), calls=%async_computation.8 | async-start | bytes 1048576
  236.9 13.5 %copy-start.9 = (f32[2,128,768]{2,1,0:T(8,128)S(1)}, f32[2,128,768]{2,1,0:T(8,128)}, u32[]{:S(2)}) copy-start(f32[2,128,768]{2,1,0:T(8,128)} %copy-done.8) | copy-start | bytes 2359300
  247.6 50.3 %collective-permute-start.9 = (bf16[128,1536]{1,0:T(8,128)(2,1)}, bf16[128,1536]{1,0:T(8,128)(2,1)S(1)}, u32[]{:S(2)}, u32[]{:S(2)}) collective-permute-start(bf16[128,1536]{1,0:T(8,128)(2,1)} %get-tuple-element.69), channel_id=1, source_target_pairs={{0,3},{1,0},{2,1},{3,2},{4,7},{5,4},{6,5},{7,6},{8,11},{9,8},{10,9... | collective-permute-start | bytes 1179656 | tf_op jit(solution)/shard_map/ppermute | solution.py:767
  249.0 48.9 %collective-permute-start.8 = (bf16[128,1536]{1,0:T(8,128)(2,1)}, bf16[128,1536]{1,0:T(8,128)(2,1)}, u32[]{:S(2)}, u32[]{:S(2)}) collective-permute-start(bf16[128,1536]{1,0:T(8,128)(2,1)} %get-tuple-element.68), channel_id=1, source_target_pairs={{0,2},{1,3},{2,0},{3,1},{4,6},{5,7},{6,4},{7,5},{8,10},{9,11},{10,... | collective-permute-start | bytes 1179656 | tf_op jit(solution)/shard_map/ppermute | solution.py:767
  250.5 47.5 %collective-permute-start.7 = (bf16[128,1536]{1,0:T(8,128)(2,1)}, bf16[128,1536]{1,0:T(8,128)(2,1)}, u32[]{:S(2)}, u32[]{:S(2)}) collective-permute-start(bf16[128,1536]{1,0:T(8,128)(2,1)} %get-tuple-element.67), channel_id=1, source_target_pairs={{0,1},{1,2},{2,3},{3,0},{4,5},{5,6},{6,7},{7,4},{8,9},{9,10},{10,1... | collective-permute-start | bytes 1179656 | tf_op jit(solution)/shard_map/ppermute | solution.py:767
  251.2 34.9 %copy-start.17 = (bf16[128,768]{1,0:T(8,128)(2,1)S(1)}, bf16[128,768]{1,0:T(8,128)(2,1)}, u32[]{:S(2)}) copy-start(bf16[128,768]{1,0:T(8,128)(2,1)} %shard_map.256) | copy-start | bytes 589828
  286.2 5.2 %copy-start.14 = (bf16[1024,256]{1,0:T(8,128)(2,1)}, bf16[1024,256]{1,0:T(8,128)(2,1)S(1)}, u32[]{:S(2)}) copy-start(bf16[1024,256]{1,0:T(8,128)(2,1)S(1)} %convert_dynamic-update-slice_fusion) | copy-start | bytes 1572868
  287.7 3.6 copy-start.34
  294.3 3.6 copy-start.36
  (42 other events, 76.0 us)
Sparse Core Ops, SparseCore 0:
  10.9 90.5 all-gather.1
  221.4 121.2 reduce-scatter.1

commit v6 on v4

--- a/solution.py
+++ b/solution.py
@@ -149,16 +149,83 @@
                     push(ref, ref, self.down_s.at[slot], self.line_r.at[slot], at.down).wait_send()
 
 
+class LineGather(Gather):
+    def begin(self):
+        at = self.at
+        me = at.unit(at.a, at.f, at.s)
+        pltpu.make_async_copy(self.shard, self.full.at[me], self.one.at[3]).start()
+        self.to_lines(self.shard, at.a, me, True, True)
+        self.to_pairs(self.shard, at.a, me)
+
+    def to_pairs(self, src, a, index):
+        at = self.at
+        push(src, self.full.at[index], self.one.at[2], self.line_r.at[at.lines + a], at.first).start()
+        self.across(src, a * 2 + at.f, index)
+
+    def after_first(self):
+        self.from_first(0)
+
+    def from_first(self, k):
+        at = self.at
+        for sign in (-1, 1) if k else (1,):
+            a = at.a + sign * k
+
+            @pl.when(a >= 0 if sign < 0 else a < at.lines)
+            def _():
+                index = at.unit(a, 1 - at.f, at.s)
+                ref = self.full.at[index]
+                push(ref, ref, self.one.at[2], self.line_r.at[at.lines + a], at.first).wait_recv()
+                self.across(ref, a * 2 + 1 - at.f, index)
+
+    def after_line(self, k, g):
+        at = self.at
+        if g:
+            self.from_first(k)
+            return
+        for sign in (-1, 1):
+            a = at.a + sign * k
+
+            @pl.when(a >= 0 if sign < 0 else a < at.lines)
+            def _():
+                index = at.unit(a, at.f, at.s)
+                ref = self.full.at[index]
+                push(ref, ref, self.up_s.at[a], self.line_r.at[a], at.up).wait_recv()
+                self.to_lines(ref, a, index, sign < 0, sign > 0)
+                self.to_pairs(ref, a, index)
+
+    def finish(self):
+        at, n = self.at, self.at.lines
+        me = at.unit(at.a, at.f, at.s)
+        half = self.full.at[pl.ds(0, 4 * n)]
+        push(half, half, self.sum_s.at[1], self.one.at[1], at.sibling).wait_recv()
+        pltpu.make_async_copy(self.shard, self.full.at[me], self.one.at[3]).wait()
+        push(half, half, self.sum_s.at[1], self.one.at[1], at.sibling).wait_send()
+        line = self.full.at[pl.ds(0, n)]
+        push(line, line, self.one.at[2], self.one.at[0], at.first).wait_send()
+        part = self.full.at[pl.ds(0, 2 * n)]
+        push(part, part, self.sum_s.at[0], self.one.at[0], at.second).wait_send()
+        ref = self.full.at[0]
+        for a in range(n):
+            @pl.when(jnp.logical_and(at.has_up, a <= at.a))
+            def _():
+                push(ref, ref, self.up_s.at[a], self.line_r.at[a], at.up).wait_send()
+
+            @pl.when(jnp.logical_and(at.has_down, a >= at.a))
+            def _():
+                push(ref, ref, self.down_s.at[a], self.line_r.at[a], at.down).wait_send()
+
+
 def gather_sems(n):
     dma = pltpu.SemaphoreType.DMA
     return [dma((2 * n,)), dma((2 * n,)), dma((2,)), dma((2 * n,)), dma((2 * n,)), dma((4,))]
 
 
-def gather_kernel(dp_size, count, *refs):
+def gather_kernel(dp_size, count, early, *refs):
     shards, fulls, sems = refs[:count], refs[count : 2 * count], refs[2 * count :]
     at = Place(dp_size)
     at.barrier()
-    jobs = [Gather(at, shards[i], fulls[i], sems[6 * i : 6 * i + 6]) for i in range(count)]
+    kinds = [LineGather if i in early else Gather for i in range(count)]
+    jobs = [kinds[i](at, shards[i], fulls[i], sems[6 * i : 6 * i + 6]) for i in range(count)]
     for job in jobs:
         job.begin()
     for job in jobs:
@@ -176,10 +243,10 @@
         job.finish()
 
 
-def gather_all(dp_size, devices, shards, cid=1):
+def gather_all(dp_size, devices, shards, early, cid=1):
     count = len(shards)
     return pl.pallas_call(
-        functools.partial(gather_kernel, dp_size, count),
+        functools.partial(gather_kernel, dp_size, count, early),
         out_shape=[jax.ShapeDtypeStruct((devices,) + x.shape, x.dtype) for x in shards],
         in_specs=[pl.BlockSpec(memory_space=pl.ANY)] * count,
         out_specs=[pl.BlockSpec(memory_space=pl.ANY)] * count,
@@ -193,13 +260,14 @@
 
 
 def add_into(dst, src):
-    dst[...] = (wide(dst[...]) + wide(src[...])).astype(dst.dtype)
+    dst[...] = dst[...] + src[...]
 
 
 class Scatter:
     def __init__(self, at, part, out, bufs, sems):
         self.at, self.part, self.out = at, part, out
         self.own, self.sib, self.sec, self.line, self.fst = bufs
+        self.per = 2
         self.one, self.line_s, self.line_r = sems
 
     def begin(self):
@@ -253,13 +321,16 @@
 
         lax.fori_loop(0, 2 * at.lines, body, 0)
 
+    def spot(self, q):
+        return q * 2 + self.at.s
+
     def hop(self, low, high, inward, dst, extra):
         at = self.at
         has, who = (at.has_up, at.down) if dst < 0 else (at.has_down, at.up)
 
         def take(q, carry):
             push(self.line.at[q], self.line.at[q], self.line_s.at[q], self.line_r.at[q], who).wait_recv()
-            add_into(self.own.at[q * 2 + at.s], self.line.at[q])
+            add_into(self.own.at[self.spot(q)], self.line.at[q])
             return carry
 
         @pl.when(has)
@@ -267,8 +338,9 @@
             lax.fori_loop(low, high, take, 0)
 
         def send(q, carry):
-            slot = q if dst < 0 else jnp.where(q // 2 == at.a + 1, 2 * at.lines + lax.rem(q, 2), q)
-            push(self.own.at[q * 2 + at.s], self.line.at[slot], self.line_s.at[q], self.line_r.at[slot], who).start()
+            per = self.per
+            slot = q if dst < 0 else jnp.where(q // per == at.a + 1, per * at.lines + lax.rem(q, per), q)
+            push(self.own.at[self.spot(q)], self.line.at[slot], self.line_s.at[q], self.line_r.at[slot], who).start()
             return carry
 
         lax.fori_loop(low, high, send, 0)
@@ -280,11 +352,11 @@
 
         @pl.when(jnp.logical_and(at.has_down, at.lines - 1 - at.a == h) if hops > 1 else at.has_down)
         def _():
-            self.hop(0, 2 * at.a, at.up, -1, None)
+            self.hop(0, self.per * at.a, at.up, -1, None)
 
         @pl.when(jnp.logical_and(at.has_up, at.a == h) if hops > 1 else at.has_up)
         def _():
-            self.hop(2 * at.a + 2, 2 * n, at.down, 1, None)
+            self.hop(self.per * (at.a + 1), self.per * n, at.down, 1, None)
 
     def ends(self, f, into):
         at = self.at
@@ -316,17 +388,67 @@
         push(self.fst, self.fst, self.one.at[5], self.one.at[6], at.first).wait_send()
 
         def body(q, carry):
-            @pl.when(q // 2 != at.a)
+            @pl.when(q // self.per != at.a)
             def _():
                 push(self.own.at[q], self.own.at[q], self.line_s.at[q], self.line_r.at[q], at.first).wait_send()
             return carry
 
-        lax.fori_loop(0, 2 * n, body, 0)
-
-
-def scatter_buffers(n, shape, dtype):
+        lax.fori_loop(0, self.per * n, body, 0)
+
+    def stages(self):
+        return [type(self).after_sibling, type(self).after_second] + self.hops() + [type(self).last_send, type(self).finish]
+
+    def hops(self):
+        lines = self.at.lines
+        return [functools.partial(type(self).along, h=h) for h in range(lines - 1 if lines <= 4 else 1)]
+
+
+class LineScatter(Scatter):
+    def __init__(self, *args):
+        super().__init__(*args)
+        self.per = 1
+
+    def spot(self, q):
+        return (2 * q + self.at.f) * 2 + self.at.s
+
+    def after_second(self):
+        super().after_second()
+        at = self.at
+
+        def send(a, carry):
+            push(self.own.at[(2 * a + 1 - at.f) * 2 + at.s], self.fst.at[a], self.one.at[5], self.one.at[6], at.first).start()
+            return carry
+
+        lax.fori_loop(0, at.lines, send, 0)
+
+    def after_first(self):
+        at = self.at
+        push(self.fst, self.fst, self.one.at[5], self.one.at[6], at.first).wait_recv()
+
+        def body(a, carry):
+            add_into(self.own.at[self.spot(a)], self.fst.at[a])
+            return carry
+
+        lax.fori_loop(0, at.lines, body, 0)
+
+    def finish(self):
+        at = self.at
+        self.out[...] = wide(self.own[self.spot(at.a)])
+        for has, slot in ((at.has_up, at.a), (at.has_down, at.lines)):
+            @pl.when(has)
+            def _():
+                ref = self.line.at[slot]
+                push(ref, ref, self.line_s.at[0], self.line_r.at[slot], at.first).wait_recv()
+                self.out[...] = self.out[...] + wide(ref[...])
+
+    def stages(self):
+        kind = type(self)
+        return [kind.after_sibling, kind.after_second, kind.after_first] + self.hops() + [kind.finish]
+
+
+def scatter_buffers(n, shape, dtype, late):
     v = lambda k: pltpu.VMEM((k,) + shape, dtype)
-    return [v(4 * n), v(4 * n), v(2 * n), v(2 * n + 2), pltpu.VMEM(shape, dtype)]
+    return [v(4 * n), v(4 * n), v(2 * n)] + ([v(n + 1), v(n)] if late else [v(2 * n + 2), pltpu.VMEM(shape, dtype)])
 
 
 def scatter_sems(n):
@@ -334,15 +456,8 @@
     return [dma((7,)), dma((2 * n,)), dma((2 * n + 2,))]
 
 
-def scatter_stages(lines):
-    hops = lines - 1 if lines <= 4 else 1
-    stages = [Scatter.after_sibling, Scatter.after_second]
-    for h in range(hops):
-        stages.append(functools.partial(Scatter.along, h=h))
-    return stages + [Scatter.last_send, Scatter.finish]
-
-
 LANES = 128
+AHEAD = 2
 
 
 def window_start(unit, width, features):
@@ -371,7 +486,19 @@
     return [((0, rows), (k * step, step)) for k in range(pieces)]
 
 
-def scatter_kernel(dp_size, chunks, count, width, *refs):
+def weave(many, few):
+    order, i, j = [], 0, 0
+    while i < len(many) or j < len(few):
+        if j < len(few) and (2 * j + 1) * len(many) <= (2 * i + 1) * len(few):
+            order.append(few[j])
+            j += 1
+        else:
+            order.append(many[i])
+            i += 1
+    return order
+
+
+def scatter_kernel(dp_size, chunks, count, width, late, *refs):
     parts, outs, rest = refs[:count], refs[count : 2 * count], refs[2 * count :]
     at = Place(dp_size)
     at.barrier()
@@ -380,33 +507,37 @@
         last = i == count - 1
         part = window_part(parts[i], width) if last else whole_part(parts[i], rows, cols)
         out = outs[i] if last else outs[i].at[pl.ds(*rows), pl.ds(*cols)]
-        jobs.append(Scatter(at, part, out, rest[8 * k : 8 * k + 5], rest[8 * k + 5 : 8 * k + 8]))
-    for job in jobs:
+        kind = LineScatter if i in late else Scatter
+        jobs.append(kind(at, part, out, rest[8 * k : 8 * k + 5], rest[8 * k + 5 : 8 * k + 8]))
+    total = len(jobs)
+    for job in jobs[:AHEAD]:
         job.begin()
-    stages = scatter_stages(at.lines)
-    total = len(jobs)
-    for t in range(total + len(stages) - 1):
-        for k, stage in enumerate(stages):
+    stages = [job.stages() for job in jobs]
+    depth = len(stages[0])
+    for t in range(total + depth - 1):
+        if t + AHEAD < total:
+            jobs[t + AHEAD].begin()
+        for k in range(depth):
             if 0 <= t - k < total:
-                stage(jobs[t - k])
+                stages[t - k][k](jobs[t - k])
     for job in jobs:
         job.drain()
 
 
-def scatter_all(dp_size, parts, norm_rows, width, cap=36864, cid=2):
+def scatter_all(dp_size, parts, norm_rows, width, late, cap=36864, cid=2):
     count = len(parts) + 1
     n = dp_size // 2
     outs = [jax.ShapeDtypeStruct(x.shape[1:], jnp.float32) for x in parts]
     outs.append(jax.ShapeDtypeStruct((norm_rows.shape[0], 2 * LANES), jnp.float32))
-    chunks, scratch = [], []
-    for i, x in enumerate(parts):
-        for rows, cols in cut(x.shape[1:], cap):
-            chunks.append((i, rows, cols))
-            scratch += scatter_buffers(n, (rows[1], cols[1]), x.dtype) + scatter_sems(n)
+    pieces = [(i, *piece) for i, x in enumerate(parts) for piece in cut(x.shape[1:], cap)]
+    chunks = weave([p for p in pieces if p[0] not in late], [p for p in pieces if p[0] in late])
+    scratch = []
+    for i, rows, cols in chunks:
+        scratch += scatter_buffers(n, (rows[1], cols[1]), parts[i].dtype, i in late) + scatter_sems(n)
     chunks.append((count - 1, None, None))
-    scratch += scatter_buffers(n, outs[-1].shape, jnp.float32) + scatter_sems(n)
+    scratch += scatter_buffers(n, outs[-1].shape, jnp.float32, count - 1 in late) + scatter_sems(n)
     return pl.pallas_call(
-        functools.partial(scatter_kernel, dp_size, chunks, count, width),
+        functools.partial(scatter_kernel, dp_size, chunks, count, width, late),
         out_shape=outs,
         in_specs=[pl.BlockSpec(memory_space=pl.ANY)] * count,
         out_specs=[pl.BlockSpec(memory_space=pltpu.VMEM)] * count,
@@ -809,7 +940,7 @@
     me = lax.axis_index("dp") * lax.axis_size("seq") + lax.axis_index("seq")
     norms = place_norms(norm_gain, norm_bias, me, devices)
     order = (char_table, gru_input, gru_recur, norms, qkv_weight, out_weight, up_weight, down_weight, merge_weight, conv_weight)
-    gathered = gather_all(dp_size, devices, order)
+    gathered = gather_all(dp_size, devices, order, (2, 9))
     all_norms = jnp.sum(gathered[3].astype(jnp.float32), axis=0)
     (full_table, full_input, full_recur, _, full_qkv, full_out, full_up, full_down, full_merge, full_conv) = [
         x.reshape(-1, x.shape[2]) for x in gathered
@@ -917,7 +1048,7 @@
     terms = [input_mats, recur_sum, merge_grad, conv_grad, down_grad, up_grad, qkv_grad, out_grad, table_grad]
     parts = [x.astype(jnp.bfloat16).reshape(devices, -1, x.shape[-1]) for x in terms]
     width = norm_gain.shape[1]
-    *sums, norm_sum = scatter_all(dp_size, parts, norm_grads, width)
+    *sums, norm_sum = scatter_all(dp_size, parts, norm_grads, width, (1, 3))
     input_total, recur_total, merge_sum, conv_sum, down_sum, up_sum, qkv_sum, out_sum, table_sum = settle(sums)
     skip = me * width - window_start(me, width, features)
     gain_sum = lax.dynamic_slice(norm_sum, (0, skip), (3, width))

time: 436 us -> 402 us (0.922)
  Pallas kernels: 350 us -> 317 us
    pallas_call x1, Pallas kernels: 151 us -> 134 us  [scatter_all(): pl.pallas_call(functools.partial(scatter_kernel, dp_size, chunks, count,...]
    pallas_call x1, Pallas kernels: 126 us -> 110 us  [gather_all(): pl.pallas_call(functools.partial(gather_kernel, dp_size, count, early), o...]
  transfers between devices with their start and end apart: 10 -> 10, of which waited for: 1 -> 1; matrix products, arithmetic and copies ran while one was open for 5% -> 5% of each run, Pallas kernels for 13% -> 14%
where the time goes in v6:
time: 402 us; the launch traced here: 396 us
  Pallas kernels  317 us (79%)
  matrix products  44.6 us (11%)
  starting transfers between devices  15.1 us (4%)
  local copies, waits for them, and re-layouts  9.08 us (2%)
  other arithmetic  6.28 us (2%)
    pallas_call x1, Pallas kernels, scatter_all(): pl.pallas_call(functools.partial(scatter_kernel, dp_size, chunks, count,...  134 us
    pallas_call x1, Pallas kernels, gather_all(): pl.pallas_call(functools.partial(gather_kernel, dp_size, count, early), o...  110 us
    pallas_call x1, Pallas kernels, gru_backward(): pl.pallas_call(gru_backward_kernel, grid=(nchar,), out_shape=[shape(w_in....  33.4 us
    pallas_call x1, Pallas kernels, gru_forward(): pl.pallas_call(gru_forward_kernel, grid=(nchar,), out_shape=[shape((rows,...  20.9 us
    dot_general x5, matrix products, grad_dot(): lax.dot_general(left, right, (((0,), (0,)), ((), ())), preferred_element_...  16.7 us
    dot_general x8, matrix products, plain_dot(): return jnp.dot(left, right, preferred_element_type=jnp.float32)  14.2 us
    dot_general x7, matrix products, back_dot(): lax.dot_general(left, right, (((1,), (1,)), ((), ())), preferred_element_...  10.1 us
    pallas_call x1, Pallas kernels, attention_back(): pl.pallas_call(functools.partial(attention_back_kernel, len(blocks)), out...  9.36 us
  transfers between devices with their start and end apart: 10, of which 1 were waited for; matrix products, arithmetic and copies ran while one was open for 5% of the time, Pallas kernels for 14%

profile of v6, /device:TPU:0, one launch (start us, length us, event | category | flops | bytes accessed | tf_op | source)
XLA Modules:
  0.0 395.9 jit_solution(11324057041828413301)
XLA Ops:
  2.2 110.2 %shard_map.255 = (bf16[32,32,256]{2,1,0:T(8,128)(2,1)}, bf16[32,16,1152]{2,1,0:T(8,128)(2,1)}, bf16[32,24,1152]{2,1,0:T(8,128)(2,1)}, bf16[32,8,768]{2,1,0:T(8,1...) custom-call(bf16[32,256]{1,0:T(8,128)(2,1)} %refs_0_.1, ...), custom_call_target="tpu_custom_call" | custom-call | tf_op jit(solution)/shard_map/pallas_call | solution.py:248
  112.4 2.8 fusion
  115.8 1.5 collective-permute-start.1
  119.0 1.5 constant_dynamic-slice_fusion.1.table
  120.5 20.9 %shard_map.257 = (bf16[128,768]{1,0:T(8,128)(2,1)}, bf16[16,128,256]{2,1,0:T(8,128)(2,1)}, bf16[16,128,1536]{2,1,0:T(8,128)(2,1)}, bf16[16,128,1536]{2,1,0:T(8,1...) custom-call(s32[128,16]{1,0:T(8,128)} %bitcast.159, ...), custom_call_target="tpu_custom_call" | custom-call | flops 12079595520 | bytes 25165824 | tf_op jit(solution)/shard_map/pallas_call | solution.py:690
  145.0 6.4 %shard_map.256 = bf16[128,768]{1,0:T(8,128)(2,1)} custom-call(bf16[128,768]{1,0:T(8,128)(2,1)} %slice.107.q_ref, s32[1,512]{1,0:T(1,128)} %bitcast.161, bf16[128,1536]{1,0:T(8,128)(2,1)} %copy-done.3, bf16[128,1536]{1,0:T(8,128)(2,1)} %copy-done.8, bf16[128,1536]{1,0:T(8,128)(2,1)} %copy-done.9, bf16[128,1536]{1,0:T(8,128)(2,1)} %collective-permute-done.2.refs_3_), custom_call_target="tpu_custom_call" | custom-call | flops 201326592 | bytes 3145728 | tf_op jit(solution)/shard_map/pallas_call | solution.py:869
  151.4 1.5 fusion.83
  153.2 6.5 %multiply_convert_fusion = (bf16[128,3072]{1,0:T(8,128)(2,1)S(1)}, f32[128,3072]{1,0:T(8,128)S(1)}, f32[128,3072]{1,0:T(8,128)S(1)}) fusion(bf16[768,3072]{1,0:T(8,128)(2,1)} %bitcast.142, f32[128,768]{1,0:T(8,128)S(1)} %get-tuple-element.139, f32[768]{0:T(1024)S(1)} %get-tuple-element.118, f32[768]{0:T(1024)S(1)} %get-tuple-element.119, ...), kind=kOutput, calls=%fused_computation.21 | convolution fusion | flops 630030336 | bytes 9051136 | tf_op jit(solution)/shard_map/dot_general | solution.py:589
  159.8 0.9 fusion.84
  162.0 2.5 collective-permute-start.3
  164.5 1.3 collective-permute-start.4
  166.3 1.2 collective-permute-done.4
  170.2 3.8 collective-permute-start.6
  174.0 4.9 %convolution_convert_fusion = bf16[4608,768]{1,0:T(8,128)(2,1)} fusion(bf16[128,1536]{1,0:T(8,128)(2,1)S(1)} %get-tuple-element.129, bf16[128,768]{1,0:T(8,128)(2,1)S(1)} %bitcast.153, bf16[128,768]{1,0:T(8,128)(2,1)S(1)} %bitcast.151, bf16[128,1536]{1,0:T(8,128)(2,1)S(1)} %get-tuple-element.128, f32[128,768]{1,0:T(8,128)S(1)} %get-tuple-element.122), kind=kOutput, calls=%fused_computation | convolution fusion | flops 914325504 | bytes 8650752 | tf_op jit(solution)/shard_map/dot_general | solution.py:593
  179.9 1.7 collective-permute-start.5
  186.7 3.6 convolution_convert_fusion.3
  190.2 1.9 add_convert_fusion
  192.2 2.4 multiply_reduce_fusion.1
  194.7 1.2 convolution_convert_fusion.7.seed_ref
  195.9 1.5 convolution_convert_fusion.6
  197.4 9.4 %shard_map.258 = (bf16[128,768]{1,0:T(8,128)(2,1)}, bf16[128,1536]{1,0:T(8,128)(2,1)}, bf16[128,1536]{1,0:T(8,128)(2,1)}, bf16[128,1536]{1,0:T(8,128)(2,1)}, bf16[128,1536]{1,0:T(8,128)(2,1)}) custom-call(bf16[128,768]{1,0:T(8,128)(2,1)} %slice.107.q_ref, s32[1,512]{1,0:T(1,128)} %bitcast.162, bf16[128,768]{1,0:T(8,128)(2,1)} %convolution_convert_fusion.7.seed_ref, ...), custom_call_target="tpu_custom_call" | custom-call | flops 503316480 | bytes 3145728 | tf_op jit(solution)/shard_map/pallas_call | solution.py:881
  207.5 2.7 collective-permute-start.8
  210.4 33.4 %shard_map.259 = (bf16[2,256,1152]{2,1,0:T(8,128)(2,1)}, bf16[2,384,1152]{2,1,0:T(8,128)(2,1)}, f32[128,256]{1,0:T(8,128)}) custom-call(s32[128,16]{1,0:T(8,128)} %bitcast.160, f32[128,768]{1,0:T(8,128)} %slice_bitcast_fusion.15.seed, bf16[2,256,1152]{2,1,0:T(8,128)(2,1)} %bitcast.167, bf16[2,384,1152]{2,1,0:T(8,128)(2,1)} %bitcast.165, ...), custom_call_target="tpu_custom_call" | custom-call | flops 24159191040 | bytes 25165824 | tf_op jit(solution)/shard_map/pallas_call | solution.py:777
  243.8 0.9 convert_dynamic-update-slice_fusion
  244.8 2.2 convolution_convert_fusion.5
  247.8 3.7 convolution_convert_fusion.2
  251.5 1.4 add_convert_fusion.1
  252.9 2.0 fusion.25
  254.9 3.0 convolution_convert_fusion.1
  257.9 133.8 %shard_map.260 = (f32[16,1152]{1,0:T(8,128)}, f32[24,1152]{1,0:T(8,128)}, f32[48,768]{1,0:T(8,128)}, f32[144,768]{1,0:T(8,128)}, f32[96,768]{1,0:T(8,128)}, /*in...) custom-call(bf16[32,16,1152]{2,1,0:T(8,128)(2,1)} %bitcast.156, ...), custom_call_target="tpu_custom_call" | custom-call | tf_op jit(solution)/shard_map/pallas_call | solution.py:539
  391.6 1.4 constant_dynamic-slice_fusion.2
  393.1 2.6 shard_map.261
  (128 shorter events, 18.2 us)
Async XLA Ops:
  112.4 5.1 %copy-start.22 = (s32[1,128,16]{1,2,0:T(8,128)S(1)}, s32[1,128,16]{1,2,0:T(8,128)}, u32[]{:S(2)}) copy-start(s32[1,128,16]{1,2,0:T(8,128)} %param.17) | copy-start | bytes 24580
  112.4 6.5 %copy-start.13 = (bf16[32,8,768]{2,1,0:T(8,128)(2,1)S(1)}, bf16[32,8,768]{2,1,0:T(8,128)(2,1)}, u32[]{:S(2)}) copy-start(bf16[32,8,768]{2,1,0:T(8,128)(2,1)} %get-tuple-element.60) | copy-start | bytes 1179652
  112.4 6.6 %copy-start.7 = (bf16[1,128,768]{2,1,0:T(8,128)(2,1)S(1)}, bf16[1,128,768]{2,1,0:T(8,128)(2,1)}, u32[]{:S(2)}) copy-start(bf16[1,128,768]{2,1,0:T(8,128)(2,1)} %param.20) | copy-start | bytes 589828
  115.3 26.2 %copy-start.3 = (bf16[128,1536]{1,0:T(8,128)(2,1)}, bf16[128,1536]{1,0:T(8,128)(2,1)S(1)}, u32[]{:S(2)}) copy-start(bf16[128,1536]{1,0:T(8,128)(2,1)S(1)} %slice.108.refs_0_) | copy-start | bytes 1179652
  115.3 28.8 %collective-permute-start = (bf16[128,1536]{1,0:T(8,128)(2,1)S(1)}, bf16[128,1536]{1,0:T(8,128)(2,1)S(1)}, u32[]{:S(2)}, u32[]{:S(2)}) collective-permute-start(bf16[128,1536]{1,0:T(8,128)(2,1)S(1)} %slice.108.refs_0_), channel_id=1, source_target_pairs={{1,0},{2,1},{3,2},{0,3},{5,4},{6,5},{7,6},{4,7},{9,8},{10,9},{11,1... | collective-permute-start | bytes 1179656 | tf_op jit(solution)/shard_map/ppermute | solution.py:893
  115.8 28.3 %collective-permute-start.1 = (bf16[128,1536]{1,0:T(8,128)(2,1)S(1)}, bf16[128,1536]{1,0:T(8,128)(2,1)S(1)}, u32[]{:S(2)}, u32[]{:S(2)}) collective-permute-start(bf16[128,1536]{1,0:T(8,128)(2,1)S(1)} %slice.108.refs_0_), channel_id=1, source_target_pairs={{2,0},{3,1},{0,2},{1,3},{6,4},{7,5},{4,6},{5,7},{10,8},{11,9},{8,1... | collective-permute-start | bytes 1179656 | tf_op jit(solution)/shard_map/ppermute | solution.py:893
  117.3 26.8 %collective-permute-start.2 = (bf16[128,1536]{1,0:T(8,128)(2,1)S(1)}, bf16[128,1536]{1,0:T(8,128)(2,1)}, u32[]{:S(2)}, u32[]{:S(2)}) collective-permute-start(bf16[128,1536]{1,0:T(8,128)(2,1)S(1)} %slice.108.refs_0_), channel_id=1, source_target_pairs={{3,0},{0,1},{1,2},{2,3},{7,4},{4,5},{5,6},{6,7},{11,8},{8,9},{9,10... | collective-permute-start | bytes 1179656 | tf_op jit(solution)/shard_map/ppermute | solution.py:893
  141.4 10.0 %copy-start.2 = (bf16[32,24,768]{2,1,0:T(8,128)(2,1)S(1)}, bf16[32,24,768]{2,1,0:T(8,128)(2,1)}, u32[]{:S(2)}) copy-start(bf16[32,24,768]{2,1,0:T(8,128)(2,1)} %get-tuple-element.59) | copy-start | bytes 3538948
  141.4 10.0 %copy-start.5 = (bf16[1,128,768]{2,1,0:T(8,128)(2,1)S(1)}, bf16[1,128,768]{2,1,0:T(8,128)(2,1)}, u32[]{:S(2)}) copy-start(bf16[1,128,768]{2,1,0:T(8,128)(2,1)} %param.16) | copy-start | bytes 589828
  151.4 8.3 %slice-start.4 = ((s8[4718592]{0:T(1024)(128)(4,1)}), s8[4194304]{0:T(1024)(128)(4,1)S(1)}, s32[]{:S(2)}) async-start(s8[4718592]{0:T(1024)(128)(4,1)} %bitcast.146), calls=%async_computation.4 | async-start | bytes 8388608
  151.4 14.4 %slice-start = ((s8[7077888]{0:T(1024)(128)(4,1)}), s8[4194304]{0:T(1024)(128)(4,1)S(1)}, s32[]{:S(2)}) async-start(s8[7077888]{0:T(1024)(128)(4,1)} %bitcast.131), calls=%async_computation | async-start | bytes 8388608
  153.1 41.4 %copy-start.18 = (f32[128]{0:T(128)}, f32[128]{0:T(128)S(1)}, u32[]{:S(2)}) copy-start(f32[128]{0:T(128)S(1)} %add_rsqrt_fusion.2) | copy-start | bytes 1540
  153.1 6.6 %slice-start.5 = ((s8[4718592]{0:T(1024)(128)(4,1)}), s8[524288]{0:T(1024)(128)(4,1)S(1)}, s32[]{:S(2)}) async-start(s8[4718592]{0:T(1024)(128)(4,1)} %bitcast.146), calls=%async_computation.5 | async-start | bytes 1048576
  153.2 12.7 %slice-start.1 = ((s8[7077888]{0:T(1024)(128)(4,1)}), s8[2883584]{0:T(1024)(128)(4,1)S(1)}, s32[]{:S(2)}) async-start(s8[7077888]{0:T(1024)(128)(4,1)} %bitcast.131), calls=%async_computation.1 | async-start | bytes 5767168
  162.0 4.3 %collective-permute-start.3 = (bf16[1,1,1536]{2,1,0:T(2,128)(2,1)S(1)}, bf16[1,1,1536]{2,1,0:T(2,128)(2,1)S(1)}, u32[]{:S(2)}, u32[]{:S(2)}) collective-permute-start(bf16[1,1,1536]{2,1,0:T(2,128)(2,1)S(1)} %get-tuple-element.130), channel_id=1, source_target_pairs={{0,1},{1,2},{2,3},{4,5},{5,6},{6,7},{8,9},{9,10},{10,11},{12,13},{... | collective-permute-start | bytes 9224 | tf_op jit(solution)/shard_map/ppermute | solution.py:572
  164.5 3.1 collective-permute-start.4
  170.2 11.9 %collective-permute-start.6 = (bf16[1,1,768]{2,1,0:T(2,128)(2,1)S(1)}, bf16[1,1,768]{2,1,0:T(2,128)(2,1)S(1)}, u32[]{:S(2)}, u32[]{:S(2)}) collective-permute-start(bf16[1,1,768]{2,1,0:T(2,128)(2,1)S(1)} %get-tuple-element.135), channel_id=1, source_target_pairs={{0,1},{1,2},{2,3},{4,5},{5,6},{6,7},{8,9},{9,10},{10,11},{12,13},{... | collective-permute-start | bytes 4616 | tf_op jit(solution)/shard_map/ppermute | solution.py:572
  179.9 3.2 collective-permute-start.5
  185.7 6.4 %slice-start.2 = ((s8[4718592]{0:T(1024)(128)(4,1)}), s8[4194304]{0:T(1024)(128)(4,1)S(1)}, s32[]{:S(2)}) async-start(s8[4718592]{0:T(1024)(128)(4,1)} %bitcast.143), calls=%async_computation.2 | async-start | bytes 8388608
  186.6 5.5 %slice-start.3 = ((s8[4718592]{0:T(1024)(128)(4,1)}), s8[524288]{0:T(1024)(128)(4,1)S(1)}, s32[]{:S(2)}) async-start(s8[4718592]{0:T(1024)(128)(4,1)} %bitcast.143), calls=%async_computation.3 | async-start | bytes 1048576
  206.8 44.7 %collective-permute-start.9 = (bf16[128,1536]{1,0:T(8,128)(2,1)}, bf16[128,1536]{1,0:T(8,128)(2,1)S(1)}, u32[]{:S(2)}, u32[]{:S(2)}) collective-permute-start(bf16[128,1536]{1,0:T(8,128)(2,1)} %get-tuple-element.73), channel_id=1, source_target_pairs={{0,3},{1,0},{2,1},{3,2},{4,7},{5,4},{6,5},{7,6},{8,11},{9,8},{10,9... | collective-permute-start | bytes 1179656 | tf_op jit(solution)/shard_map/ppermute | solution.py:898
  207.5 44.1 %collective-permute-start.8 = (bf16[128,1536]{1,0:T(8,128)(2,1)}, bf16[128,1536]{1,0:T(8,128)(2,1)}, u32[]{:S(2)}, u32[]{:S(2)}) collective-permute-start(bf16[128,1536]{1,0:T(8,128)(2,1)} %get-tuple-element.72), channel_id=1, source_target_pairs={{0,2},{1,3},{2,0},{3,1},{4,6},{5,7},{6,4},{7,5},{8,10},{9,11},{10,... | collective-permute-start | bytes 1179656 | tf_op jit(solution)/shard_map/ppermute | solution.py:898
  210.2 41.3 %collective-permute-start.7 = (bf16[128,1536]{1,0:T(8,128)(2,1)}, bf16[128,1536]{1,0:T(8,128)(2,1)}, u32[]{:S(2)}, u32[]{:S(2)}) collective-permute-start(bf16[128,1536]{1,0:T(8,128)(2,1)} %get-tuple-element.71), channel_id=1, source_target_pairs={{0,1},{1,2},{2,3},{3,0},{4,5},{5,6},{6,7},{7,4},{8,9},{9,10},{10,1... | collective-permute-start | bytes 1179656 | tf_op jit(solution)/shard_map/ppermute | solution.py:898
  210.4 34.4 %copy-start.12 = (bf16[128,768]{1,0:T(8,128)(2,1)S(1)}, bf16[128,768]{1,0:T(8,128)(2,1)}, u32[]{:S(2)}) copy-start(bf16[128,768]{1,0:T(8,128)(2,1)} %get-tuple-element.66) | copy-start | bytes 589828
  244.7 2.3 copy-start.4
  244.8 2.3 copy-start.17
  244.8 2.3 copy-start.16
  244.8 2.3 copy-start.20
  244.8 2.3 copy-start.21
  244.8 3.0 copy-start.19
  247.8 3.8 copy-start.14
  247.8 5.1 %copy-start = (bf16[32,24,2304]{2,1,0:T(8,128)(2,1)S(1)}, bf16[32,24,2304]{2,1,0:T(8,128)(2,1)}, u32[]{:S(2)}) copy-start(bf16[32,24,2304]{2,1,0:T(8,128)(2,1)} %get-tuple-element.58) | copy-start | bytes 10616836
  (7 other events, 10.0 us)

commit v7 on v6

--- a/solution.py
+++ b/solution.py
@@ -457,7 +457,8 @@
 
 
 LANES = 128
-AHEAD = 2
+AHEAD = 3
+ROUNDS = (0, 2, 4, 6, 8, 10, 12)
 
 
 def window_start(unit, width, features):
@@ -514,17 +515,18 @@
         job.begin()
     stages = [job.stages() for job in jobs]
     depth = len(stages[0])
-    for t in range(total + depth - 1):
+    for t in range(total + ROUNDS[depth - 1]):
         if t + AHEAD < total:
             jobs[t + AHEAD].begin()
         for k in range(depth):
-            if 0 <= t - k < total:
-                stages[t - k][k](jobs[t - k])
+            j = t - ROUNDS[k]
+            if 0 <= j < total:
+                stages[j][k](jobs[j])
     for job in jobs:
         job.drain()
 
 
-def scatter_all(dp_size, parts, norm_rows, width, late, cap=36864, cid=2):
+def scatter_all(dp_size, parts, norm_rows, width, late, cap=18432, cid=2):
     count = len(parts) + 1
     n = dp_size // 2
     outs = [jax.ShapeDtypeStruct(x.shape[1:], jnp.float32) for x in parts]
@@ -707,7 +709,7 @@
     )(ids, table, w_in, w_rec)
 
 
-def gru_back_step(d, slot, factor, keep, w_rec, grad, seeds):
+def gru_back_step(d, slot, factor, keep, flipped, grad, seeds):
     units = grad.shape[2]
     g = grad[d]
     part = lambda k: factor[:, k * units : (k + 1) * units].astype(jnp.float32)
@@ -716,7 +718,7 @@
     seeds[d, slot, :, units : 2 * units] = (g * part(1)).astype(seeds.dtype)
     seeds[d, slot, :, 2 * units : 3 * units] = (by_cand * part(3)).astype(seeds.dtype)
     seeds[d, slot, :, 3 * units :] = by_cand.astype(seeds.dtype)
-    grad[d] = g * keep[...] + back_dot(seeds[d, slot, :, : 3 * units], w_rec[d])
+    grad[d] = g * keep[...] + plain_dot(seeds[d, slot, :, : 3 * units], flipped[d])
 
 
 def gru_weight_grads(d, seeds, emb, prior, d_in, d_rec):
@@ -724,11 +726,10 @@
     units = wide // 4
     states = prior[...].reshape(nchar * rows, units)
     chars = emb[...].reshape(nchar * rows, -1)
-    col = lambda k: seeds[d, :, :, k * units : (k + 1) * units].reshape(nchar * rows, units)
-    for k in range(3):
-        d_rec[d, :, k * units : (k + 1) * units] = grad_dot(states, col(k)).astype(d_rec.dtype)
-        own = col(3 if k == 2 else k)
-        d_in[d, :, k * units : (k + 1) * units] = grad_dot(chars, own).astype(d_in.dtype)
+    col = lambda k, n: seeds[d, :, :, k * units : (k + n) * units].reshape(nchar * rows, n * units)
+    d_rec[d] = grad_dot(states, col(0, 3)).astype(d_rec.dtype)
+    d_in[d, :, : 2 * units] = grad_dot(chars, col(0, 2)).astype(d_in.dtype)
+    d_in[d, :, 2 * units :] = grad_dot(chars, col(3, 1)).astype(d_in.dtype)
 
 
 def gru_char_grads(ids_ref, seeds, w_in, d_table, chunk=4):
@@ -748,7 +749,7 @@
     d_table[...] = total
 
 
-def gru_backward_kernel(ids_ref, seed, w_in, w_rec, emb, h0, h1, f0, f1, z0, z1, d_in, d_rec, d_table, grad, seeds):
+def gru_backward_kernel(ids_ref, seed, w_in, w_rec, emb, h0, h1, f0, f1, z0, z1, d_in, d_rec, d_table, grad, seeds, flipped):
     i = pl.program_id(0)
     nchar = pl.num_programs(0)
 
@@ -757,9 +758,11 @@
         units = grad.shape[2]
         grad[0] = seed[:, :units]
         grad[1] = seed[:, units:]
-
-    gru_back_step(0, nchar - 1 - i, f0.at[0], z0.at[0], w_rec, grad, seeds)
-    gru_back_step(1, i, f1.at[0], z1.at[0], w_rec, grad, seeds)
+        for d in range(2):
+            flipped[d] = w_rec[d].T
+
+    gru_back_step(0, nchar - 1 - i, f0.at[0], z0.at[0], flipped, grad, seeds)
+    gru_back_step(1, i, f1.at[0], z1.at[0], flipped, grad, seeds)
 
     @pl.when(i == nchar - 1)
     def _():
@@ -787,6 +790,7 @@
         scratch_shapes=[
             pltpu.VMEM((2, rows, units), jnp.float32),
             pltpu.VMEM((2, nchar, rows, 4 * units), jnp.bfloat16),
+            pltpu.VMEM((2, 3 * units, units), jnp.bfloat16),
         ],
         compiler_params=pltpu.CompilerParams(vmem_limit_bytes=60000000),
         cost_estimate=gru_cost(nchar, rows, width, units, 2),
@@ -1048,7 +1052,7 @@
     terms = [input_mats, recur_sum, merge_grad, conv_grad, down_grad, up_grad, qkv_grad, out_grad, table_grad]
     parts = [x.astype(jnp.bfloat16).reshape(devices, -1, x.shape[-1]) for x in terms]
     width = norm_gain.shape[1]
-    *sums, norm_sum = scatter_all(dp_size, parts, norm_grads, width, (1, 3))
+    *sums, norm_sum = scatter_all(dp_size, parts, norm_grads, width, (3, 6))
     input_total, recur_total, merge_sum, conv_sum, down_sum, up_sum, qkv_sum, out_sum, table_sum = settle(sums)
     skip = me * width - window_start(me, width, features)
     gain_sum = lax.dynamic_slice(norm_sum, (0, skip), (3, width))

time: 402 us -> 400 us (level); the launches traced: 396 us -> 399 us
  starting transfers between devices: 15.1 us -> 25.6 us
  Pallas kernels: 317 us -> 309 us
    ppermute x3, starting transfers between devices: 2.22 us -> 12.6 us  [from_next(): return lax.ppermute(x, axis, [((i + step) % size, i) for i in range(size)])]
    pallas_call x1, Pallas kernels: 134 us -> 129 us  [scatter_all(): pl.pallas_call(functools.partial(scatter_kernel, dp_size, chunks, count,...]
  transfers between devices with their start and end apart: 10 -> 10, of which waited for: 1 -> 2; matrix products, arithmetic and copies ran while one was open for 5% -> 5% of each run, Pallas kernels for 14% -> 13%
where the time goes in v7:
time: 400 us; the launch traced here: 399 us
  Pallas kernels  309 us (77%)
  matrix products  44.6 us (11%)
  starting transfers between devices  25.6 us (6%)
  local copies, waits for them, and re-layouts  9.08 us (2%)
  other arithmetic  6.28 us (2%)
    pallas_call x1, Pallas kernels, scatter_all(): pl.pallas_call(functools.partial(scatter_kernel, dp_size, chunks, count,...  129 us
    pallas_call x1, Pallas kernels, gather_all(): pl.pallas_call(functools.partial(gather_kernel, dp_size, count, early), o...  110 us
    pallas_call x1, Pallas kernels, gru_backward(): pl.pallas_call(gru_backward_kernel, grid=(nchar,), out_shape=[shape(w_in....  31.2 us
    pallas_call x1, Pallas kernels, gru_forward(): pl.pallas_call(gru_forward_kernel, grid=(nchar,), out_shape=[shape((rows,...  20.9 us
    dot_general x5, matrix products, grad_dot(): lax.dot_general(left, right, (((0,), (0,)), ((), ())), preferred_element_...  16.7 us
    dot_general x8, matrix products, plain_dot(): return jnp.dot(left, right, preferred_element_type=jnp.float32)  14.2 us
    ppermute x3, starting transfers between devices, from_next(): return lax.ppermute(x, axis, [((i + step) % size, i) for i in range(size)])  12.6 us
    dot_general x7, matrix products, back_dot(): lax.dot_general(left, right, (((1,), (1,)), ((), ())), preferred_element_...  10.1 us
  transfers between devices with their start and end apart: 10, of which 2 were waited for; matrix products, arithmetic and copies ran while one was open for 5% of the time, Pallas kernels for 13%

profile of v7, /device:TPU:0, one launch (start us, length us, event | category | flops | bytes accessed | tf_op | source)
XLA Modules:
  0.0 399.0 jit_solution(658278587071487751)
XLA Ops:
  2.2 110.2 %shard_map.255 = (bf16[32,32,256]{2,1,0:T(8,128)(2,1)}, bf16[32,16,1152]{2,1,0:T(8,128)(2,1)}, bf16[32,24,1152]{2,1,0:T(8,128)(2,1)}, bf16[32,8,768]{2,1,0:T(8,1...) custom-call(bf16[32,256]{1,0:T(8,128)(2,1)} %refs_0_.1, ...), custom_call_target="tpu_custom_call" | custom-call | tf_op jit(solution)/shard_map/pallas_call | solution.py:248
  112.4 2.8 fusion
  115.8 1.5 collective-permute-start.1
  117.3 10.5 %collective-permute-start.2 = (bf16[128,1536]{1,0:T(8,128)(2,1)S(1)}, bf16[128,1536]{1,0:T(8,128)(2,1)}, u32[]{:S(2)}, u32[]{:S(2)}) collective-permute-start(bf16[128,1536]{1,0:T(8,128)(2,1)S(1)} %slice.108.refs_0_), channel_id=1, source_target_pairs={{3,0},{0,1},{1,2},{2,3},{7,4},{4,5},{5,6},{6,7},{11,8},{8,9},{9,10... | collective-permute-start | bytes 1179656 | tf_op jit(solution)/shard_map/ppermute | solution.py:897
  129.4 1.5 constant_dynamic-slice_fusion.1.table
  130.9 20.9 %shard_map.257 = (bf16[128,768]{1,0:T(8,128)(2,1)}, bf16[16,128,256]{2,1,0:T(8,128)(2,1)}, bf16[16,128,1536]{2,1,0:T(8,128)(2,1)}, bf16[16,128,1536]{2,1,0:T(8,1...) custom-call(s32[128,16]{1,0:T(8,128)} %bitcast.159, ...), custom_call_target="tpu_custom_call" | custom-call | flops 12079595520 | bytes 25165824 | tf_op jit(solution)/shard_map/pallas_call | solution.py:692
  155.4 6.4 %shard_map.256 = bf16[128,768]{1,0:T(8,128)(2,1)} custom-call(bf16[128,768]{1,0:T(8,128)(2,1)} %slice.107.q_ref, s32[1,512]{1,0:T(1,128)} %bitcast.161, bf16[128,1536]{1,0:T(8,128)(2,1)} %copy-done.3, bf16[128,1536]{1,0:T(8,128)(2,1)} %copy-done.8, bf16[128,1536]{1,0:T(8,128)(2,1)} %copy-done.9, bf16[128,1536]{1,0:T(8,128)(2,1)} %collective-permute-done.2.refs_3_), custom_call_target="tpu_custom_call" | custom-call | flops 201326592 | bytes 3145728 | tf_op jit(solution)/shard_map/pallas_call | solution.py:873
  161.8 1.5 fusion.83
  163.6 6.5 %multiply_convert_fusion = (bf16[128,3072]{1,0:T(8,128)(2,1)S(1)}, f32[128,3072]{1,0:T(8,128)S(1)}, f32[128,3072]{1,0:T(8,128)S(1)}) fusion(bf16[768,3072]{1,0:T(8,128)(2,1)} %bitcast.142, f32[128,768]{1,0:T(8,128)S(1)} %get-tuple-element.139, f32[768]{0:T(1024)S(1)} %get-tuple-element.118, f32[768]{0:T(1024)S(1)} %get-tuple-element.119, ...), kind=kOutput, calls=%fused_computation.21 | convolution fusion | flops 630030336 | bytes 9051136 | tf_op jit(solution)/shard_map/dot_general | solution.py:591
  170.1 0.9 fusion.84
  172.4 2.5 collective-permute-start.3
  174.9 1.3 collective-permute-start.4
  176.7 1.2 collective-permute-done.4
  180.6 3.8 collective-permute-start.6
  184.4 4.9 %convolution_convert_fusion = bf16[4608,768]{1,0:T(8,128)(2,1)} fusion(bf16[128,1536]{1,0:T(8,128)(2,1)S(1)} %get-tuple-element.129, bf16[128,768]{1,0:T(8,128)(2,1)S(1)} %bitcast.153, bf16[128,768]{1,0:T(8,128)(2,1)S(1)} %bitcast.151, bf16[128,1536]{1,0:T(8,128)(2,1)S(1)} %get-tuple-element.128, f32[128,768]{1,0:T(8,128)S(1)} %get-tuple-element.122), kind=kOutput, calls=%fused_computation | convolution fusion | flops 914325504 | bytes 8650752 | tf_op jit(solution)/shard_map/dot_general | solution.py:595
  190.3 1.5 collective-permute-start.5
  196.9 3.6 convolution_convert_fusion.3
  200.5 1.9 add_convert_fusion
  202.4 2.4 multiply_reduce_fusion.1
  205.0 1.2 convolution_convert_fusion.7.seed_ref
  206.2 1.5 convolution_convert_fusion.6
  207.7 9.4 %shard_map.258 = (bf16[128,768]{1,0:T(8,128)(2,1)}, bf16[128,1536]{1,0:T(8,128)(2,1)}, bf16[128,1536]{1,0:T(8,128)(2,1)}, bf16[128,1536]{1,0:T(8,128)(2,1)}, bf16[128,1536]{1,0:T(8,128)(2,1)}) custom-call(bf16[128,768]{1,0:T(8,128)(2,1)} %slice.107.q_ref, s32[1,512]{1,0:T(1,128)} %bitcast.162, bf16[128,768]{1,0:T(8,128)(2,1)} %convolution_convert_fusion.7.seed_ref, ...), custom_call_target="tpu_custom_call" | custom-call | flops 503316480 | bytes 3145728 | tf_op jit(solution)/shard_map/pallas_call | solution.py:885
  217.6 2.9 collective-permute-start.8
  221.0 31.2 %shard_map.259 = (bf16[2,256,1152]{2,1,0:T(8,128)(2,1)}, bf16[2,384,1152]{2,1,0:T(8,128)(2,1)}, f32[128,256]{1,0:T(8,128)}) custom-call(s32[128,16]{1,0:T(8,128)} %bitcast.160, f32[128,768]{1,0:T(8,128)} %slice_bitcast_fusion.15.seed, bf16[2,256,1152]{2,1,0:T(8,128)(2,1)} %bitcast.167, bf16[2,384,1152]{2,1,0:T(8,128)(2,1)} %bitcast.165, ...), custom_call_target="tpu_custom_call" | custom-call | flops 24159191040 | bytes 25165824 | tf_op jit(solution)/shard_map/pallas_call | solution.py:780
  253.2 2.2 convolution_convert_fusion.5
  256.2 3.7 convolution_convert_fusion.2
  260.0 1.4 add_convert_fusion.1
  261.4 2.0 fusion.25
  263.3 3.0 convolution_convert_fusion.1
  266.3 128.5 %shard_map.260 = (f32[16,1152]{1,0:T(8,128)}, f32[24,1152]{1,0:T(8,128)}, f32[48,768]{1,0:T(8,128)}, f32[144,768]{1,0:T(8,128)}, f32[96,768]{1,0:T(8,128)}, /*in...) custom-call(bf16[32,16,1152]{2,1,0:T(8,128)(2,1)} %bitcast.156, ...), custom_call_target="tpu_custom_call" | custom-call | tf_op jit(solution)/shard_map/pallas_call | solution.py:541
  394.8 1.4 constant_dynamic-slice_fusion.2
  396.3 2.6 shard_map.261
  (128 shorter events, 19.2 us)
Async XLA Ops:
  112.4 15.5 %copy-start.22 = (s32[1,128,16]{1,2,0:T(8,128)S(1)}, s32[1,128,16]{1,2,0:T(8,128)}, u32[]{:S(2)}) copy-start(s32[1,128,16]{1,2,0:T(8,128)} %param.17) | copy-start | bytes 24580
  112.4 16.9 %copy-start.13 = (bf16[32,8,768]{2,1,0:T(8,128)(2,1)S(1)}, bf16[32,8,768]{2,1,0:T(8,128)(2,1)}, u32[]{:S(2)}) copy-start(bf16[32,8,768]{2,1,0:T(8,128)(2,1)} %get-tuple-element.60) | copy-start | bytes 1179652
  112.4 16.9 %copy-start.7 = (bf16[1,128,768]{2,1,0:T(8,128)(2,1)S(1)}, bf16[1,128,768]{2,1,0:T(8,128)(2,1)}, u32[]{:S(2)}) copy-start(bf16[1,128,768]{2,1,0:T(8,128)(2,1)} %param.20) | copy-start | bytes 589828
  115.3 36.5 %copy-start.3 = (bf16[128,1536]{1,0:T(8,128)(2,1)}, bf16[128,1536]{1,0:T(8,128)(2,1)S(1)}, u32[]{:S(2)}) copy-start(bf16[128,1536]{1,0:T(8,128)(2,1)S(1)} %slice.108.refs_0_) | copy-start | bytes 1179652
  115.3 39.2 %collective-permute-start = (bf16[128,1536]{1,0:T(8,128)(2,1)S(1)}, bf16[128,1536]{1,0:T(8,128)(2,1)S(1)}, u32[]{:S(2)}, u32[]{:S(2)}) collective-permute-start(bf16[128,1536]{1,0:T(8,128)(2,1)S(1)} %slice.108.refs_0_), channel_id=1, source_target_pairs={{1,0},{2,1},{3,2},{0,3},{5,4},{6,5},{7,6},{4,7},{9,8},{10,9},{11,1... | collective-permute-start | bytes 1179656 | tf_op jit(solution)/shard_map/ppermute | solution.py:897
  115.8 38.7 %collective-permute-start.1 = (bf16[128,1536]{1,0:T(8,128)(2,1)S(1)}, bf16[128,1536]{1,0:T(8,128)(2,1)S(1)}, u32[]{:S(2)}, u32[]{:S(2)}) collective-permute-start(bf16[128,1536]{1,0:T(8,128)(2,1)S(1)} %slice.108.refs_0_), channel_id=1, source_target_pairs={{2,0},{3,1},{0,2},{1,3},{6,4},{7,5},{4,6},{5,7},{10,8},{11,9},{8,1... | collective-permute-start | bytes 1179656 | tf_op jit(solution)/shard_map/ppermute | solution.py:897
  117.3 37.2 %collective-permute-start.2 = (bf16[128,1536]{1,0:T(8,128)(2,1)S(1)}, bf16[128,1536]{1,0:T(8,128)(2,1)}, u32[]{:S(2)}, u32[]{:S(2)}) collective-permute-start(bf16[128,1536]{1,0:T(8,128)(2,1)S(1)} %slice.108.refs_0_), channel_id=1, source_target_pairs={{3,0},{0,1},{1,2},{2,3},{7,4},{4,5},{5,6},{6,7},{11,8},{8,9},{9,10... | collective-permute-start | bytes 1179656 | tf_op jit(solution)/shard_map/ppermute | solution.py:897
  151.8 10.0 %copy-start.2 = (bf16[32,24,768]{2,1,0:T(8,128)(2,1)S(1)}, bf16[32,24,768]{2,1,0:T(8,128)(2,1)}, u32[]{:S(2)}) copy-start(bf16[32,24,768]{2,1,0:T(8,128)(2,1)} %get-tuple-element.59) | copy-start | bytes 3538948
  151.8 10.0 %copy-start.5 = (bf16[1,128,768]{2,1,0:T(8,128)(2,1)S(1)}, bf16[1,128,768]{2,1,0:T(8,128)(2,1)}, u32[]{:S(2)}) copy-start(bf16[1,128,768]{2,1,0:T(8,128)(2,1)} %param.16) | copy-start | bytes 589828
  161.8 8.3 %slice-start.4 = ((s8[4718592]{0:T(1024)(128)(4,1)}), s8[4194304]{0:T(1024)(128)(4,1)S(1)}, s32[]{:S(2)}) async-start(s8[4718592]{0:T(1024)(128)(4,1)} %bitcast.146), calls=%async_computation.4 | async-start | bytes 8388608
  161.8 14.4 %slice-start = ((s8[7077888]{0:T(1024)(128)(4,1)}), s8[4194304]{0:T(1024)(128)(4,1)S(1)}, s32[]{:S(2)}) async-start(s8[7077888]{0:T(1024)(128)(4,1)} %bitcast.131), calls=%async_computation | async-start | bytes 8388608
  163.5 41.3 %copy-start.18 = (f32[128]{0:T(128)}, f32[128]{0:T(128)S(1)}, u32[]{:S(2)}) copy-start(f32[128]{0:T(128)S(1)} %add_rsqrt_fusion.2) | copy-start | bytes 1540
  163.5 6.6 %slice-start.5 = ((s8[4718592]{0:T(1024)(128)(4,1)}), s8[524288]{0:T(1024)(128)(4,1)S(1)}, s32[]{:S(2)}) async-start(s8[4718592]{0:T(1024)(128)(4,1)} %bitcast.146), calls=%async_computation.5 | async-start | bytes 1048576
  163.5 12.7 %slice-start.1 = ((s8[7077888]{0:T(1024)(128)(4,1)}), s8[2883584]{0:T(1024)(128)(4,1)S(1)}, s32[]{:S(2)}) async-start(s8[7077888]{0:T(1024)(128)(4,1)} %bitcast.131), calls=%async_computation.1 | async-start | bytes 5767168
  172.4 4.3 %collective-permute-start.3 = (bf16[1,1,1536]{2,1,0:T(2,128)(2,1)S(1)}, bf16[1,1,1536]{2,1,0:T(2,128)(2,1)S(1)}, u32[]{:S(2)}, u32[]{:S(2)}) collective-permute-start(bf16[1,1,1536]{2,1,0:T(2,128)(2,1)S(1)} %get-tuple-element.130), channel_id=1, source_target_pairs={{0,1},{1,2},{2,3},{4,5},{5,6},{6,7},{8,9},{9,10},{10,11},{12,13},{... | collective-permute-start | bytes 9224 | tf_op jit(solution)/shard_map/ppermute | solution.py:574
  174.9 3.1 collective-permute-start.4
  180.6 11.8 %collective-permute-start.6 = (bf16[1,1,768]{2,1,0:T(2,128)(2,1)S(1)}, bf16[1,1,768]{2,1,0:T(2,128)(2,1)S(1)}, u32[]{:S(2)}, u32[]{:S(2)}) collective-permute-start(bf16[1,1,768]{2,1,0:T(2,128)(2,1)S(1)} %get-tuple-element.135), channel_id=1, source_target_pairs={{0,1},{1,2},{2,3},{4,5},{5,6},{6,7},{8,9},{9,10},{10,11},{12,13},{... | collective-permute-start | bytes 4616 | tf_op jit(solution)/shard_map/ppermute | solution.py:574
  190.3 3.1 collective-permute-start.5
  195.9 6.4 %slice-start.2 = ((s8[4718592]{0:T(1024)(128)(4,1)}), s8[4194304]{0:T(1024)(128)(4,1)S(1)}, s32[]{:S(2)}) async-start(s8[4718592]{0:T(1024)(128)(4,1)} %bitcast.143), calls=%async_computation.2 | async-start | bytes 8388608
  196.9 5.5 %slice-start.3 = ((s8[4718592]{0:T(1024)(128)(4,1)}), s8[524288]{0:T(1024)(128)(4,1)S(1)}, s32[]{:S(2)}) async-start(s8[4718592]{0:T(1024)(128)(4,1)} %bitcast.143), calls=%async_computation.3 | async-start | bytes 1048576
  217.0 42.9 %collective-permute-start.9 = (bf16[128,1536]{1,0:T(8,128)(2,1)}, bf16[128,1536]{1,0:T(8,128)(2,1)S(1)}, u32[]{:S(2)}, u32[]{:S(2)}) collective-permute-start(bf16[128,1536]{1,0:T(8,128)(2,1)} %get-tuple-element.73), channel_id=1, source_target_pairs={{0,3},{1,0},{2,1},{3,2},{4,7},{5,4},{6,5},{7,6},{8,11},{9,8},{10,9... | collective-permute-start | bytes 1179656 | tf_op jit(solution)/shard_map/ppermute | solution.py:902
  217.6 42.3 %collective-permute-start.8 = (bf16[128,1536]{1,0:T(8,128)(2,1)}, bf16[128,1536]{1,0:T(8,128)(2,1)}, u32[]{:S(2)}, u32[]{:S(2)}) collective-permute-start(bf16[128,1536]{1,0:T(8,128)(2,1)} %get-tuple-element.72), channel_id=1, source_target_pairs={{0,2},{1,3},{2,0},{3,1},{4,6},{5,7},{6,4},{7,5},{8,10},{9,11},{10,... | collective-permute-start | bytes 1179656 | tf_op jit(solution)/shard_map/ppermute | solution.py:902
  220.6 39.4 %collective-permute-start.7 = (bf16[128,1536]{1,0:T(8,128)(2,1)}, bf16[128,1536]{1,0:T(8,128)(2,1)}, u32[]{:S(2)}, u32[]{:S(2)}) collective-permute-start(bf16[128,1536]{1,0:T(8,128)(2,1)} %get-tuple-element.71), channel_id=1, source_target_pairs={{0,1},{1,2},{2,3},{3,0},{4,5},{5,6},{6,7},{7,4},{8,9},{9,10},{10,1... | collective-permute-start | bytes 1179656 | tf_op jit(solution)/shard_map/ppermute | solution.py:902
  221.0 32.2 %copy-start.12 = (bf16[128,768]{1,0:T(8,128)(2,1)S(1)}, bf16[128,768]{1,0:T(8,128)(2,1)}, u32[]{:S(2)}) copy-start(bf16[128,768]{1,0:T(8,128)(2,1)} %get-tuple-element.66) | copy-start | bytes 589828
  253.2 2.3 copy-start.4
  253.2 2.3 copy-start.17
  253.2 2.3 copy-start.16
  253.2 2.3 copy-start.20
  253.2 2.3 copy-start.21
  253.2 3.0 copy-start.19
  256.2 3.8 copy-start.14
  256.2 5.1 %copy-start = (bf16[32,24,2304]{2,1,0:T(8,128)(2,1)S(1)}, bf16[32,24,2304]{2,1,0:T(8,128)(2,1)}, u32[]{:S(2)}) copy-start(bf16[32,24,2304]{2,1,0:T(8,128)(2,1)} %get-tuple-element.58) | copy-start | bytes 10616836
  (7 other events, 10.0 us)

commit v8 on v7

--- a/solution.py
+++ b/solution.py
@@ -944,7 +944,7 @@
     me = lax.axis_index("dp") * lax.axis_size("seq") + lax.axis_index("seq")
     norms = place_norms(norm_gain, norm_bias, me, devices)
     order = (char_table, gru_input, gru_recur, norms, qkv_weight, out_weight, up_weight, down_weight, merge_weight, conv_weight)
-    gathered = gather_all(dp_size, devices, order, (2, 9))
+    gathered = gather_all(dp_size, devices, order, (6, 9))
     all_norms = jnp.sum(gathered[3].astype(jnp.float32), axis=0)
     (full_table, full_input, full_recur, _, full_qkv, full_out, full_up, full_down, full_merge, full_conv) = [
         x.reshape(-1, x.shape[2]) for x in gathered

time: 400 us -> 394 us (0.985)
  Pallas kernels: 309 us -> 303 us
    pallas_call x1, Pallas kernels: 110 us -> 105 us  [gather_all(): pl.pallas_call(functools.partial(gather_kernel, dp_size, count, early), o...]
where the time goes in v8:
time: 394 us; the launch traced here: 393 us
  Pallas kernels  303 us (77%)
  matrix products  44.6 us (11%)
  starting transfers between devices  26.1 us (7%)
  local copies, waits for them, and re-layouts  9.08 us (2%)
  other arithmetic  6.28 us (2%)
    pallas_call x1, Pallas kernels, scatter_all(): pl.pallas_call(functools.partial(scatter_kernel, dp_size, chunks, count,...  128 us
    pallas_call x1, Pallas kernels, gather_all(): pl.pallas_call(functools.partial(gather_kernel, dp_size, count, early), o...  105 us
    pallas_call x1, Pallas kernels, gru_backward(): pl.pallas_call(gru_backward_kernel, grid=(nchar,), out_shape=[shape(w_in....  31.2 us
    pallas_call x1, Pallas kernels, gru_forward(): pl.pallas_call(gru_forward_kernel, grid=(nchar,), out_shape=[shape((rows,...  20.9 us
    dot_general x5, matrix products, grad_dot(): lax.dot_general(left, right, (((0,), (0,)), ((), ())), preferred_element_...  16.7 us
    dot_general x8, matrix products, plain_dot(): return jnp.dot(left, right, preferred_element_type=jnp.float32)  14.2 us
    ppermute x3, starting transfers between devices, from_next(): return lax.ppermute(x, axis, [((i + step) % size, i) for i in range(size)])  12.6 us
    dot_general x7, matrix products, back_dot(): lax.dot_general(left, right, (((1,), (1,)), ((), ())), preferred_element_...  10.1 us
  transfers between devices with their start and end apart: 10, of which 2 were waited for; matrix products, arithmetic and copies ran while one was open for 5% of the time, Pallas kernels for 13%

profile of v8, /device:TPU:0, one launch (start us, length us, event | category | flops | bytes accessed | tf_op | source)
XLA Modules:
  0.0 393.4 jit_solution(10592393157179651290)
XLA Ops:
  2.2 104.8 %shard_map.255 = (bf16[32,32,256]{2,1,0:T(8,128)(2,1)}, bf16[32,16,1152]{2,1,0:T(8,128)(2,1)}, bf16[32,24,1152]{2,1,0:T(8,128)(2,1)}, bf16[32,8,768]{2,1,0:T(8,1...) custom-call(bf16[32,256]{1,0:T(8,128)(2,1)} %refs_0_.1, ...), custom_call_target="tpu_custom_call" | custom-call | tf_op jit(solution)/shard_map/pallas_call | solution.py:248
  107.0 2.8 fusion
  109.9 1.0 collective-permute-start
  110.9 1.0 collective-permute-start.1
  111.9 10.5 %collective-permute-start.2 = (bf16[128,1536]{1,0:T(8,128)(2,1)S(1)}, bf16[128,1536]{1,0:T(8,128)(2,1)}, u32[]{:S(2)}, u32[]{:S(2)}) collective-permute-start(bf16[128,1536]{1,0:T(8,128)(2,1)S(1)} %slice.108.refs_0_), channel_id=1, source_target_pairs={{3,0},{0,1},{1,2},{2,3},{7,4},{4,5},{5,6},{6,7},{11,8},{8,9},{9,10... | collective-permute-start | bytes 1179656 | tf_op jit(solution)/shard_map/ppermute | solution.py:897
  124.0 1.5 constant_dynamic-slice_fusion.1.table
  125.4 20.9 %shard_map.257 = (bf16[128,768]{1,0:T(8,128)(2,1)}, bf16[16,128,256]{2,1,0:T(8,128)(2,1)}, bf16[16,128,1536]{2,1,0:T(8,128)(2,1)}, bf16[16,128,1536]{2,1,0:T(8,1...) custom-call(s32[128,16]{1,0:T(8,128)} %bitcast.159, ...), custom_call_target="tpu_custom_call" | custom-call | flops 12079595520 | bytes 25165824 | tf_op jit(solution)/shard_map/pallas_call | solution.py:692
  150.0 6.4 %shard_map.256 = bf16[128,768]{1,0:T(8,128)(2,1)} custom-call(bf16[128,768]{1,0:T(8,128)(2,1)} %slice.107.q_ref, s32[1,512]{1,0:T(1,128)} %bitcast.161, bf16[128,1536]{1,0:T(8,128)(2,1)} %copy-done.3, bf16[128,1536]{1,0:T(8,128)(2,1)} %copy-done.8, bf16[128,1536]{1,0:T(8,128)(2,1)} %copy-done.9, bf16[128,1536]{1,0:T(8,128)(2,1)} %collective-permute-done.2.refs_3_), custom_call_target="tpu_custom_call" | custom-call | flops 201326592 | bytes 3145728 | tf_op jit(solution)/shard_map/pallas_call | solution.py:873
  156.4 1.5 fusion.83
  158.1 6.5 %multiply_convert_fusion = (bf16[128,3072]{1,0:T(8,128)(2,1)S(1)}, f32[128,3072]{1,0:T(8,128)S(1)}, f32[128,3072]{1,0:T(8,128)S(1)}) fusion(bf16[768,3072]{1,0:T(8,128)(2,1)} %bitcast.142, f32[128,768]{1,0:T(8,128)S(1)} %get-tuple-element.139, f32[768]{0:T(1024)S(1)} %get-tuple-element.118, f32[768]{0:T(1024)S(1)} %get-tuple-element.119, ...), kind=kOutput, calls=%fused_computation.21 | convolution fusion | flops 630030336 | bytes 9051136 | tf_op jit(solution)/shard_map/dot_general | solution.py:591
  167.0 3.0 collective-permute-start.3
  170.0 1.3 collective-permute-start.4
  171.8 1.2 collective-permute-done.4
  175.7 3.8 collective-permute-start.6
  179.5 4.9 %convolution_convert_fusion = bf16[4608,768]{1,0:T(8,128)(2,1)} fusion(bf16[128,1536]{1,0:T(8,128)(2,1)S(1)} %get-tuple-element.129, bf16[128,768]{1,0:T(8,128)(2,1)S(1)} %bitcast.153, bf16[128,768]{1,0:T(8,128)(2,1)S(1)} %bitcast.151, bf16[128,1536]{1,0:T(8,128)(2,1)S(1)} %get-tuple-element.128, f32[128,768]{1,0:T(8,128)S(1)} %get-tuple-element.122), kind=kOutput, calls=%fused_computation | convolution fusion | flops 914325504 | bytes 8650752 | tf_op jit(solution)/shard_map/dot_general | solution.py:595
  185.3 1.5 collective-permute-start.5
  192.0 3.6 convolution_convert_fusion.3
  195.6 1.9 add_convert_fusion
  197.5 2.4 multiply_reduce_fusion.1
  200.0 1.2 convolution_convert_fusion.7.seed_ref
  201.3 1.5 convolution_convert_fusion.6
  202.7 9.4 %shard_map.258 = (bf16[128,768]{1,0:T(8,128)(2,1)}, bf16[128,1536]{1,0:T(8,128)(2,1)}, bf16[128,1536]{1,0:T(8,128)(2,1)}, bf16[128,1536]{1,0:T(8,128)(2,1)}, bf16[128,1536]{1,0:T(8,128)(2,1)}) custom-call(bf16[128,768]{1,0:T(8,128)(2,1)} %slice.107.q_ref, s32[1,512]{1,0:T(1,128)} %bitcast.162, bf16[128,768]{1,0:T(8,128)(2,1)} %convolution_convert_fusion.7.seed_ref, ...), custom_call_target="tpu_custom_call" | custom-call | flops 503316480 | bytes 3145728 | tf_op jit(solution)/shard_map/pallas_call | solution.py:885
  212.7 2.9 collective-permute-start.8
  216.1 31.2 %shard_map.259 = (bf16[2,256,1152]{2,1,0:T(8,128)(2,1)}, bf16[2,384,1152]{2,1,0:T(8,128)(2,1)}, f32[128,256]{1,0:T(8,128)}) custom-call(s32[128,16]{1,0:T(8,128)} %bitcast.160, f32[128,768]{1,0:T(8,128)} %slice_bitcast_fusion.15.seed, bf16[2,256,1152]{2,1,0:T(8,128)(2,1)} %bitcast.167, bf16[2,384,1152]{2,1,0:T(8,128)(2,1)} %bitcast.165, ...), custom_call_target="tpu_custom_call" | custom-call | flops 24159191040 | bytes 25165824 | tf_op jit(solution)/shard_map/pallas_call | solution.py:780
  248.3 2.2 convolution_convert_fusion.5
  251.3 3.7 convolution_convert_fusion.2
  255.1 1.4 add_convert_fusion.1
  256.4 2.0 fusion.25
  258.4 3.0 convolution_convert_fusion.1
  261.4 127.8 %shard_map.260 = (f32[16,1152]{1,0:T(8,128)}, f32[24,1152]{1,0:T(8,128)}, f32[48,768]{1,0:T(8,128)}, f32[144,768]{1,0:T(8,128)}, f32[96,768]{1,0:T(8,128)}, /*in...) custom-call(bf16[32,16,1152]{2,1,0:T(8,128)(2,1)} %bitcast.156, ...), custom_call_target="tpu_custom_call" | custom-call | tf_op jit(solution)/shard_map/pallas_call | solution.py:541
  389.2 1.4 constant_dynamic-slice_fusion.2
  390.6 2.6 shard_map.261
  (128 shorter events, 19.6 us)
Async XLA Ops:
  107.0 15.5 %copy-start.22 = (s32[1,128,16]{1,2,0:T(8,128)S(1)}, s32[1,128,16]{1,2,0:T(8,128)}, u32[]{:S(2)}) copy-start(s32[1,128,16]{1,2,0:T(8,128)} %param.17) | copy-start | bytes 24580
  107.0 16.9 %copy-start.13 = (bf16[32,8,768]{2,1,0:T(8,128)(2,1)S(1)}, bf16[32,8,768]{2,1,0:T(8,128)(2,1)}, u32[]{:S(2)}) copy-start(bf16[32,8,768]{2,1,0:T(8,128)(2,1)} %get-tuple-element.60) | copy-start | bytes 1179652
  107.0 16.9 %copy-start.7 = (bf16[1,128,768]{2,1,0:T(8,128)(2,1)S(1)}, bf16[1,128,768]{2,1,0:T(8,128)(2,1)}, u32[]{:S(2)}) copy-start(bf16[1,128,768]{2,1,0:T(8,128)(2,1)} %param.20) | copy-start | bytes 589828
  109.8 36.5 %copy-start.3 = (bf16[128,1536]{1,0:T(8,128)(2,1)}, bf16[128,1536]{1,0:T(8,128)(2,1)S(1)}, u32[]{:S(2)}) copy-start(bf16[128,1536]{1,0:T(8,128)(2,1)S(1)} %slice.108.refs_0_) | copy-start | bytes 1179652
  109.9 39.2 %collective-permute-start = (bf16[128,1536]{1,0:T(8,128)(2,1)S(1)}, bf16[128,1536]{1,0:T(8,128)(2,1)S(1)}, u32[]{:S(2)}, u32[]{:S(2)}) collective-permute-start(bf16[128,1536]{1,0:T(8,128)(2,1)S(1)} %slice.108.refs_0_), channel_id=1, source_target_pairs={{1,0},{2,1},{3,2},{0,3},{5,4},{6,5},{7,6},{4,7},{9,8},{10,9},{11,1... | collective-permute-start | bytes 1179656 | tf_op jit(solution)/shard_map/ppermute | solution.py:897
  110.9 38.2 %collective-permute-start.1 = (bf16[128,1536]{1,0:T(8,128)(2,1)S(1)}, bf16[128,1536]{1,0:T(8,128)(2,1)S(1)}, u32[]{:S(2)}, u32[]{:S(2)}) collective-permute-start(bf16[128,1536]{1,0:T(8,128)(2,1)S(1)} %slice.108.refs_0_), channel_id=1, source_target_pairs={{2,0},{3,1},{0,2},{1,3},{6,4},{7,5},{4,6},{5,7},{10,8},{11,9},{8,1... | collective-permute-start | bytes 1179656 | tf_op jit(solution)/shard_map/ppermute | solution.py:897
  111.9 37.2 %collective-permute-start.2 = (bf16[128,1536]{1,0:T(8,128)(2,1)S(1)}, bf16[128,1536]{1,0:T(8,128)(2,1)}, u32[]{:S(2)}, u32[]{:S(2)}) collective-permute-start(bf16[128,1536]{1,0:T(8,128)(2,1)S(1)} %slice.108.refs_0_), channel_id=1, source_target_pairs={{3,0},{0,1},{1,2},{2,3},{7,4},{4,5},{5,6},{6,7},{11,8},{8,9},{9,10... | collective-permute-start | bytes 1179656 | tf_op jit(solution)/shard_map/ppermute | solution.py:897
  146.4 10.0 %copy-start.2 = (bf16[32,24,768]{2,1,0:T(8,128)(2,1)S(1)}, bf16[32,24,768]{2,1,0:T(8,128)(2,1)}, u32[]{:S(2)}) copy-start(bf16[32,24,768]{2,1,0:T(8,128)(2,1)} %get-tuple-element.59) | copy-start | bytes 3538948
  146.4 10.0 %copy-start.5 = (bf16[1,128,768]{2,1,0:T(8,128)(2,1)S(1)}, bf16[1,128,768]{2,1,0:T(8,128)(2,1)}, u32[]{:S(2)}) copy-start(bf16[1,128,768]{2,1,0:T(8,128)(2,1)} %param.16) | copy-start | bytes 589828
  156.4 8.3 %slice-start.4 = ((s8[4718592]{0:T(1024)(128)(4,1)}), s8[4194304]{0:T(1024)(128)(4,1)S(1)}, s32[]{:S(2)}) async-start(s8[4718592]{0:T(1024)(128)(4,1)} %bitcast.146), calls=%async_computation.4 | async-start | bytes 8388608
  156.4 14.9 %slice-start = ((s8[7077888]{0:T(1024)(128)(4,1)}), s8[4194304]{0:T(1024)(128)(4,1)S(1)}, s32[]{:S(2)}) async-start(s8[7077888]{0:T(1024)(128)(4,1)} %bitcast.131), calls=%async_computation | async-start | bytes 8388608
  158.1 41.8 %copy-start.18 = (f32[128]{0:T(128)}, f32[128]{0:T(128)S(1)}, u32[]{:S(2)}) copy-start(f32[128]{0:T(128)S(1)} %add_rsqrt_fusion.2) | copy-start | bytes 1540
  158.1 6.6 %slice-start.5 = ((s8[4718592]{0:T(1024)(128)(4,1)}), s8[524288]{0:T(1024)(128)(4,1)S(1)}, s32[]{:S(2)}) async-start(s8[4718592]{0:T(1024)(128)(4,1)} %bitcast.146), calls=%async_computation.5 | async-start | bytes 1048576
  158.1 13.1 %slice-start.1 = ((s8[7077888]{0:T(1024)(128)(4,1)}), s8[2883584]{0:T(1024)(128)(4,1)S(1)}, s32[]{:S(2)}) async-start(s8[7077888]{0:T(1024)(128)(4,1)} %bitcast.131), calls=%async_computation.1 | async-start | bytes 5767168
  167.0 4.8 %collective-permute-start.3 = (bf16[1,1,1536]{2,1,0:T(2,128)(2,1)S(1)}, bf16[1,1,1536]{2,1,0:T(2,128)(2,1)S(1)}, u32[]{:S(2)}, u32[]{:S(2)}) collective-permute-start(bf16[1,1,1536]{2,1,0:T(2,128)(2,1)S(1)} %get-tuple-element.130), channel_id=1, source_target_pairs={{0,1},{1,2},{2,3},{4,5},{5,6},{6,7},{8,9},{9,10},{10,11},{12,13},{... | collective-permute-start | bytes 9224 | tf_op jit(solution)/shard_map/ppermute | solution.py:574
  170.0 3.1 collective-permute-start.4
  175.7 11.8 %collective-permute-start.6 = (bf16[1,1,768]{2,1,0:T(2,128)(2,1)S(1)}, bf16[1,1,768]{2,1,0:T(2,128)(2,1)S(1)}, u32[]{:S(2)}, u32[]{:S(2)}) collective-permute-start(bf16[1,1,768]{2,1,0:T(2,128)(2,1)S(1)} %get-tuple-element.135), channel_id=1, source_target_pairs={{0,1},{1,2},{2,3},{4,5},{5,6},{6,7},{8,9},{9,10},{10,11},{12,13},{... | collective-permute-start | bytes 4616 | tf_op jit(solution)/shard_map/ppermute | solution.py:574
  185.3 3.1 collective-permute-start.5
  191.0 6.4 %slice-start.2 = ((s8[4718592]{0:T(1024)(128)(4,1)}), s8[4194304]{0:T(1024)(128)(4,1)S(1)}, s32[]{:S(2)}) async-start(s8[4718592]{0:T(1024)(128)(4,1)} %bitcast.143), calls=%async_computation.2 | async-start | bytes 8388608
  192.0 5.5 %slice-start.3 = ((s8[4718592]{0:T(1024)(128)(4,1)}), s8[524288]{0:T(1024)(128)(4,1)S(1)}, s32[]{:S(2)}) async-start(s8[4718592]{0:T(1024)(128)(4,1)} %bitcast.143), calls=%async_computation.3 | async-start | bytes 1048576
  212.1 42.9 %collective-permute-start.9 = (bf16[128,1536]{1,0:T(8,128)(2,1)}, bf16[128,1536]{1,0:T(8,128)(2,1)S(1)}, u32[]{:S(2)}, u32[]{:S(2)}) collective-permute-start(bf16[128,1536]{1,0:T(8,128)(2,1)} %get-tuple-element.73), channel_id=1, source_target_pairs={{0,3},{1,0},{2,1},{3,2},{4,7},{5,4},{6,5},{7,6},{8,11},{9,8},{10,9... | collective-permute-start | bytes 1179656 | tf_op jit(solution)/shard_map/ppermute | solution.py:902
  212.7 42.3 %collective-permute-start.8 = (bf16[128,1536]{1,0:T(8,128)(2,1)}, bf16[128,1536]{1,0:T(8,128)(2,1)}, u32[]{:S(2)}, u32[]{:S(2)}) collective-permute-start(bf16[128,1536]{1,0:T(8,128)(2,1)} %get-tuple-element.72), channel_id=1, source_target_pairs={{0,2},{1,3},{2,0},{3,1},{4,6},{5,7},{6,4},{7,5},{8,10},{9,11},{10,... | collective-permute-start | bytes 1179656 | tf_op jit(solution)/shard_map/ppermute | solution.py:902
  215.6 39.4 %collective-permute-start.7 = (bf16[128,1536]{1,0:T(8,128)(2,1)}, bf16[128,1536]{1,0:T(8,128)(2,1)}, u32[]{:S(2)}, u32[]{:S(2)}) collective-permute-start(bf16[128,1536]{1,0:T(8,128)(2,1)} %get-tuple-element.71), channel_id=1, source_target_pairs={{0,1},{1,2},{2,3},{3,0},{4,5},{5,6},{6,7},{7,4},{8,9},{9,10},{10,1... | collective-permute-start | bytes 1179656 | tf_op jit(solution)/shard_map/ppermute | solution.py:902
  216.0 32.2 %copy-start.12 = (bf16[128,768]{1,0:T(8,128)(2,1)S(1)}, bf16[128,768]{1,0:T(8,128)(2,1)}, u32[]{:S(2)}) copy-start(bf16[128,768]{1,0:T(8,128)(2,1)} %get-tuple-element.66) | copy-start | bytes 589828
  248.3 2.3 copy-start.4
  248.3 2.3 copy-start.17
  248.3 2.3 copy-start.16
  248.3 2.3 copy-start.20
  248.3 2.3 copy-start.21
  248.3 3.0 copy-start.19
  251.3 3.8 copy-start.14
  251.3 5.1 %copy-start = (bf16[32,24,2304]{2,1,0:T(8,128)(2,1)S(1)}, bf16[32,24,2304]{2,1,0:T(8,128)(2,1)}, u32[]{:S(2)}) copy-start(bf16[32,24,2304]{2,1,0:T(8,128)(2,1)} %get-tuple-element.58) | copy-start | bytes 10616836
  (7 other events, 10.0 us)

commit v9 on v8

--- a/solution.py
+++ b/solution.py
@@ -645,13 +645,14 @@
         factor[:, k * units : (k + 1) * units] = x.astype(factor.dtype)
 
 
-def gru_forward_kernel(ids_ref, table, w_in, w_rec, vec, emb, f0, f1, z0, z1, h0, h1, gates, state):
+def gru_forward_kernel(group, ids_ref, tables, w_in, w_rec, vec, emb, f0, f1, z0, z1, h0, h1, gates, state):
     i = pl.program_id(0)
     nchar = pl.num_programs(0)
 
     @pl.when(i == 0)
     def _():
-        gru_embed(ids_ref, table, w_in, emb, gates)
+        own = pl.ds(pl.multiple_of(group[0] * SUBV, SUBV), SUBV)
+        gru_embed(ids_ref, tables.at[own], w_in, emb, gates)
         state[...] = jnp.zeros_like(state)
 
     count = jnp.sum((ids_ref[...] > 0).astype(jnp.int32), axis=1, keepdims=True)
@@ -680,7 +681,7 @@
     )
 
 
-def gru_forward(ids, table, w_in, w_rec):
+def gru_forward(group, ids, table, w_in, w_rec):
     rows, nchar = ids.shape
     width, units = table.shape[1], w_rec.shape[1]
     whole = lambda shape: pl.BlockSpec(shape, lambda i: (0,) * len(shape))
@@ -697,7 +698,7 @@
             shape((nchar, rows, width), jnp.bfloat16),
             factor, factor, keep, keep, prior, prior,
         ],
-        in_specs=[whole(x.shape) for x in (ids, table, w_in, w_rec)],
+        in_specs=[pl.BlockSpec(memory_space=pltpu.SMEM)] + [whole(x.shape) for x in (ids, table, w_in, w_rec)],
         out_specs=[whole((rows, 2 * units)), whole((nchar, rows, width))]
         + slots(4 * units) + slots(units) + slots(units),
         scratch_shapes=[
@@ -706,7 +707,7 @@
         ],
         compiler_params=pltpu.CompilerParams(vmem_limit_bytes=60000000),
         cost_estimate=gru_cost(nchar, rows, width, units, 1),
-    )(ids, table, w_in, w_rec)
+    )(group, ids, table, w_in, w_rec)
 
 
 def gru_back_step(d, slot, factor, keep, flipped, grad, seeds):
@@ -966,10 +967,9 @@
     assert seq_count == 1
     flat_ids = char_ids.reshape(tokens, nchar)
     table_start = groups[0] * SUBV
-    own_table = lax.dynamic_slice_in_dim(full_table, table_start, SUBV, 0)
     inward = full_input.reshape(2, -1, full_input.shape[1])
     recurrent = full_recur.reshape(2, -1, full_recur.shape[1])
-    char_vec, char_emb, *kept = gru_forward(flat_ids, own_table, inward, recurrent)
+    char_vec, char_emb, *kept = gru_forward(groups, flat_ids, full_table, inward, recurrent)
     factors, keeps, priors = kept[:2], kept[2:4], kept[4:]
     attended = attention(queries, key_valid, kv_blocks)
     resid_one = flat_in.astype(jnp.float32) + plain_dot(attended, full_out)

time: 394 us -> 393 us (level)
  no operation moved by 1% of the time
where the time goes in v9:
time: 393 us; the launch traced here: 392 us
  Pallas kernels  303 us (77%)
  matrix products  44.7 us (11%)
  starting transfers between devices  26.1 us (7%)
  local copies, waits for them, and re-layouts  7.61 us (2%)
  other arithmetic  6.28 us (2%)
    pallas_call x1, Pallas kernels, scatter_all(): pl.pallas_call(functools.partial(scatter_kernel, dp_size, chunks, count,...  128 us
    pallas_call x1, Pallas kernels, gather_all(): pl.pallas_call(functools.partial(gather_kernel, dp_size, count, early), o...  105 us
    pallas_call x1, Pallas kernels, gru_backward(): pl.pallas_call(gru_backward_kernel, grid=(nchar,), out_shape=[shape(w_in....  31.2 us
    pallas_call x1, Pallas kernels, gru_forward(): pl.pallas_call(gru_forward_kernel, grid=(nchar,), out_shape=[shape((rows,...  21.3 us
    dot_general x5, matrix products, grad_dot(): lax.dot_general(left, right, (((0,), (0,)), ((), ())), preferred_element_...  16.7 us
    dot_general x8, matrix products, plain_dot(): return jnp.dot(left, right, preferred_element_type=jnp.float32)  14.2 us
    ppermute x3, starting transfers between devices, from_next(): return lax.ppermute(x, axis, [((i + step) % size, i) for i in range(size)])  12.6 us
    dot_general x7, matrix products, back_dot(): lax.dot_general(left, right, (((1,), (1,)), ((), ())), preferred_element_...  10.1 us
  transfers between devices with their start and end apart: 10, of which 2 were waited for; matrix products, arithmetic and copies ran while one was open for 5% of the time, Pallas kernels for 13%

profile of v9, /device:TPU:0, one launch (start us, length us, event | category | flops | bytes accessed | tf_op | source)
XLA Modules:
  0.0 392.2 jit_solution(11888845851665768774)
XLA Ops:
  2.2 104.8 %shard_map.255 = (bf16[32,32,256]{2,1,0:T(8,128)(2,1)}, bf16[32,16,1152]{2,1,0:T(8,128)(2,1)}, bf16[32,24,1152]{2,1,0:T(8,128)(2,1)}, bf16[32,8,768]{2,1,0:T(8,1...) custom-call(bf16[32,256]{1,0:T(8,128)(2,1)} %refs_0_.1, ...), custom_call_target="tpu_custom_call" | custom-call | tf_op jit(solution)/shard_map/pallas_call | solution.py:248
  107.0 2.8 fusion
  109.9 1.0 collective-permute-start
  110.9 1.0 collective-permute-start.1
  111.9 10.5 %collective-permute-start.2 = (bf16[128,1536]{1,0:T(8,128)(2,1)S(1)}, bf16[128,1536]{1,0:T(8,128)(2,1)}, u32[]{:S(2)}, u32[]{:S(2)}) collective-permute-start(bf16[128,1536]{1,0:T(8,128)(2,1)S(1)} %slice.108.refs_0_), channel_id=1, source_target_pairs={{3,0},{0,1},{1,2},{2,3},{7,4},{4,5},{5,6},{6,7},{11,8},{8,9},{9,10... | collective-permute-start | bytes 1179656 | tf_op jit(solution)/shard_map/ppermute | solution.py:898
  123.9 21.3 %shard_map.257 = (bf16[128,768]{1,0:T(8,128)(2,1)}, bf16[16,128,256]{2,1,0:T(8,128)(2,1)}, bf16[16,128,1536]{2,1,0:T(8,128)(2,1)}, bf16[16,128,1536]{2,1,0:T(8,1...) custom-call(s32[1]{0:T(128)S(6)} %copy.35.group, ...), custom_call_target="tpu_custom_call" | custom-call | flops 12079595520 | bytes 25165824 | tf_op jit(solution)/shard_map/pallas_call | solution.py:693
  148.8 6.4 %shard_map.256 = bf16[128,768]{1,0:T(8,128)(2,1)} custom-call(bf16[128,768]{1,0:T(8,128)(2,1)} %slice.107.q_ref, s32[1,512]{1,0:T(1,128)} %bitcast.161, bf16[128,1536]{1,0:T(8,128)(2,1)} %copy-done.3, bf16[128,1536]{1,0:T(8,128)(2,1)} %copy-done.8, bf16[128,1536]{1,0:T(8,128)(2,1)} %copy-done.9, bf16[128,1536]{1,0:T(8,128)(2,1)} %collective-permute-done.2.refs_3_), custom_call_target="tpu_custom_call" | custom-call | flops 201326592 | bytes 3145728 | tf_op jit(solution)/shard_map/pallas_call | solution.py:874
  155.2 1.5 fusion.83
  157.0 6.5 %multiply_convert_fusion = (bf16[128,3072]{1,0:T(8,128)(2,1)S(1)}, f32[128,3072]{1,0:T(8,128)S(1)}, f32[128,3072]{1,0:T(8,128)S(1)}) fusion(bf16[768,3072]{1,0:T(8,128)(2,1)} %bitcast.142, f32[128,768]{1,0:T(8,128)S(1)} %get-tuple-element.139, f32[768]{0:T(1024)S(1)} %get-tuple-element.118, f32[768]{0:T(1024)S(1)} %get-tuple-element.119, ...), kind=kOutput, calls=%fused_computation.21 | convolution fusion | flops 630030336 | bytes 9051136 | tf_op jit(solution)/shard_map/dot_general | solution.py:591
  163.6 0.9 fusion.84
  165.8 2.9 collective-permute-start.3
  168.7 1.3 collective-permute-start.4
  170.6 1.2 collective-permute-done.4
  174.5 3.9 collective-permute-start.6
  178.3 4.9 %convolution_convert_fusion = bf16[4608,768]{1,0:T(8,128)(2,1)} fusion(bf16[128,1536]{1,0:T(8,128)(2,1)S(1)} %get-tuple-element.129, bf16[128,768]{1,0:T(8,128)(2,1)S(1)} %bitcast.153, bf16[128,768]{1,0:T(8,128)(2,1)S(1)} %bitcast.151, bf16[128,1536]{1,0:T(8,128)(2,1)S(1)} %get-tuple-element.128, f32[128,768]{1,0:T(8,128)S(1)} %get-tuple-element.122), kind=kOutput, calls=%fused_computation | convolution fusion | flops 914325504 | bytes 8650752 | tf_op jit(solution)/shard_map/dot_general | solution.py:595
  184.2 1.5 collective-permute-start.5
  190.8 3.6 convolution_convert_fusion.3
  194.5 1.9 add_convert_fusion
  196.4 2.4 multiply_reduce_fusion.1
  199.0 1.2 convolution_convert_fusion.7.seed_ref
  200.2 1.5 convolution_convert_fusion.6
  201.7 9.4 %shard_map.258 = (bf16[128,768]{1,0:T(8,128)(2,1)}, bf16[128,1536]{1,0:T(8,128)(2,1)}, bf16[128,1536]{1,0:T(8,128)(2,1)}, bf16[128,1536]{1,0:T(8,128)(2,1)}, bf16[128,1536]{1,0:T(8,128)(2,1)}) custom-call(bf16[128,768]{1,0:T(8,128)(2,1)} %slice.107.q_ref, s32[1,512]{1,0:T(1,128)} %bitcast.162, bf16[128,768]{1,0:T(8,128)(2,1)} %convolution_convert_fusion.7.seed_ref, ...), custom_call_target="tpu_custom_call" | custom-call | flops 503316480 | bytes 3145728 | tf_op jit(solution)/shard_map/pallas_call | solution.py:886
  211.7 2.9 collective-permute-start.8
  215.0 31.2 %shard_map.259 = (bf16[2,256,1152]{2,1,0:T(8,128)(2,1)}, bf16[2,384,1152]{2,1,0:T(8,128)(2,1)}, f32[128,256]{1,0:T(8,128)}) custom-call(s32[128,16]{1,0:T(8,128)} %bitcast.160, f32[128,768]{1,0:T(8,128)} %slice_bitcast_fusion.15.seed, bf16[2,256,1152]{2,1,0:T(8,128)(2,1)} %bitcast.166, bf16[2,384,1152]{2,1,0:T(8,128)(2,1)} %bitcast.164, ...), custom_call_target="tpu_custom_call" | custom-call | flops 24159191040 | bytes 25165824 | tf_op jit(solution)/shard_map/pallas_call | solution.py:781
  247.3 2.2 convolution_convert_fusion.5
  250.3 3.7 convolution_convert_fusion.2
  254.0 1.4 add_convert_fusion.1
  255.4 2.0 fusion.25
  257.4 2.9 convolution_convert_fusion.1
  260.3 127.8 %shard_map.260 = (f32[16,1152]{1,0:T(8,128)}, f32[24,1152]{1,0:T(8,128)}, f32[48,768]{1,0:T(8,128)}, f32[144,768]{1,0:T(8,128)}, f32[96,768]{1,0:T(8,128)}, /*in...) custom-call(bf16[32,16,1152]{2,1,0:T(8,128)(2,1)} %bitcast.156, ...), custom_call_target="tpu_custom_call" | custom-call | tf_op jit(solution)/shard_map/pallas_call | solution.py:541
  388.1 1.4 constant_dynamic-slice_fusion.1
  389.5 2.6 shard_map.261
  (127 shorter events, 18.7 us)
Async XLA Ops:
  107.0 16.1 %copy-start.22 = (s32[1,128,16]{1,2,0:T(8,128)S(1)}, s32[1,128,16]{1,2,0:T(8,128)}, u32[]{:S(2)}) copy-start(s32[1,128,16]{1,2,0:T(8,128)} %param.17) | copy-start | bytes 24580
  107.0 16.8 %copy-start.13 = (bf16[32,8,768]{2,1,0:T(8,128)(2,1)S(1)}, bf16[32,8,768]{2,1,0:T(8,128)(2,1)}, u32[]{:S(2)}) copy-start(bf16[32,8,768]{2,1,0:T(8,128)(2,1)} %get-tuple-element.60) | copy-start | bytes 1179652
  107.0 16.9 %copy-start.7 = (bf16[1,128,768]{2,1,0:T(8,128)(2,1)S(1)}, bf16[1,128,768]{2,1,0:T(8,128)(2,1)}, u32[]{:S(2)}) copy-start(bf16[1,128,768]{2,1,0:T(8,128)(2,1)} %param.20) | copy-start | bytes 589828
  109.8 35.4 %copy-start.3 = (bf16[128,1536]{1,0:T(8,128)(2,1)}, bf16[128,1536]{1,0:T(8,128)(2,1)S(1)}, u32[]{:S(2)}) copy-start(bf16[128,1536]{1,0:T(8,128)(2,1)S(1)} %slice.108.refs_0_) | copy-start | bytes 1179652
  109.9 38.1 %collective-permute-start = (bf16[128,1536]{1,0:T(8,128)(2,1)S(1)}, bf16[128,1536]{1,0:T(8,128)(2,1)S(1)}, u32[]{:S(2)}, u32[]{:S(2)}) collective-permute-start(bf16[128,1536]{1,0:T(8,128)(2,1)S(1)} %slice.108.refs_0_), channel_id=1, source_target_pairs={{1,0},{2,1},{3,2},{0,3},{5,4},{6,5},{7,6},{4,7},{9,8},{10,9},{11,1... | collective-permute-start | bytes 1179656 | tf_op jit(solution)/shard_map/ppermute | solution.py:898
  110.9 37.0 %collective-permute-start.1 = (bf16[128,1536]{1,0:T(8,128)(2,1)S(1)}, bf16[128,1536]{1,0:T(8,128)(2,1)S(1)}, u32[]{:S(2)}, u32[]{:S(2)}) collective-permute-start(bf16[128,1536]{1,0:T(8,128)(2,1)S(1)} %slice.108.refs_0_), channel_id=1, source_target_pairs={{2,0},{3,1},{0,2},{1,3},{6,4},{7,5},{4,6},{5,7},{10,8},{11,9},{8,1... | collective-permute-start | bytes 1179656 | tf_op jit(solution)/shard_map/ppermute | solution.py:898
  111.9 36.0 %collective-permute-start.2 = (bf16[128,1536]{1,0:T(8,128)(2,1)S(1)}, bf16[128,1536]{1,0:T(8,128)(2,1)}, u32[]{:S(2)}, u32[]{:S(2)}) collective-permute-start(bf16[128,1536]{1,0:T(8,128)(2,1)S(1)} %slice.108.refs_0_), channel_id=1, source_target_pairs={{3,0},{0,1},{1,2},{2,3},{7,4},{4,5},{5,6},{6,7},{11,8},{8,9},{9,10... | collective-permute-start | bytes 1179656 | tf_op jit(solution)/shard_map/ppermute | solution.py:898
  145.2 10.0 %copy-start.2 = (bf16[32,24,768]{2,1,0:T(8,128)(2,1)S(1)}, bf16[32,24,768]{2,1,0:T(8,128)(2,1)}, u32[]{:S(2)}) copy-start(bf16[32,24,768]{2,1,0:T(8,128)(2,1)} %get-tuple-element.59) | copy-start | bytes 3538948
  145.2 10.0 %copy-start.5 = (bf16[1,128,768]{2,1,0:T(8,128)(2,1)S(1)}, bf16[1,128,768]{2,1,0:T(8,128)(2,1)}, u32[]{:S(2)}) copy-start(bf16[1,128,768]{2,1,0:T(8,128)(2,1)} %param.16) | copy-start | bytes 589828
  155.2 8.3 %slice-start.4 = ((s8[4718592]{0:T(1024)(128)(4,1)}), s8[4194304]{0:T(1024)(128)(4,1)S(1)}, s32[]{:S(2)}) async-start(s8[4718592]{0:T(1024)(128)(4,1)} %bitcast.146), calls=%async_computation.4 | async-start | bytes 8388608
  155.2 14.8 %slice-start = ((s8[7077888]{0:T(1024)(128)(4,1)}), s8[4194304]{0:T(1024)(128)(4,1)S(1)}, s32[]{:S(2)}) async-start(s8[7077888]{0:T(1024)(128)(4,1)} %bitcast.131), calls=%async_computation | async-start | bytes 8388608
  156.9 41.8 %copy-start.18 = (f32[128]{0:T(128)}, f32[128]{0:T(128)S(1)}, u32[]{:S(2)}) copy-start(f32[128]{0:T(128)S(1)} %add_rsqrt_fusion.2) | copy-start | bytes 1540
  157.0 6.6 %slice-start.5 = ((s8[4718592]{0:T(1024)(128)(4,1)}), s8[524288]{0:T(1024)(128)(4,1)S(1)}, s32[]{:S(2)}) async-start(s8[4718592]{0:T(1024)(128)(4,1)} %bitcast.146), calls=%async_computation.5 | async-start | bytes 1048576
  157.0 13.1 %slice-start.1 = ((s8[7077888]{0:T(1024)(128)(4,1)}), s8[2883584]{0:T(1024)(128)(4,1)S(1)}, s32[]{:S(2)}) async-start(s8[7077888]{0:T(1024)(128)(4,1)} %bitcast.131), calls=%async_computation.1 | async-start | bytes 5767168
  165.8 4.8 %collective-permute-start.3 = (bf16[1,1,1536]{2,1,0:T(2,128)(2,1)S(1)}, bf16[1,1,1536]{2,1,0:T(2,128)(2,1)S(1)}, u32[]{:S(2)}, u32[]{:S(2)}) collective-permute-start(bf16[1,1,1536]{2,1,0:T(2,128)(2,1)S(1)} %get-tuple-element.130), channel_id=1, source_target_pairs={{0,1},{1,2},{2,3},{4,5},{5,6},{6,7},{8,9},{9,10},{10,11},{12,13},{... | collective-permute-start | bytes 9224 | tf_op jit(solution)/shard_map/ppermute | solution.py:574
  168.7 3.1 collective-permute-start.4
  174.5 11.8 %collective-permute-start.6 = (bf16[1,1,768]{2,1,0:T(2,128)(2,1)S(1)}, bf16[1,1,768]{2,1,0:T(2,128)(2,1)S(1)}, u32[]{:S(2)}, u32[]{:S(2)}) collective-permute-start(bf16[1,1,768]{2,1,0:T(2,128)(2,1)S(1)} %get-tuple-element.135), channel_id=1, source_target_pairs={{0,1},{1,2},{2,3},{4,5},{5,6},{6,7},{8,9},{9,10},{10,11},{12,13},{... | collective-permute-start | bytes 4616 | tf_op jit(solution)/shard_map/ppermute | solution.py:574
  184.2 3.1 collective-permute-start.5
  189.9 6.5 %slice-start.2 = ((s8[4718592]{0:T(1024)(128)(4,1)}), s8[4194304]{0:T(1024)(128)(4,1)S(1)}, s32[]{:S(2)}) async-start(s8[4718592]{0:T(1024)(128)(4,1)} %bitcast.143), calls=%async_computation.2 | async-start | bytes 8388608
  190.8 5.6 %slice-start.3 = ((s8[4718592]{0:T(1024)(128)(4,1)}), s8[524288]{0:T(1024)(128)(4,1)S(1)}, s32[]{:S(2)}) async-start(s8[4718592]{0:T(1024)(128)(4,1)} %bitcast.143), calls=%async_computation.3 | async-start | bytes 1048576
  211.1 42.9 %collective-permute-start.9 = (bf16[128,1536]{1,0:T(8,128)(2,1)}, bf16[128,1536]{1,0:T(8,128)(2,1)S(1)}, u32[]{:S(2)}, u32[]{:S(2)}) collective-permute-start(bf16[128,1536]{1,0:T(8,128)(2,1)} %get-tuple-element.73), channel_id=1, source_target_pairs={{0,3},{1,0},{2,1},{3,2},{4,7},{5,4},{6,5},{7,6},{8,11},{9,8},{10,9... | collective-permute-start | bytes 1179656 | tf_op jit(solution)/shard_map/ppermute | solution.py:903
  211.7 42.3 %collective-permute-start.8 = (bf16[128,1536]{1,0:T(8,128)(2,1)}, bf16[128,1536]{1,0:T(8,128)(2,1)}, u32[]{:S(2)}, u32[]{:S(2)}) collective-permute-start(bf16[128,1536]{1,0:T(8,128)(2,1)} %get-tuple-element.72), channel_id=1, source_target_pairs={{0,2},{1,3},{2,0},{3,1},{4,6},{5,7},{6,4},{7,5},{8,10},{9,11},{10,... | collective-permute-start | bytes 1179656 | tf_op jit(solution)/shard_map/ppermute | solution.py:903
  214.6 39.4 %collective-permute-start.7 = (bf16[128,1536]{1,0:T(8,128)(2,1)}, bf16[128,1536]{1,0:T(8,128)(2,1)}, u32[]{:S(2)}, u32[]{:S(2)}) collective-permute-start(bf16[128,1536]{1,0:T(8,128)(2,1)} %get-tuple-element.71), channel_id=1, source_target_pairs={{0,1},{1,2},{2,3},{3,0},{4,5},{5,6},{6,7},{7,4},{8,9},{9,10},{10,1... | collective-permute-start | bytes 1179656 | tf_op jit(solution)/shard_map/ppermute | solution.py:903
  215.0 32.2 %copy-start.12 = (bf16[128,768]{1,0:T(8,128)(2,1)S(1)}, bf16[128,768]{1,0:T(8,128)(2,1)}, u32[]{:S(2)}) copy-start(bf16[128,768]{1,0:T(8,128)(2,1)} %get-tuple-element.66) | copy-start | bytes 589828
  247.2 2.3 copy-start.4
  247.2 2.3 copy-start.17
  247.3 2.3 copy-start.16
  247.3 2.4 copy-start.20
  247.3 2.4 copy-start.21
  247.3 3.0 copy-start.19
  250.3 3.7 copy-start.14
  250.3 5.1 %copy-start = (bf16[32,24,2304]{2,1,0:T(8,128)(2,1)S(1)}, bf16[32,24,2304]{2,1,0:T(8,128)(2,1)}, u32[]{:S(2)}) copy-start(bf16[32,24,2304]{2,1,0:T(8,128)(2,1)} %get-tuple-element.58) | copy-start | bytes 10616836
  (7 other events, 10.1 us)
